TPU v7x, 32 devices: a whole 2x2x4 slice. The times are simulated.
32 devices in a mesh: dp: 8 (over z, core), tensor: 4 (over y, x).
Axes of the slice: x: 2, y: 2, z: 4, core: 2. Of those that a mesh axis runs over, the one named last changes fastest.
Arguments:
- tokens: bfloat16 [8192, 2048], P('dp'), may hold values from -6 to 6
- cotangent: bfloat16 [8192, 2048], P('dp'), may hold values from -6 to 6
- seq_lengths: int32 [4], replicated, may hold values from 1536 to 2048, as said below
- slot_seq: int32 [4], replicated, may hold values from 0 to 3, each once
- w_query: float32 [2048, 2048], P('dp', 'tensor'), may hold values from -0.125 to 0.125
- w_key: float32 [2048, 2048], P('dp', 'tensor'), may hold values from -0.125 to 0.125
- w_value: float32 [2048, 2048], P('dp', 'tensor'), may hold values from -0.125 to 0.125
- b_query: float32 [2048], P('tensor'), may hold values from -3 to 3
- b_value: float32 [2048], P('tensor'), may hold values from -3 to 3
- w_out: float32 [2048, 2048], P('tensor', 'dp'), may hold values from -4 to 4
- b_out: float32 [2048], replicated, may hold values from -3 to 3
- ln1_gain: float32 [2048], replicated, may hold values from 0.5 to 1.5
- ln1_bias: float32 [2048], replicated, may hold values from -3 to 3
- w_inner: float32 [2048, 8192], P('dp', 'tensor'), may hold values from -0.125 to 0.125
- b_inner: float32 [8192], P('tensor'), may hold values from -3 to 3
- w_outer: float32 [8192, 2048], P('tensor', 'dp'), may hold values from -0.0625 to 0.0625
- b_outer: float32 [2048], replicated, may hold values from -3 to 3
- ln2_gain: float32 [2048], replicated, may hold values from 0.5 to 1.5
- ln2_bias: float32 [2048], replicated, may hold values from -3 to 3
Outputs:
- output: float32 [8192, 2048], P('dp')
- grad_tokens: float32 [8192, 2048], P('dp')
- grad_w_query: float32 [2048, 2048], P('dp', 'tensor')
- grad_w_key: float32 [2048, 2048], P('dp', 'tensor')
- grad_w_value: float32 [2048, 2048], P('dp', 'tensor')
- grad_b_query: float32 [2048], P('tensor')
- grad_b_value: float32 [2048], P('tensor')
- grad_w_out: float32 [2048, 2048], P('tensor', 'dp')
- grad_b_out: float32 [2048], replicated
- grad_ln1_gain: float32 [2048], replicated
- grad_ln1_bias: float32 [2048], replicated
- grad_w_inner: float32 [2048, 8192], P('dp', 'tensor')
- grad_b_inner: float32 [8192], P('tensor')
- grad_w_outer: float32 [8192, 2048], P('tensor', 'dp')
- grad_b_outer: float32 [2048], replicated
- grad_ln2_gain: float32 [2048], replicated
- grad_ln2_bias: float32 [2048], replicated
Inputs may be any that keep to these rules, and one draw needn't show every extreme that they name: `seq_lengths`: each sequence's valid tokens; some sequence has exactly 2048 and some exactly 1536. `slot_seq`: each sequence stands in exactly one slot.
All inputs are finite; a program needn't handle non-finite values.
Results may differ from a plain program's by a relative error of at most 0.019.
Values may be sent and summed in bfloat16 or wider, within the bound.
No kernel may reach another device: no remote copies, remote signals or barrier semaphores. Data moves between devices by JAX's collectives and lax.ppermute only.
A program may use at most 256 MiB of HBM per device.

v0:
```python
import jax
import jax.numpy as jnp
from jax import lax
from jax.sharding import PartitionSpec as P

HEAD_DIM = 128
SLOT = 2048


norm_eps = 1e-12


def passed_along(value, axis, steps):
    count = lax.axis_size(axis)
    leading, last = (max(0, -steps), min(count, count - steps))
    return lax.ppermute(value, axis, [(source, source + steps) for source in range(leading, last)])


def layer_norm(resid, gain, shift):
    center = resid - jnp.mean(resid, axis=-1, keepdims=True)
    spread = jnp.mean(center * center, axis=-1, keepdims=True)
    return center * lax.rsqrt(spread + norm_eps) * gain + shift


def gelu_tanh(inner):
    return 0.5 * inner * (1.0 + jnp.tanh(0.7978845608 * (inner + 0.044715 * inner * inner * inner)))


def mat_bf(left, right):
    return jnp.dot(left, right, preferred_element_type=jnp.float32)


def tensor_total(part):
    return lax.psum(part, "tensor")


def on_device(
    tokens,
    cotangent,
    seq_lengths,
    slot_seq,
    w_query,
    w_key,
    w_value,
    b_query,
    b_value,
    w_out,
    b_out,
    ln1_gain,
    ln1_bias,
    w_inner,
    b_inner,
    w_outer,
    b_outer,
    ln2_gain,
    ln2_bias,
):
    tok_rows = tokens.shape[0]
    shard_count = SLOT // tok_rows
    width_here = w_query.shape[1]
    heads_here = width_here // HEAD_DIM
    score_scale = HEAD_DIM ** (-0.5)
    block_rows = min(512, tok_rows)
    block_count = tok_rows // block_rows
    dp_place = lax.axis_index("dp")
    my_slot = dp_place // shard_count
    my_spot = dp_place % shard_count
    slot_ids = jnp.arange(slot_seq.shape[0])
    slot_lengths = jnp.sum(
        jnp.where(slot_seq[:, None] == slot_ids[None, :], seq_lengths[None, :], 0), axis=1
    )
    my_length = jnp.sum(jnp.where(slot_ids == my_slot, slot_lengths, 0))
    row_live = (my_spot * tok_rows + jnp.arange(tok_rows) < my_length).astype(jnp.float32)
    key_live = jnp.arange(SLOT) < my_length
    spot_ids = jnp.arange(shard_count)
    offset_list = [step_by for step_by in range(1 - shard_count, shard_count) if step_by != 0]
    own_hit = (spot_ids == my_spot)[:, None, None]
    tokens_wide = tokens.astype(jnp.float32)
    cot_wide = cotangent.astype(jnp.float32)
    full_query, full_key, full_value, full_out = (
        lax.all_gather(w_query.astype(jnp.bfloat16), "dp", axis=0, tiled=True),
        lax.all_gather(w_key.astype(jnp.bfloat16), "dp", axis=0, tiled=True),
        lax.all_gather(w_value.astype(jnp.bfloat16), "dp", axis=0, tiled=True),
        lax.all_gather(w_out.astype(jnp.bfloat16), "dp", axis=1, tiled=True),
    )
    query_rows = (mat_bf(tokens, full_query) + b_query).astype(jnp.bfloat16)
    key_rows = mat_bf(tokens, full_key).astype(jnp.bfloat16)
    value_rows = (mat_bf(tokens, full_value) + b_value).astype(jnp.bfloat16)
    empty_slab = jnp.zeros((shard_count, tok_rows, width_here), jnp.bfloat16)
    key_slab = jnp.where(own_hit, key_rows[None], empty_slab)
    value_slab = jnp.where(own_hit, value_rows[None], empty_slab)
    for step_by in offset_list:
        far_key, far_value = passed_along((key_rows, value_rows), "dp", step_by)
        far_hit = (spot_ids == my_spot - step_by)[:, None, None]
        key_slab = jnp.where(far_hit, far_key[None], key_slab)
        value_slab = jnp.where(far_hit, far_value[None], value_slab)
    slot_keys = key_slab.reshape(SLOT, heads_here, HEAD_DIM)
    slot_values = value_slab.reshape(SLOT, heads_here, HEAD_DIM)
    query_blocks = query_rows.reshape(block_count, block_rows, heads_here, HEAD_DIM)

    def score_block(query_part):
        scores = (
            jnp.einsum("qhd,khd->hqk", query_part, slot_keys, preferred_element_type=jnp.float32)
            * score_scale
        )
        return jnp.where(key_live[None, None, :], scores, -1e30)

    def forward_block(query_part):
        scores = score_block(query_part)
        top = jnp.max(scores, axis=-1, keepdims=True)
        expd = jnp.exp(scores - top)
        total = jnp.sum(expd, axis=-1, keepdims=True)
        probs = expd / total
        mixed = jnp.einsum(
            "hqk,khd->qhd",
            probs.astype(jnp.bfloat16),
            slot_values,
            preferred_element_type=jnp.float32,
        )
        return (mixed, top + jnp.log(total))

    mixed_blocks, lse_blocks = lax.map(forward_block, query_blocks)
    heads_rows = mixed_blocks.reshape(tok_rows, width_here).astype(jnp.bfloat16)
    attn_part = mat_bf(heads_rows, full_out)
    attn = tensor_total(attn_part) + b_out
    resid_one = tokens_wide + attn
    hidden, norm_one_back = jax.vjp(layer_norm, resid_one, ln1_gain, ln1_bias)
    hidden_low = hidden.astype(jnp.bfloat16)
    full_inner, full_outer = (
        lax.all_gather(w_inner.astype(jnp.bfloat16), "dp", axis=0, tiled=True),
        lax.all_gather(w_outer.astype(jnp.bfloat16), "dp", axis=1, tiled=True),
    )
    inner = mat_bf(hidden_low, full_inner) + b_inner
    act_low = gelu_tanh(inner).astype(jnp.bfloat16)
    outer_part = mat_bf(act_low, full_outer)
    outer = tensor_total(outer_part) + b_outer
    output, norm_two_back = jax.vjp(layer_norm, hidden + outer, ln2_gain, ln2_bias)
    grad_out = cot_wide * row_live[:, None]
    grad_two, grad_ln2_gain, grad_ln2_bias = norm_two_back(grad_out)
    back_inner, back_outer = (
        lax.all_gather(w_inner.astype(jnp.bfloat16), "dp", axis=0, tiled=True),
        lax.all_gather(w_outer.astype(jnp.bfloat16), "dp", axis=1, tiled=True),
    )
    outer_low = grad_two.astype(jnp.bfloat16)
    grad_b_outer = jnp.sum(grad_two, axis=0)
    grad_w_outer = jnp.einsum("tf,td->fd", act_low, outer_low, preferred_element_type=jnp.float32)
    grad_act = jnp.einsum("td,fd->tf", outer_low, back_outer, preferred_element_type=jnp.float32)
    gelu_value, gelu_back = jax.vjp(gelu_tanh, inner)
    inner_low = gelu_back(grad_act)[0].astype(jnp.bfloat16)
    grad_b_inner = jnp.sum(inner_low.astype(jnp.float32), axis=0)
    grad_w_inner = jnp.einsum(
        "td,tf->df", hidden_low, inner_low, preferred_element_type=jnp.float32
    )
    grad_w_inner, grad_w_outer = (
        lax.psum_scatter(
            grad_w_inner.astype(jnp.bfloat16), "dp", scatter_dimension=0, tiled=True
        ).astype(jnp.float32),
        lax.psum_scatter(
            grad_w_outer.astype(jnp.bfloat16), "dp", scatter_dimension=1, tiled=True
        ).astype(jnp.float32),
    )
    hidden_part = jnp.einsum("tf,df->td", inner_low, back_inner, preferred_element_type=jnp.float32)
    grad_hidden = grad_two + tensor_total(hidden_part)
    grad_one, grad_ln1_gain, grad_ln1_bias = norm_one_back(grad_hidden)
    attn_low = grad_one.astype(jnp.bfloat16)
    grad_b_out = jnp.sum(grad_one, axis=0)
    back_query, back_key, back_value, back_out = (
        lax.all_gather(w_query.astype(jnp.bfloat16), "dp", axis=0, tiled=True),
        lax.all_gather(w_key.astype(jnp.bfloat16), "dp", axis=0, tiled=True),
        lax.all_gather(w_value.astype(jnp.bfloat16), "dp", axis=0, tiled=True),
        lax.all_gather(w_out.astype(jnp.bfloat16), "dp", axis=1, tiled=True),
    )
    grad_w_out = jnp.einsum("tc,td->cd", heads_rows, attn_low, preferred_element_type=jnp.float32)
    mixed_low = jnp.einsum(
        "td,cd->tc", attn_low, back_out, preferred_element_type=jnp.float32
    ).astype(jnp.bfloat16)
    grad_blocks = mixed_low.reshape(block_count, block_rows, heads_here, HEAD_DIM)

    def backward_block(carry, inputs):
        key_sum, value_sum = carry
        query_part, grad_part, lse_part = inputs
        probs = jnp.exp(score_block(query_part) - lse_part)
        grad_probs = jnp.einsum(
            "qhd,khd->hqk", grad_part, slot_values, preferred_element_type=jnp.float32
        )
        inner_sum = jnp.sum(probs * grad_probs, axis=-1, keepdims=True)
        score_low = (probs * (grad_probs - inner_sum)).astype(jnp.bfloat16)
        grad_query = (
            jnp.einsum("hqk,khd->qhd", score_low, slot_keys, preferred_element_type=jnp.float32)
            * score_scale
        )
        key_sum = (
            key_sum
            + jnp.einsum("hqk,qhd->khd", score_low, query_part, preferred_element_type=jnp.float32)
            * score_scale
        )
        value_sum = value_sum + jnp.einsum(
            "hqk,qhd->khd",
            probs.astype(jnp.bfloat16),
            grad_part,
            preferred_element_type=jnp.float32,
        )
        return ((key_sum, value_sum), grad_query)

    zero_slab = jnp.zeros((SLOT, heads_here, HEAD_DIM), jnp.float32)
    (key_sum, value_sum), grad_query_blocks = lax.scan(
        backward_block, (zero_slab, zero_slab), (query_blocks, grad_blocks, lse_blocks)
    )
    key_grad_slab = key_sum.reshape(shard_count, tok_rows, width_here)
    value_grad_slab = value_sum.reshape(shard_count, tok_rows, width_here)
    grad_key = jnp.sum(jnp.where(own_hit, key_grad_slab, 0.0), axis=0)
    grad_value = jnp.sum(jnp.where(own_hit, value_grad_slab, 0.0), axis=0)
    for step_by in offset_list:
        far_hit = (spot_ids == my_spot - step_by)[:, None, None]
        send_key = jnp.sum(jnp.where(far_hit, key_grad_slab, 0.0), axis=0)
        send_value = jnp.sum(jnp.where(far_hit, value_grad_slab, 0.0), axis=0)
        back_key_rows, back_value_rows = (
            passed_along(send_key.astype(jnp.bfloat16), "dp", -step_by).astype(send_key.dtype),
            passed_along(send_value.astype(jnp.bfloat16), "dp", -step_by).astype(send_value.dtype),
        )
        grad_key = grad_key + back_key_rows
        grad_value = grad_value + back_value_rows
    query_low = grad_query_blocks.reshape(tok_rows, width_here).astype(jnp.bfloat16)
    key_low = grad_key.astype(jnp.bfloat16)
    value_low = grad_value.astype(jnp.bfloat16)
    grad_w_query = jnp.einsum("td,tc->dc", tokens, query_low, preferred_element_type=jnp.float32)
    grad_w_key = jnp.einsum("td,tc->dc", tokens, key_low, preferred_element_type=jnp.float32)
    grad_w_value = jnp.einsum("td,tc->dc", tokens, value_low, preferred_element_type=jnp.float32)
    grad_b_query = jnp.sum(query_low.astype(jnp.float32), axis=0)
    grad_b_value = jnp.sum(value_low.astype(jnp.float32), axis=0)
    input_part = jnp.einsum("tc,dc->td", query_low, back_query, preferred_element_type=jnp.float32)
    input_part = input_part + jnp.einsum(
        "tc,dc->td", key_low, back_key, preferred_element_type=jnp.float32
    )
    input_part = input_part + jnp.einsum(
        "tc,dc->td", value_low, back_value, preferred_element_type=jnp.float32
    )
    grad_tokens = grad_one + tensor_total(input_part)
    grad_w_query, grad_w_key, grad_w_value, grad_w_out = (
        lax.psum_scatter(
            grad_w_query.astype(jnp.bfloat16), "dp", scatter_dimension=0, tiled=True
        ).astype(jnp.float32),
        lax.psum_scatter(
            grad_w_key.astype(jnp.bfloat16), "dp", scatter_dimension=0, tiled=True
        ).astype(jnp.float32),
        lax.psum_scatter(
            grad_w_value.astype(jnp.bfloat16), "dp", scatter_dimension=0, tiled=True
        ).astype(jnp.float32),
        lax.psum_scatter(
            grad_w_out.astype(jnp.bfloat16), "dp", scatter_dimension=1, tiled=True
        ).astype(jnp.float32),
    )
    (
        grad_b_query,
        grad_b_value,
        grad_b_inner,
        grad_b_out,
        grad_b_outer,
        grad_ln1_gain,
        grad_ln1_bias,
        grad_ln2_gain,
        grad_ln2_bias,
    ) = (
        lax.psum(grad_b_query.astype(jnp.bfloat16), "dp").astype(jnp.float32),
        lax.psum(grad_b_value.astype(jnp.bfloat16), "dp").astype(jnp.float32),
        lax.psum(grad_b_inner.astype(jnp.bfloat16), "dp").astype(jnp.float32),
        lax.psum(grad_b_out.astype(jnp.bfloat16), "dp").astype(jnp.float32),
        lax.psum(grad_b_outer.astype(jnp.bfloat16), "dp").astype(jnp.float32),
        lax.psum(grad_ln1_gain.astype(jnp.bfloat16), "dp").astype(jnp.float32),
        lax.psum(grad_ln1_bias.astype(jnp.bfloat16), "dp").astype(jnp.float32),
        lax.psum(grad_ln2_gain.astype(jnp.bfloat16), "dp").astype(jnp.float32),
        lax.psum(grad_ln2_bias.astype(jnp.bfloat16), "dp").astype(jnp.float32),
    )
    return (
        output,
        grad_tokens,
        grad_w_query,
        grad_w_key,
        grad_w_value,
        grad_b_query,
        grad_b_value,
        grad_w_out,
        grad_b_out,
        grad_ln1_gain,
        grad_ln1_bias,
        grad_w_inner,
        grad_b_inner,
        grad_w_outer,
        grad_b_outer,
        grad_ln2_gain,
        grad_ln2_bias,
    )


def solution(mesh):
    return jax.shard_map(
        on_device,
        mesh=mesh,
        in_specs=(
            P("dp", None),
            P("dp", None),
            P(),
            P(),
            P("dp", "tensor"),
            P("dp", "tensor"),
            P("dp", "tensor"),
            P("tensor"),
            P("tensor"),
            P("tensor", "dp"),
            P(),
            P(),
            P(),
            P("dp", "tensor"),
            P("tensor"),
            P("tensor", "dp"),
            P(),
            P(),
            P(),
        ),
        out_specs=(
            P("dp", None),
            P("dp", None),
            P("dp", "tensor"),
            P("dp", "tensor"),
            P("dp", "tensor"),
            P("tensor"),
            P("tensor"),
            P("tensor", "dp"),
            P(),
            P(),
            P(),
            P("dp", "tensor"),
            P("tensor"),
            P("tensor", "dp"),
            P(),
            P(),
            P(),
        ),
        check_vma=False,
    )
```

profile of v0, /device:TPU:0, one launch (start us, length us, event | category | flops | bytes accessed | tf_op | source)
XLA Modules:
  0.0 1807.0 jit_solution(10736105335624038911)
XLA Ops:
  14.7 27.4 %all-gather.9.cloned.1.call-done = bf16[2048,512]{1,0:T(8,128)(2,1)} async-done(((bf16[256,512]{1,0:T(8,128)(2,1)}), bf16[2048,512]{1,0:T(8,128)(2,1)}) %all-gather.9.cloned.1.call-update) | async-done | bytes 2097168 | tf_op jit(solution)/shard_map/all_gather | solution.py:82
  52.8 25.2 %all-gather.11.cloned.1.call-done = bf16[2048,512]{1,0:T(8,128)(2,1)} async-done(((bf16[256,512]{1,0:T(8,128)(2,1)}), bf16[2048,512]{1,0:T(8,128)(2,1)}) %all-gather.11.cloned.1.call-update) | async-done | bytes 2097168 | tf_op jit(solution)/shard_map/all_gather | solution.py:83
  90.7 26.6 %all-gather.7.cloned.1.call-done = bf16[2048,512]{1,0:T(8,128)(2,1)} async-done(((bf16[256,512]{1,0:T(8,128)(2,1)}), bf16[2048,512]{1,0:T(8,128)(2,1)}) %all-gather.7.cloned.1.call-update) | async-done | bytes 2097168 | tf_op jit(solution)/shard_map/all_gather | solution.py:81
  127.3 128.1 %while.31 = (s32[]{:T(128)}, bf16[2,512,4,128]{3,1,2,0:T(8,128)(2,1)}, f32[2,4,512,1]{2,1,3,0:T(4,128)S(1)}, bf16[2,512,4,128]{3,1,2,0:T(8,128)(2,1)}, s32[]{:T(...) while((s32[]{:T(128)}, ...), condition=%wide.region_5.6_spmd.clone.clone, body=%wide.region_2.5_spmd.clone.clone.sunk | while | flops 2204106752 | bytes 137967920 | solution.py:122
  164.4 14.5 select_select_fusion.6
  228.4 14.5 select_select_fusion.6
  271.5 169.2 %all-reduce.6.cloned.1.call-done = f32[1024,2048]{1,0:T(8,128)} async-done(((f32[1024,2048]{1,0:T(8,128)}), f32[1024,2048]{1,0:T(8,128)}) %all-reduce.6.cloned.1.call-update) | async-done | bytes 8388624 | tf_op jit(solution)/shard_map/psum | solution.py:34
  450.9 74.8 %all-gather.15.cloned.1.call-done = bf16[2048,2048]{1,0:T(8,128)(2,1)} async-done(((bf16[256,2048]{1,0:T(8,128)(2,1)}), bf16[2048,2048]{1,0:T(8,128)(2,1)}) %all-gather.15.cloned.1.call-update) | async-done | bytes 8388624 | tf_op jit(solution)/shard_map/all_gather | solution.py:130
  525.6 15.8 fusion.87
  541.4 67.5 %all-gather.17.cloned.1.call-done = bf16[2048,2048]{1,0:T(8,128)(2,1)} async-done(((bf16[2048,256]{1,0:T(8,128)(2,1)}), bf16[2048,2048]{1,0:T(8,128)(2,1)}) %all-gather.17.cloned.1.call-update) | async-done | bytes 8388624 | tf_op jit(solution)/shard_map/all_gather | solution.py:131
  608.9 17.3 fusion.85
  627.4 169.3 %all-reduce.8.cloned.1.call-done = f32[1024,2048]{1,0:T(8,128)} async-done(((f32[1024,2048]{1,0:T(8,128)}), f32[1024,2048]{1,0:T(8,128)}) %all-reduce.8.cloned.1.call-update) | async-done | bytes 8388624 | tf_op jit(solution)/shard_map/psum | solution.py:34
  818.3 23.3 %fusion.94 = (bf16[2048]{0:T(1024)(128)(2,1)}, bf16[1024,2048]{1,0:T(8,128)(2,1)}) fusion(bf16[2048,2048]{1,0:T(8,128)(2,1)} %all-gather.17.cloned.1.call-done, f32[1024,2048]{1,0:T(8,128)} %get-tuple-element.655, f32[1024]{0:T(1024)S(1)} %negate_multiply_fusion.1, f32[1024,2048]{1,0:T(8,128)} %fusion.87, f32[2048]{0:T(1024)S(1)} %copy-done.68), kind=kOutput, calls=%fused_computation.149 | convolution fusion | flops 8648652800 | bytes 29376512 | tf_op jit(solution)/shard_map/td,fd->tf/dot_general | solution.py:147
  841.6 14.5 fusion.95
  856.2 172.9 %all-reduce.10.cloned.1.call-done = f32[1024,2048]{1,0:T(8,128)} async-done(((f32[1024,2048]{1,0:T(8,128)}), f32[1024,2048]{1,0:T(8,128)}) %all-reduce.10.cloned.1.call-update) | async-done | bytes 8388624 | tf_op jit(solution)/shard_map/psum | solution.py:34
  1060.8 165.7 %while.32 = (s32[]{:T(128)}, f32[2048,4,128]{0,2,1:T(8,128)}, f32[2048,4,128]{0,2,1:T(8,128)}, bf16[2,512,4,128]{3,1,2,0:T(8,128)(2,1)}, bf16[2,512,4,128]{3,1,2...) while((s32[]{:T(128)}, f32[2048,4,128]{0,2,1:T(8,128)}, ...), condition=%wide.region_19.20_spmd.clone.clone.clone, body=%wide.region_17.19_spmd.clone.clone.clone.sunk | while | flops 5443420160 | bytes 367073888 | solution.py:206
  1081.8 14.4 select_select_fusion.7
  1248.6 47.1 %select_reduce_fusion.4 = (bf16[1024,512]{0,1:T(8,128)(2,1)}, bf16[1024,512]{0,1:T(8,128)(2,1)}, f32[1024,512]{0,1:T(8,128)S(1)}, f32[1024,512]{0,1:T(8,128)S(1)...) fusion(f32[2,1024,512]{1,0,2:T(2,128)} %reshape.188, pred[2]{0:T(512)(128)(4,1)S(1)} %copy-done.63, ...), kind=kLoop, calls=%fused_computation.97 | loop fusion | flops 9437184 | bytes 16777222 | tf_op jit(solution)/shard_map/reduce_sum | solution.py:215
  1333.9 15.4 convolution_convert_fusion.1
  1350.0 20.0 %convolution_convert_fusion = bf16[2048,2048]{1,0:T(8,128)(2,1)} fusion(f32[1024,2048]{1,0:T(8,128)} %get-tuple-element.655, f32[1024]{0:T(1024)S(1)} %copy-done.54, f32[1024,2048]{1,0:T(8,128)} %fusion.87, f32[2048]{0:T(1024)S(1)} %copy-done.69), kind=kOutput, calls=%fused_computation.84 | convolution fusion | flops 8619294720 | bytes 25178112 | tf_op jit(solution)/shard_map/tf,td->fd/dot_general | solution.py:146
  1402.8 88.4 %reduce-scatter.15.cloned.1.call-done = bf16[256,2048]{1,0:T(8,128)(2,1)} async-done(((bf16[2048,2048]{1,0:T(8,128)(2,1)}), bf16[256,2048]{1,0:T(8,128)(2,1)}) %reduce-scatter.15.cloned.1.call-update) | async-done | bytes 1048592 | tf_op jit(solution)/shard_map/reduce_scatter | solution.py:155
  1494.0 87.5 %reduce-scatter.17.cloned.1.call-done = bf16[2048,256]{1,0:T(8,128)(2,1)} async-done(((bf16[2048,2048]{1,0:T(8,128)(2,1)}), bf16[2048,256]{1,0:T(8,128)(2,1)}) %reduce-scatter.17.cloned.1.call-update) | async-done | bytes 1048592 | tf_op jit(solution)/shard_map/reduce_scatter | solution.py:158
  1584.2 172.1 %all-reduce.12.cloned.1.call-done = f32[1024,2048]{1,0:T(8,128)} async-done(((f32[1024,2048]{1,0:T(8,128)}), f32[1024,2048]{1,0:T(8,128)}) %all-reduce.12.cloned.1.call-update) | async-done | bytes 8388624 | tf_op jit(solution)/shard_map/psum | solution.py:34
  1766.4 28.6 %all-reduce = (bf16[512]{0:T(512)(128)(2,1)S(1)}, bf16[512]{0:T(512)(128)(2,1)S(1)}, bf16[2048]{0:T(1024)(128)(2,1)S(1)}, bf16[2048]{0:T(1024)(128)(2,1)S(1)}, b...) all-reduce(bf16[512]{0:T(512)(128)(2,1)S(1)} %bitcast.117, ...), channel_id=1, replica_groups=mesh['dp'=8,'tensor'=4] {'dp'}, use_global_device_ids=true, to_apply=%region_31.32 | all-reduce | flops 15360 | bytes 61440 | tf_op jit(solution)/shard_map/psum | solution.py:264
  (392 shorter events, 484.6 us)
Async XLA Ops:
  7.2 34.8 %all-gather.9.cloned.1.call-start = ((), (), s32[]{:S(2)}) async-start(), calls=%async_computation.7 | async-start | bytes 2359296 | tf_op jit(solution)/shard_map/all_gather | solution.py:82
  9.0 68.9 %all-gather.11.cloned.1.call-start = ((), (), s32[]{:S(2)}) async-start(), calls=%async_computation.8 | async-start | bytes 2359296 | tf_op jit(solution)/shard_map/all_gather | solution.py:83
  10.9 106.4 %all-gather.7.cloned.1.call-start = ((), (), s32[]{:S(2)}) async-start(), calls=%async_computation.6 | async-start | bytes 2359296 | tf_op jit(solution)/shard_map/all_gather | solution.py:81
  12.7 245.5 %all-gather.13.cloned.1.call-start = ((), (), s32[]{:S(2)}) async-start(), calls=%async_computation.9 | async-start | bytes 2359296 | tf_op jit(solution)/shard_map/all_gather | solution.py:84
  14.6 426.1 %all-reduce.6.cloned.1.call-start = ((), (), s32[]{:S(2)}) async-start(), calls=%async_computation.10 | async-start | bytes 16777216 | tf_op jit(solution)/shard_map/psum | solution.py:34
  47.3 78.9 %collective-permute-start.1 = (bf16[1024,512]{1,0:T(8,128)(2,1)S(1)}, bf16[1024,512]{1,0:T(8,128)(2,1)}, u32[]{:S(2)}, u32[]{:S(2)}) collective-permute-start(bf16[1024,512]{1,0:T(8,128)(2,1)S(1)} %convolution_convert_fusion.7), channel_id=1, source_target_pairs={{4,0},{8,4},{12,8},{16,12},{20,16},{24,20},{28,24},{5,1},{9,5},{13... | collective-permute-start | bytes 3145736 | tf_op jit(solution)/shard_map/ppermute | solution.py:16
  48.7 77.4 %collective-permute-start = (bf16[1024,512]{1,0:T(8,128)(2,1)S(1)}, bf16[1024,512]{1,0:T(8,128)(2,1)}, u32[]{:S(2)}, u32[]{:S(2)}) collective-permute-start(bf16[1024,512]{1,0:T(8,128)(2,1)S(1)} %convolution_convert_fusion.7), channel_id=1, source_target_pairs={{0,4},{4,8},{8,12},{12,16},{16,20},{20,24},{24,28},{1,5},{5,9},{9,... | collective-permute-start | bytes 3145736 | tf_op jit(solution)/shard_map/ppermute | solution.py:16
  83.2 43.0 %collective-permute-start.3 = (bf16[1024,512]{1,0:T(8,128)(2,1)S(1)}, bf16[1024,512]{1,0:T(8,128)(2,1)}, u32[]{:S(2)}, u32[]{:S(2)}) collective-permute-start(bf16[1024,512]{1,0:T(8,128)(2,1)S(1)} %add_convert_fusion.4), channel_id=1, source_target_pairs={{4,0},{8,4},{12,8},{16,12},{20,16},{24,20},{28,24},{5,1},{9,5},{13... | collective-permute-start | bytes 3145736 | tf_op jit(solution)/shard_map/ppermute | solution.py:16
  84.5 41.7 %collective-permute-start.2 = (bf16[1024,512]{1,0:T(8,128)(2,1)S(1)}, bf16[1024,512]{1,0:T(8,128)(2,1)}, u32[]{:S(2)}, u32[]{:S(2)}) collective-permute-start(bf16[1024,512]{1,0:T(8,128)(2,1)S(1)} %add_convert_fusion.4), channel_id=1, source_target_pairs={{0,4},{4,8},{8,12},{12,16},{16,20},{20,24},{24,28},{1,5},{5,9},{9,... | collective-permute-start | bytes 3145736 | tf_op jit(solution)/shard_map/ppermute | solution.py:16
  265.7 259.9 %all-gather.15.cloned.1.call-start = ((), (), s32[]{:S(2)}) async-start(), calls=%async_computation.11 | async-start | bytes 9437184 | tf_op jit(solution)/shard_map/all_gather | solution.py:130
  268.5 340.5 %all-gather.17.cloned.1.call-start = ((), (), s32[]{:S(2)}) async-start(), calls=%async_computation.12 | async-start | bytes 9437184 | tf_op jit(solution)/shard_map/all_gather | solution.py:131
  271.2 525.5 %all-reduce.8.cloned.1.call-start = ((), (), s32[]{:S(2)}) async-start(), calls=%async_computation.13 | async-start | bytes 16777216 | tf_op jit(solution)/shard_map/psum | solution.py:34
  626.3 402.8 %all-reduce.10.cloned.1.call-start = ((), (), s32[]{:S(2)}) async-start(), calls=%async_computation.14 | async-start | bytes 16777216 | tf_op jit(solution)/shard_map/psum | solution.py:34
  856.1 529.1 %reduce-scatter.13.cloned.1.call-start = ((), (), s32[]{:S(2)}) async-start(), calls=%async_computation.19 | async-start | bytes 2359296 | tf_op jit(solution)/shard_map/reduce_scatter | solution.py:249
  1059.6 327.4 %reduce-scatter.7.cloned.1.call-start = ((), (), s32[]{:S(2)}) async-start(), calls=%async_computation.16 | async-start | bytes 2359296 | tf_op jit(solution)/shard_map/reduce_scatter | solution.py:240
  1235.4 153.5 %reduce-scatter.11.cloned.1.call-start = ((), (), s32[]{:S(2)}) async-start(), calls=%async_computation.18 | async-start | bytes 2359296 | tf_op jit(solution)/shard_map/reduce_scatter | solution.py:246
  1295.7 4.8 collective-permute-start.7
  1297.0 5.7 collective-permute-start.6
  1306.9 93.9 %reduce-scatter.9.cloned.1.call-start = ((), (), s32[]{:S(2)}) async-start(), calls=%async_computation.17 | async-start | bytes 2359296 | tf_op jit(solution)/shard_map/reduce_scatter | solution.py:243
  1307.0 15.0 collective-permute-start.4
  1319.6 6.7 collective-permute-start.5
  1333.8 157.4 %reduce-scatter.15.cloned.1.call-start = ((), (), s32[]{:S(2)}) async-start(), calls=%async_computation.20 | async-start | bytes 9437184 | tf_op jit(solution)/shard_map/reduce_scatter | solution.py:155
  1349.3 232.1 %reduce-scatter.17.cloned.1.call-start = ((), (), s32[]{:S(2)}) async-start(), calls=%async_computation.21 | async-start | bytes 9437184 | tf_op jit(solution)/shard_map/reduce_scatter | solution.py:158
  1370.0 386.3 %all-reduce.12.cloned.1.call-start = ((), (), s32[]{:S(2)}) async-start(), calls=%async_computation.15 | async-start | bytes 16777216 | tf_op jit(solution)/shard_map/psum | solution.py:34
  (93 other events, 4400.3 us)
Sparse Core Ops, SparseCore 0:
  10.2 31.7 all-gather.8
  44.2 33.7 all-gather.10
  80.1 37.1 all-gather.6
  119.3 33.6 all-gather.12
  265.8 174.9 all-reduce.5
  442.8 82.7 all-gather.14
  527.9 81.0 all-gather.16
  626.4 170.2 all-reduce.7
  856.2 172.7 all-reduce.9
  1059.7 36.5 reduce-scatter.12
  1235.5 36.5 reduce-scatter.6
  1307.1 52.7 reduce-scatter.10
  1362.8 38.0 reduce-scatter.8
  1403.1 88.0 reduce-scatter.14
  1493.4 87.9 reduce-scatter.16
  1585.8 170.4 all-reduce.11
where the time goes:
time: 1810 us
  waiting for transfers between devices  1100 us (61%)
  matrix products  235 us (13%)
  other arithmetic  222 us (12%)
  local copies, waits for them, and re-layouts  175 us (10%)
  starting transfers between devices  30.9 us (2%)
  blocking collectives  28.6 us (2%)
    psum x4, waiting for transfers between devices, tensor_total(): return lax.psum(part, 'tensor')  684 us
    reduce_scatter x1, waiting for transfers between devices, on_device(): lax.psum_scatter(grad_w_inner.astype(jnp.bfloat16), 'dp', scatter_dimensi...  88.4 us
    reduce_scatter x1, waiting for transfers between devices, on_device(): lax.psum_scatter(grad_w_outer.astype(jnp.bfloat16), 'dp', scatter_dimensi...  87.5 us
    all_gather x1, waiting for transfers between devices, on_device(): lax.all_gather(w_inner.astype(jnp.bfloat16), 'dp', axis=0, tiled=True)  74.8 us
    all_gather x1, waiting for transfers between devices, on_device(): lax.all_gather(w_outer.astype(jnp.bfloat16), 'dp', axis=1, tiled=True)  67.5 us
    select_n x4, other arithmetic, on_device(): key_slab = jnp.where(far_hit, far_key[None], key_slab)  57.8 us
    dot_general x6, matrix products, mat_bf(): return jnp.dot(left, right, preferred_element_type=jnp.float32)  57 us
    reduce_sum x1, other arithmetic, on_device(): send_key = jnp.sum(jnp.where(far_hit, key_grad_slab, 0.0), axis=0)  47.1 us
  transfers between devices with their start and end apart: 24, of which 15 were waited for; matrix products, arithmetic and copies ran while one was open for 26% of the time, Pallas kernels for 0%

commit v1 on v0

v1 whole, which is shorter than its diff:
```python
import functools

import jax
import jax.numpy as jnp
from jax import lax
from jax.experimental import pallas as pl
from jax.experimental.pallas import tpu as pltpu
from jax.sharding import PartitionSpec as P

HEAD_DIM = 128
SLOT = 2048
LOG2E = 1.4426950408889634

norm_eps = 1e-12

F32 = jnp.float32
LOW = jnp.bfloat16
BOTH_LAST = (((1,), (1,)), ((), ()))
BOTH_FIRST = (((0,), (0,)), ((), ()))


def layer_norm(resid, gain, shift):
    center = resid - jnp.mean(resid, axis=-1, keepdims=True)
    spread = jnp.mean(center * center, axis=-1, keepdims=True)
    return center * lax.rsqrt(spread + norm_eps) * gain + shift


def gelu_tanh(inner):
    return 0.5 * inner * (1.0 + jnp.tanh(0.7978845608 * (inner + 0.044715 * inner * inner * inner)))


def mat_bf(left, right):
    return jnp.dot(left, right, preferred_element_type=F32)


def mat_last(left, right):
    return lax.dot_general(left, right, BOTH_LAST, preferred_element_type=F32)


def mat_first(left, right):
    return lax.dot_general(left, right, BOTH_FIRST, preferred_element_type=F32)


def swap(value, axis, flip):
    count = lax.axis_size(axis)
    return lax.ppermute(value, axis, [(source, source ^ flip) for source in range(count)])


def after(value, *others):
    return lax.optimization_barrier((value, *others))[0]


def gather_rows(block):
    half = block.shape[0] // 2
    one, two = swap(block, "tensor", 1), swap(block, "tensor", 2)
    three_top = swap(two[:half], "tensor", 1)
    three_low = swap(one[half:], "tensor", 2)
    rows = [block, one, two, three_top, three_low]
    count, flip = lax.axis_size("tensor"), 4
    while flip < count:
        rows.append(swap(jnp.concatenate(rows), "tensor", flip))
        flip *= 2
    return jnp.concatenate(rows)


def scatter_rows(part, rows):
    count = lax.axis_size("tensor")
    block = rows // count
    half = block // 2
    flip = count // 2
    extra = None
    while flip >= 4:
        away = part(flip * block, 2 * flip * block)
        if extra is not None:
            away = away + extra[flip * block :].astype(F32)
        come = swap(away.astype(LOW), "tensor", flip)
        extra = come if extra is None else extra[: flip * block].astype(F32) + come.astype(F32)
        flip //= 2

    def piece(k):
        value = part(k * block, (k + 1) * block)
        if extra is not None:
            value = value + extra[k * block : (k + 1) * block].astype(F32)
        return value

    three = piece(3).astype(LOW)
    come_top = swap(three[:half], "tensor", 1)
    come_low = swap(three[half:], "tensor", 2)
    one, two = piece(1), piece(2)
    one = jnp.concatenate([one[:half].astype(LOW), (one[half:] + come_low.astype(F32)).astype(LOW)])
    two = jnp.concatenate([(two[:half] + come_top.astype(F32)).astype(LOW), two[half:].astype(LOW)])
    come_one, come_two = swap(one, "tensor", 1), swap(two, "tensor", 2)
    return piece(0) + come_one.astype(F32) + come_two.astype(F32)


def fwd_kernel(q_ref,ko_ref,kf_ref,vo_ref,vf_ref,bo_ref,bf_ref,o_ref,l_ref,*,scale):
    q=q_ref[...]
    so=lax.dot_general(q,ko_ref[...],BOTH_LAST,preferred_element_type=F32)*scale+bo_ref[...]
    sf=lax.dot_general(q,kf_ref[...],BOTH_LAST,preferred_element_type=F32)*scale+bf_ref[...]
    top=jnp.maximum(jnp.max(so,axis=1,keepdims=True),jnp.max(sf,axis=1,keepdims=True))
    po=jnp.exp2(so-top); pf=jnp.exp2(sf-top)
    tot=jnp.sum(po,axis=1,keepdims=True)+jnp.sum(pf,axis=1,keepdims=True)
    o=jnp.dot(po.astype(LOW),vo_ref[...],preferred_element_type=F32)+jnp.dot(pf.astype(LOW),vf_ref[...],preferred_element_type=F32)
    o_ref[...]=(o/tot).astype(LOW)
    lse=top+jnp.log2(tot)
    l_ref[0]=jnp.transpose(jnp.broadcast_to(lse,(lse.shape[0],HEAD_DIM)))[0:1,:]
def attn_fwd(qkv,kv_far,bias_own,bias_far,heads,bq=256):
    rows=qkv.shape[0]
    scale=LOG2E*HEAD_DIM**-0.5
    return pl.pallas_call(
        functools.partial(fwd_kernel,scale=scale),
        grid=(heads,rows//bq),
        in_specs=[pl.BlockSpec((bq,HEAD_DIM),lambda h,i:(i,h)),
          pl.BlockSpec((rows,HEAD_DIM),lambda h,i:(0,heads+h)),
          pl.BlockSpec((rows,HEAD_DIM),lambda h,i:(0,h)),
          pl.BlockSpec((rows,HEAD_DIM),lambda h,i:(0,2*heads+h)),
          pl.BlockSpec((rows,HEAD_DIM),lambda h,i:(0,heads+h)),
          pl.BlockSpec((1,rows),lambda h,i:(0,0)),
          pl.BlockSpec((1,rows),lambda h,i:(0,0))],
        out_specs=[pl.BlockSpec((bq,HEAD_DIM),lambda h,i:(i,h)),pl.BlockSpec((1,1,bq),lambda h,i:(h,0,i))],
        out_shape=[jax.ShapeDtypeStruct((rows,heads*HEAD_DIM),LOW),jax.ShapeDtypeStruct((heads,1,rows),F32)],
        compiler_params=pltpu.CompilerParams(vmem_limit_bytes=48<<20),
        cost_estimate=pl.CostEstimate(flops=4*rows*2*rows*HEAD_DIM*heads,transcendentals=heads*rows*2*rows,bytes_accessed=heads*HEAD_DIM*rows*2*6),
        name='attention_forward')(qkv,qkv,kv_far,qkv,kv_far,bias_own,bias_far)

def bwd_kernel(q_ref,do_ref,o_ref,l_ref,ko_ref,kf_ref,vo_ref,vf_ref,bo_ref,bf_ref,dq_ref,dko_ref,dvo_ref,dkf_ref,dvf_ref,
               ako,avo,akf,avf,kto,ktf,*,scale,chunk):
    i=pl.program_id(1); last=pl.num_programs(1)-1
    @pl.when(i==0)
    def _():
        kto[...]=jnp.transpose(ko_ref[...]); ktf[...]=jnp.transpose(kf_ref[...])
        for a in (ako,avo,akf,avf): a[...]=jnp.zeros_like(a)
    q=q_ref[...]; do=do_ref[...]
    lse=l_ref[0]
    delta=jnp.sum(jnp.transpose(do.astype(F32)*o_ref[...].astype(F32)),axis=0,keepdims=True)
    rows=ko_ref.shape[0]; bq=q.shape[0]
    dqt=jnp.zeros((HEAD_DIM,bq),F32)
    for k_ref,v_ref,b_ref,ak,av,kt in ((ko_ref,vo_ref,bo_ref,ako,avo,kto),(kf_ref,vf_ref,bf_ref,akf,avf,ktf)):
        for c in range(rows//chunk):
            sl=pl.ds(c*chunk,chunk)
            st=lax.dot_general(k_ref[sl,:],q,BOTH_LAST,preferred_element_type=F32)
            b=b_ref[sl,:]
            b=jnp.concatenate([b]*(bq//HEAD_DIM),axis=1)
            p=jnp.exp2(st*scale+b-lse)
            dp=lax.dot_general(v_ref[sl,:],do,BOTH_LAST,preferred_element_type=F32)
            ds=(p*(dp-delta)).astype(LOW)
            av[sl,:]+=jnp.dot(p.astype(LOW),do,preferred_element_type=F32)
            ak[sl,:]+=jnp.dot(ds,q,preferred_element_type=F32)
            dqt=dqt+jnp.dot(kt[:,sl],ds,preferred_element_type=F32)
    s=HEAD_DIM**-0.5
    dq_ref[...]=(jnp.transpose(dqt)*s).astype(LOW)
    @pl.when(i==last)
    def _():
        dko_ref[...]=ako[...]*s; dvo_ref[...]=avo[...]
        dkf_ref[...]=(akf[...]*s).astype(LOW); dvf_ref[...]=avf[...].astype(LOW)
def attn_bwd(qkv,kv_far,do,o,lse,bias_own,bias_far,heads,bq=256,chunk=512):
    rows=qkv.shape[0]
    scale=LOG2E*HEAD_DIM**-0.5
    full=lambda off: pl.BlockSpec((rows,HEAD_DIM),lambda h,i:(0,off+h))
    qb=pl.BlockSpec((bq,HEAD_DIM),lambda h,i:(i,h))
    return pl.pallas_call(
        functools.partial(bwd_kernel,scale=scale,chunk=chunk),
        grid=(heads,rows//bq),
        in_specs=[qb,qb,qb,pl.BlockSpec((1,1,bq),lambda h,i:(h,0,i)),
          full(heads),full(0),full(2*heads),full(heads),
          pl.BlockSpec((rows,HEAD_DIM),lambda h,i:(0,0)),pl.BlockSpec((rows,HEAD_DIM),lambda h,i:(0,0))],
        out_specs=[qb,full(0),full(0),full(0),full(0)],
        out_shape=[jax.ShapeDtypeStruct((rows,heads*HEAD_DIM),LOW)]+[jax.ShapeDtypeStruct((rows,heads*HEAD_DIM),F32)]*2+[jax.ShapeDtypeStruct((rows,heads*HEAD_DIM),LOW)]*2,
        scratch_shapes=[pltpu.VMEM((rows,HEAD_DIM),F32)]*4+[pltpu.VMEM((HEAD_DIM,rows),LOW)]*2,
        compiler_params=pltpu.CompilerParams(vmem_limit_bytes=48<<20),
        cost_estimate=pl.CostEstimate(flops=10*rows*2*rows*HEAD_DIM*heads,transcendentals=heads*rows*2*rows,bytes_accessed=heads*HEAD_DIM*rows*2*12),
        name='attention_backward')(qkv,do,o,lse,qkv,kv_far,qkv,kv_far,bias_own,bias_far)


def on_device(
    tokens,
    cotangent,
    seq_lengths,
    slot_seq,
    w_query,
    w_key,
    w_value,
    b_query,
    b_value,
    w_out,
    b_out,
    ln1_gain,
    ln1_bias,
    w_inner,
    b_inner,
    w_outer,
    b_outer,
    ln2_gain,
    ln2_bias,
):
    tok_rows, model = tokens.shape
    assert SLOT == 2 * tok_rows
    tensor_count = lax.axis_size("tensor")
    tensor_place = lax.axis_index("tensor")
    block = tok_rows // tensor_count
    width_here = w_query.shape[1]
    heads_here = width_here // HEAD_DIM
    dp_place = lax.axis_index("dp")
    my_slot = dp_place // 2
    my_spot = dp_place % 2
    slot_ids = jnp.arange(slot_seq.shape[0])
    slot_lengths = jnp.sum(
        jnp.where(slot_seq[:, None] == slot_ids[None, :], seq_lengths[None, :], 0), axis=1
    )
    my_length = jnp.sum(jnp.where(slot_ids == my_slot, slot_lengths, 0))
    row_ids = jnp.arange(tok_rows)
    place = ((row_ids // block) ^ tensor_place) * block + row_ids % block
    own_bias = jnp.where(my_spot * tok_rows + place < my_length, 0.0, -1e30).astype(F32)
    far_bias = jnp.where((1 - my_spot) * tok_rows + place < my_length, 0.0, -1e30).astype(F32)
    own_bias_wide = jnp.broadcast_to(own_bias[:, None], (tok_rows, HEAD_DIM))
    far_bias_wide = jnp.broadcast_to(far_bias[:, None], (tok_rows, HEAD_DIM))

    def my_block(value):
        return lax.dynamic_slice_in_dim(value, tensor_place * block, block, 0)

    def reorder(value):
        return jnp.concatenate(
            [
                lax.dynamic_slice_in_dim(value, (tensor_place ^ k) * block, block, 0)
                for k in range(tensor_count)
            ]
        )

    row_live = (my_spot * tok_rows + place[:block] < my_length).astype(F32)
    rows_in = reorder(tokens)
    in_here = my_block(tokens).astype(F32)
    grad_out = my_block(cotangent).astype(F32) * row_live[:, None]

    low_qkv = jnp.concatenate([w_query, w_key, w_value], axis=1).astype(LOW)
    low_out = w_out.T.astype(LOW)
    low_inner = w_inner.astype(LOW)
    low_outer = w_outer.T.astype(LOW)
    full_qkv = lax.all_gather(low_qkv, "dp", axis=0, tiled=True)
    full_out = lax.all_gather(low_out, "dp", axis=0, tiled=True)
    full_inner = lax.all_gather(low_inner, "dp", axis=0, tiled=True)
    full_outer = lax.all_gather(low_outer, "dp", axis=0, tiled=True)

    b_qkv = jnp.concatenate([b_query, jnp.zeros_like(b_query), b_value])
    qkv = (mat_bf(rows_in, full_qkv) + b_qkv).astype(LOW)
    far_kv = swap(qkv[:, width_here:], "dp", 1)
    mixed, lse = attn_fwd(qkv, far_kv, own_bias[None], far_bias[None], heads_here)

    attn = scatter_rows(lambda a, b: mat_last(mixed[a:b], full_out), tok_rows)
    hidden, norm_one_back = jax.vjp(layer_norm, in_here + (attn + b_out), ln1_gain, ln1_bias)
    hidden_low = gather_rows(hidden.astype(LOW))
    inner = mat_bf(hidden_low, full_inner) + b_inner
    act_low = gelu_tanh(inner).astype(LOW)
    outer = scatter_rows(lambda a, b: mat_last(act_low[a:b], full_outer), tok_rows)
    output, norm_two_back = jax.vjp(layer_norm, hidden + (outer + b_outer), ln2_gain, ln2_bias)
    grad_two, grad_ln2_gain, grad_ln2_bias = norm_two_back(grad_out)
    grad_b_outer = jnp.sum(grad_two, axis=0)
    outer_low = gather_rows(grad_two.astype(LOW))
    output = reorder(gather_rows(after(output.astype(LOW), outer_low))).astype(F32)

    grad_w_outer = lax.psum_scatter(
        mat_first(outer_low, act_low).astype(LOW), "dp", scatter_dimension=0, tiled=True
    )
    grad_act = mat_bf(outer_low, full_outer)
    gelu_value, gelu_back = jax.vjp(gelu_tanh, inner)
    inner_low = gelu_back(grad_act)[0].astype(LOW)
    grad_b_inner = jnp.sum(inner_low.astype(F32), axis=0)
    grad_hidden = grad_two + scatter_rows(lambda a, b: mat_last(inner_low[a:b], full_inner), tok_rows)
    grad_w_inner = lax.psum_scatter(
        mat_first(hidden_low, inner_low).astype(LOW), "dp", scatter_dimension=0, tiled=True
    )
    grad_one, grad_ln1_gain, grad_ln1_bias = norm_one_back(grad_hidden)
    grad_b_out = jnp.sum(grad_one, axis=0)
    attn_low = gather_rows(grad_one.astype(LOW))
    mixed_low = mat_bf(attn_low, full_out).astype(LOW)
    grad_w_out = lax.psum_scatter(
        mat_first(attn_low, mixed).astype(LOW), "dp", scatter_dimension=0, tiled=True
    )
    query_low, own_key, own_value, far_key, far_value = attn_bwd(
        qkv, far_kv, mixed_low, mixed, lse, own_bias_wide, far_bias_wide, heads_here
    )
    key_low = (own_key + swap(far_key, "dp", 1).astype(F32)).astype(LOW)
    value_low = (own_value + swap(far_value, "dp", 1).astype(F32)).astype(LOW)
    qkv_low = jnp.concatenate([query_low, key_low, value_low], axis=1)
    grad_w_qkv = lax.psum_scatter(
        mat_first(rows_in, qkv_low).astype(LOW), "dp", scatter_dimension=0, tiled=True
    )
    grad_b_qkv = jnp.sum(qkv_low.astype(F32), axis=0)
    input_part = scatter_rows(lambda a, b: mat_last(qkv_low[a:b], full_qkv), tok_rows)
    grad_tokens = reorder(gather_rows((grad_one + input_part).astype(LOW))).astype(F32)

    over_rows = lax.psum(
        jnp.stack(
            [grad_b_out, grad_b_outer, grad_ln1_gain, grad_ln1_bias, grad_ln2_gain, grad_ln2_bias]
        ),
        ("dp", "tensor"),
    )
    grad_b_inner, grad_b_qkv = lax.psum((grad_b_inner, grad_b_qkv), "dp")
    grad_b_out, grad_b_outer, grad_ln1_gain, grad_ln1_bias, grad_ln2_gain, grad_ln2_bias = over_rows
    grad_w_query, grad_w_key, grad_w_value = jnp.split(grad_w_qkv.astype(F32), 3, axis=1)
    return (
        output,
        grad_tokens,
        grad_w_query,
        grad_w_key,
        grad_w_value,
        grad_b_qkv[:width_here],
        grad_b_qkv[2 * width_here :],
        grad_w_out.T.astype(F32),
        grad_b_out,
        grad_ln1_gain,
        grad_ln1_bias,
        grad_w_inner.astype(F32),
        grad_b_inner,
        grad_w_outer.T.astype(F32),
        grad_b_outer,
        grad_ln2_gain,
        grad_ln2_bias,
    )


def solution(mesh):
    return jax.shard_map(
        on_device,
        mesh=mesh,
        in_specs=(
            P("dp", None),
            P("dp", None),
            P(),
            P(),
            P("dp", "tensor"),
            P("dp", "tensor"),
            P("dp", "tensor"),
            P("tensor"),
            P("tensor"),
            P("tensor", "dp"),
            P(),
            P(),
            P(),
            P("dp", "tensor"),
            P("tensor"),
            P("tensor", "dp"),
            P(),
            P(),
            P(),
        ),
        out_specs=(
            P("dp", None),
            P("dp", None),
            P("dp", "tensor"),
            P("dp", "tensor"),
            P("dp", "tensor"),
            P("tensor"),
            P("tensor"),
            P("tensor", "dp"),
            P(),
            P(),
            P(),
            P("dp", "tensor"),
            P("tensor"),
            P("tensor", "dp"),
            P(),
            P(),
            P(),
        ),
        check_vma=False,
    )
```

time: 1810 us -> 783 us (0.43)
  waiting for transfers between devices: 1100 us -> 359 us
  other arithmetic: 222 us -> 40 us
  local copies, waits for them, and re-layouts: 175 us -> 42.7 us
  matrix products: 235 us -> 149 us
  Pallas kernels: 0 us -> 51.5 us
  blocking collectives: 28.6 us -> 71.3 us
    psum x4 -> x0, waiting for transfers between devices: 684 us -> none  [tensor_total(): return lax.psum(part, 'tensor')]
    ppermute x8 -> x39, waiting for transfers between devices: 7.59 us -> 228 us  [swap(): lax.ppermute(value, axis, [(source, source ^ flip) for source in range(co...]
    reduce_scatter x6 -> x4, waiting for transfers between devices: 186 us -> 15.8 us  [the longest x1 15.8 us: on_device(): lax.psum_scatter(mat_first(hidden_low, inner_low).astype(LOW), 'dp', scat...]
    broadcast_in_dim x54 -> x3, local copies, waits for them, and re-layouts: 109 us -> 0.38 us  [the longest x1 0.19 us: on_device(): far_bias_wide = jnp.broadcast_to(far_bias[:, None], (tok_rows, HEAD_DIM))]
    all_gather x6 -> x4, waiting for transfers between devices: 221 us -> 116 us  [the longest x1 59.2 us: on_device(): full_qkv = lax.all_gather(low_qkv, 'dp', axis=0, tiled=True)]
    dot_general x32 -> x24, matrix products: 235 us -> 149 us  [the longest x4 54.4 us: mat_bf(): return jnp.dot(left, right, preferred_element_type=F32)]
    select_n x4 -> x2, other arithmetic: 57.8 us -> 1.46 us  [the longest x1 0.79 us: on_device(): jnp.where(my_spot * tok_rows + place < my_length, 0.0, -1e+30).astype(F32)]
    reduce_sum x5 -> x1, other arithmetic: 55.2 us -> 0.63 us  [on_device(): grad_b_qkv = jnp.sum(qkv_low.astype(F32), axis=0)]
  transfers between devices with their start and end apart: 24 -> 47, of which waited for: 15 -> 31; matrix products, arithmetic and copies ran while one was open for 26% -> 22% of each run, Pallas kernels for 0% -> 7%
where the time goes in v1:
time: 783 us; the launch traced here: 774 us
  waiting for transfers between devices  359 us (46%)
  matrix products  149 us (19%)
  blocking collectives  71.3 us (9%)
  Pallas kernels  51.5 us (7%)
  starting transfers between devices  44.6 us (6%)
  local copies, waits for them, and re-layouts  42.7 us (5%)
  other arithmetic  40 us (5%)
  between operations  15.6 us (2%)
    ppermute x39, waiting for transfers between devices, swap(): lax.ppermute(value, axis, [(source, source ^ flip) for source in range(co...  228 us
    all_gather x1, waiting for transfers between devices, on_device(): full_qkv = lax.all_gather(low_qkv, 'dp', axis=0, tiled=True)  59.2 us
    all_gather x1, waiting for transfers between devices, on_device(): full_outer = lax.all_gather(low_outer, 'dp', axis=0, tiled=True)  56.9 us
    dot_general x4, matrix products, mat_bf(): return jnp.dot(left, right, preferred_element_type=F32)  54.4 us
    dot_general x16, matrix products, mat_last(): return lax.dot_general(left, right, BOTH_LAST, preferred_element_type=F32)  53.5 us
    ppermute x39, starting transfers between devices, swap(): lax.ppermute(value, axis, [(source, source ^ flip) for source in range(co...  44.3 us
    psum x1, blocking collectives, on_device(): lax.psum(jnp.stack([grad_b_out, grad_b_outer, grad_ln1_gain, grad_ln1_bia...  42.8 us
    dot_general x4, matrix products, mat_first(): return lax.dot_general(left, right, BOTH_FIRST, preferred_element_type=F32)  40.7 us
  transfers between devices with their start and end apart: 47, of which 31 were waited for; matrix products, arithmetic and copies ran while one was open for 22% of the time, Pallas kernels for 7%

profile of v1, /device:TPU:0, one launch (start us, length us, event | category | flops | bytes accessed | tf_op | source)
XLA Modules:
  0.0 773.8 jit_solution(34256271403297479)
XLA Ops:
  20.1 59.2 %all-gather.5.cloned.1.call-done = bf16[2048,1536]{1,0:T(8,128)(2,1)} async-done(((bf16[256,1536]{1,0:T(8,128)(2,1)}), bf16[2048,1536]{1,0:T(8,128)(2,1)}) %all-gather.5.cloned.1.call-update) | async-done | bytes 6291472 | tf_op jit(solution)/shard_map/all_gather | solution.py:238
  79.2 11.9 %add_convert_fusion.q_ref.ko_ref.vo_ref = bf16[1024,1536]{1,0:T(8,128)(2,1)S(1)} fusion(bf16[2048,1536]{1,0:T(8,128)(2,1)} %all-gather.5.cloned.1.call-done, f32[1536]{0:T(1024)S(1)} %pad_maximum_fusion.13, bf16[256,2048]{1,0:T(8,128)(2,1)S(1)} %get-tuple-element.104, bf16[256,2048]{1,0:T(8,128)(2,1)} %get-tuple-element.105, ...), kind=kOutput, calls=%fused_computation.16 | convolution fusion | flops 6462373888 | bytes 13637632 | tf_op jit(solution)/shard_map/dot_general | solution.py:33
  97.9 21.1 %attention_forward.1 = (bf16[1024,512]{1,0:T(8,128)(2,1)S(1)}, f32[4,1,1024]{2,1,0:T(1,128)S(1)}) custom-call(bf16[1024,1536]{1,0:T(8,128)(2,1)} %copy-done.14, bf16[1024,1536]{1,0:T(8,128)(2,1)} %copy-done.14, bf16[1024,1024]{1,0:T(8,128)(2,1)S(1)} %collective-permute-done.kf_ref.vf_ref, bf16[1024,1536]{1,0:T(8,128)(2,1)} %copy-done.14, ...), custom_call_target="tpu_custom_call" | custom-call | flops 4294967296 | bytes 6291456 | tf_op jit(solution)/shard_map/attention_forward/pallas_call | solution.py:110
  126.9 9.3 %collective-permute-done.1 = bf16[128,2048]{1,0:T(8,128)(2,1)S(1)} collective-permute-done((bf16[128,2048]{1,0:T(8,128)(2,1)S(1)}, bf16[128,2048]{1,0:T(8,128)(2,1)S(1)}, u32[]{:S(2)}, u32[]{:S(2)}) %collective-permute-start.1) | collective-permute-done | bytes 524320 | tf_op jit(solution)/shard_map/ppermute | solution.py:46
  139.8 21.2 %collective-permute-done.2 = bf16[256,2048]{1,0:T(8,128)(2,1)S(1)} collective-permute-done((bf16[256,2048]{1,0:T(8,128)(2,1)S(1)}, bf16[256,2048]{1,0:T(8,128)(2,1)S(1)}, u32[]{:S(2)}, u32[]{:S(2)}) %collective-permute-start.2) | collective-permute-done | bytes 1048608 | tf_op jit(solution)/shard_map/ppermute | solution.py:46
  167.7 21.4 %collective-permute-done.6 = bf16[256,2048]{1,0:T(8,128)(2,1)S(1)} collective-permute-done((bf16[256,2048]{1,0:T(8,128)(2,1)S(1)}, bf16[256,2048]{1,0:T(8,128)(2,1)S(1)}, u32[]{:S(2)}, u32[]{:S(2)}) %collective-permute-start.6) | collective-permute-done | bytes 1048608 | tf_op jit(solution)/shard_map/ppermute | solution.py:46
  203.0 17.5 %multiply_convert_fusion = (bf16[1024,2048]{1,0:T(8,128)(2,1)}, f32[1024,2048]{1,0:T(8,128)}) fusion(f32[2048]{0:T(1024)S(1)} %copy-done.33, bf16[1024,2048]{1,0:T(8,128)(2,1)} %constant_dynamic-update-slice_fusion, bf16[2048,2048]{1,0:T(8,128)(2,1)} %all-gather.9.cloned.1.call-done), kind=kOutput, calls=%fused_computation.11 | convolution fusion | flops 8610906112 | bytes 25174016 | tf_op jit(solution)/shard_map/dot_general | solution.py:33
  220.5 56.9 %all-gather.11.cloned.1.call-done = bf16[2048,2048]{0,1:T(8,128)(2,1)} async-done(((bf16[256,2048]{0,1:T(8,128)(2,1)}), bf16[2048,2048]{0,1:T(8,128)(2,1)}) %all-gather.11.cloned.1.call-update) | async-done | bytes 8388624 | tf_op jit(solution)/shard_map/all_gather | solution.py:241
  306.7 17.2 %collective-permute-done.10 = bf16[256,2048]{1,0:T(8,128)(2,1)S(1)} collective-permute-done((bf16[256,2048]{1,0:T(8,128)(2,1)S(1)}, bf16[256,2048]{1,0:T(8,128)(2,1)S(1)}, u32[]{:S(2)}, u32[]{:S(2)}) %collective-permute-start.10) | collective-permute-done | bytes 1048608 | tf_op jit(solution)/shard_map/ppermute | solution.py:46
  333.6 19.7 %collective-permute-done.14 = bf16[256,2048]{1,0:T(8,128)(2,1)S(1)} collective-permute-done((bf16[256,2048]{1,0:T(8,128)(2,1)S(1)}, bf16[256,2048]{1,0:T(8,128)(2,1)S(1)}, u32[]{:S(2)}, u32[]{:S(2)}) %collective-permute-start.14) | collective-permute-done | bytes 1048608 | tf_op jit(solution)/shard_map/ppermute | solution.py:46
  357.0 8.9 %collective-permute-done.15 = bf16[128,2048]{1,0:T(8,128)(2,1)S(1)} collective-permute-done((bf16[128,2048]{1,0:T(8,128)(2,1)S(1)}, bf16[128,2048]{1,0:T(8,128)(2,1)S(1)}, u32[]{:S(2)}, u32[]{:S(2)}) %collective-permute-start.15) | collective-permute-done | bytes 524320 | tf_op jit(solution)/shard_map/ppermute | solution.py:46
  366.1 20.5 %convert_reduce_fusion = (f32[2048]{0:T(1024)S(1)}, bf16[1024,2048]{1,0:T(8,128)(2,1)S(1)}) fusion(f32[1024,2048]{1,0:T(8,128)} %get-tuple-element.130, f32[2048]{0:T(1024)S(1)} %copy-done.33, bf16[1024,2048]{1,0:T(8,128)(2,1)S(1)} %constant_dynamic-update-slice_fusion.5, bf16[2048,2048]{0,1:T(8,128)(2,1)} %all-gather.11.cloned.1.call-done), kind=kOutput, calls=%fused_computation.10 | convolution fusion | flops 8646555648 | bytes 25182208 | tf_op jit(solution)/shard_map/dot_general | solution.py:33
  408.1 8.9 %collective-permute-done.23 = bf16[128,2048]{1,0:T(8,128)(2,1)S(1)} collective-permute-done((bf16[128,2048]{1,0:T(8,128)(2,1)S(1)}, bf16[128,2048]{1,0:T(8,128)(2,1)S(1)}, u32[]{:S(2)}, u32[]{:S(2)}) %collective-permute-start.23) | collective-permute-done | bytes 524320 | tf_op jit(solution)/shard_map/ppermute | solution.py:46
  421.6 13.1 %collective-permute-done.22 = bf16[256,2048]{1,0:T(8,128)(2,1)S(1)} collective-permute-done((bf16[256,2048]{1,0:T(8,128)(2,1)S(1)}, bf16[256,2048]{1,0:T(8,128)(2,1)S(1)}, u32[]{:S(2)}, u32[]{:S(2)}) %collective-permute-start.22) | collective-permute-done | bytes 1048608 | tf_op jit(solution)/shard_map/ppermute | solution.py:46
  440.2 18.4 %collective-permute-done.26 = bf16[256,2048]{1,0:T(8,128)(2,1)S(1)} collective-permute-done((bf16[256,2048]{1,0:T(8,128)(2,1)S(1)}, bf16[256,2048]{1,0:T(8,128)(2,1)S(1)}, u32[]{:S(2)}, u32[]{:S(2)}) %collective-permute-start.26) | collective-permute-done | bytes 1048608 | tf_op jit(solution)/shard_map/ppermute | solution.py:46
  477.9 14.2 %convolution_convert_fusion = bf16[2048,2048]{1,0:T(8,128)(2,1)} fusion(bf16[1024,2048]{1,0:T(8,128)(2,1)} %copy-done.22, bf16[1024,2048]{1,0:T(8,128)(2,1)} %get-tuple-element.129), kind=kOutput, calls=%fused_computation.12 | convolution fusion | flops 8594128896 | bytes 16777216 | tf_op jit(solution)/shard_map/dot_general | solution.py:41
  498.6 30.4 %attention_backward.1 = (bf16[1024,512]{1,0:T(8,128)(2,1)S(1)}, f32[1024,512]{1,0:T(8,128)}, f32[1024,512]{1,0:T(8,128)}, bf16[1024,512]{1,0:T(8,128)(2,1)S(1)}, bf16[1024,512]{1,0:T(8,128)(2,1)S(1)}) custom-call(bf16[1024,1536]{1,0:T(8,128)(2,1)} %copy-done.14, bf16[1024,512]{1,0:T(8,128)(2,1)S(1)} %convolution_convert_fusion.8.do_ref, ...), custom_call_target="tpu_custom_call" | custom-call | flops 10737418240 | bytes 12582912 | tf_op jit(solution)/shard_map/attention_backward/pallas_call | solution.py:161
  537.4 8.7 %convolution_convert_fusion.2 = bf16[2048,1536]{1,0:T(8,128)(2,1)} fusion(bf16[1024,1536]{1,0:T(8,128)(2,1)S(1)} %get-tuple-element.78, bf16[256,2048]{1,0:T(8,128)(2,1)S(1)} %copy-done.18, bf16[256,2048]{1,0:T(8,128)(2,1)S(1)} %copy-done.19, bf16[256,2048]{1,0:T(8,128)(2,1)S(1)} %copy-done.16, bf16[256,2048]{1,0:T(8,128)(2,1)S(1)} %copy-done.8), kind=kOutput, calls=%fused_computation.14 | convolution fusion | flops 6462373888 | bytes 13631488 | tf_op jit(solution)/shard_map/dot_general | solution.py:41
  546.2 14.1 %convolution_convert_fusion.1 = bf16[2048,2048]{1,0:T(8,128)(2,1)} fusion(bf16[1024,2048]{1,0:T(8,128)(2,1)} %constant_dynamic-update-slice_fusion, bf16[1024,2048]{1,0:T(8,128)(2,1)} %copy-done.36), kind=kOutput, calls=%fused_computation.13 | convolution fusion | flops 8594128896 | bytes 16777216 | tf_op jit(solution)/shard_map/dot_general | solution.py:41
  564.8 21.9 %collective-permute-done.18 = bf16[256,2048]{1,0:T(8,128)(2,1)S(1)} collective-permute-done((bf16[256,2048]{1,0:T(8,128)(2,1)S(1)}, bf16[256,2048]{1,0:T(8,128)(2,1)S(1)}, u32[]{:S(2)}, u32[]{:S(2)}) %collective-permute-start.18) | collective-permute-done | bytes 1048608 | tf_op jit(solution)/shard_map/ppermute | solution.py:46
  592.3 42.8 %psum.22 = f32[6,2048]{1,0:T(8,128)S(1)} all-reduce(f32[6,2048]{1,0:T(8,128)S(1)} %stack.15), channel_id=1, replica_groups=mesh['dp'=8,'tensor'=4] {'dp','tensor'}, use_global_device_ids=true, to_apply=%region_20.21 | all-reduce | flops 12288 | bytes 98304 | tf_op jit(solution)/shard_map/psum | solution.py:291
  670.1 13.8 %collective-permute-done.32 = bf16[256,2048]{1,0:T(8,128)(2,1)S(1)} collective-permute-done((bf16[256,2048]{1,0:T(8,128)(2,1)S(1)}, bf16[256,2048]{1,0:T(8,128)(2,1)S(1)}, u32[]{:S(2)}, u32[]{:S(2)}) %collective-permute-start.32) | collective-permute-done | bytes 1048608 | tf_op jit(solution)/shard_map/ppermute | solution.py:46
  693.5 28.5 %all-reduce = (f32[1536]{0:T(1024)S(1)}, f32[2048]{0:T(1024)}) all-reduce(f32[1536]{0:T(1024)S(1)} %get-tuple-element.77, f32[2048]{0:T(1024)S(1)} %get-tuple-element.75), channel_id=1, replica_groups=mesh['dp'=8,'tensor'=4] {'dp'}, use_global_device_ids=true, to_apply=%region_12.13 | all-reduce | flops 3584 | bytes 28672 | tf_op jit(solution)/shard_map/psum | solution.py:297
  748.2 15.8 %reduce-scatter.9.cloned.1.call-done = bf16[256,2048]{1,0:T(8,128)(2,1)} async-done(((bf16[2048,2048]{1,0:T(8,128)(2,1)}), bf16[256,2048]{1,0:T(8,128)(2,1)}) %reduce-scatter.9.cloned.1.call-update) | async-done | bytes 1048592 | tf_op jit(solution)/shard_map/reduce_scatter | solution.py:268
  (306 shorter events, 242.9 us)
Async XLA Ops:
  7.2 72.0 %all-gather.5.cloned.1.call-start = ((), (), s32[]{:S(2)}) async-start(), calls=%async_computation.4 | async-start | bytes 7077888 | tf_op jit(solution)/shard_map/all_gather | solution.py:238
  11.6 107.4 %all-gather.7.cloned.1.call-start = ((), (), s32[]{:S(2)}) async-start(), calls=%async_computation.5 | async-start | bytes 2359296 | tf_op jit(solution)/shard_map/all_gather | solution.py:239
  12.4 190.6 %all-gather.9.cloned.1.call-start = ((), (), s32[]{:S(2)}) async-start(), calls=%async_computation.6 | async-start | bytes 9437184 | tf_op jit(solution)/shard_map/all_gather | solution.py:240
  13.6 263.7 %all-gather.11.cloned.1.call-start = ((), (), s32[]{:S(2)}) async-start(), calls=%async_computation.7 | async-start | bytes 9437184 | tf_op jit(solution)/shard_map/all_gather | solution.py:241
  16.4 711.6 %reduce-scatter.7.cloned.1.call-start = ((), (), s32[]{:S(2)}) async-start(), calls=%async_computation.9 | async-start | bytes 2359296 | tf_op jit(solution)/shard_map/reduce_scatter | solution.py:275
  136.4 24.6 %collective-permute-start.2 = (bf16[256,2048]{1,0:T(8,128)(2,1)S(1)}, bf16[256,2048]{1,0:T(8,128)(2,1)S(1)}, u32[]{:S(2)}, u32[]{:S(2)}) collective-permute-start(bf16[256,2048]{1,0:T(8,128)(2,1)S(1)} %pad_maximum_fusion.2), channel_id=1, source_target_pairs={{0,1},{1,0},{2,3},{3,2},{4,5},{5,4},{6,7},{7,6},{8,9},{9,8},{10,11... | collective-permute-start | bytes 3145736 | tf_op jit(solution)/shard_map/ppermute | solution.py:46
  138.5 24.2 %collective-permute-start.4 = (bf16[256,2048]{1,0:T(8,128)(2,1)S(1)}, bf16[256,2048]{1,0:T(8,128)(2,1)S(1)}, u32[]{:S(2)}, u32[]{:S(2)}) collective-permute-start(bf16[256,2048]{1,0:T(8,128)(2,1)S(1)} %pad_maximum_fusion.3), channel_id=1, source_target_pairs={{0,2},{1,3},{2,0},{3,1},{4,6},{5,7},{6,4},{7,5},{8,10},{9,11},{10,... | collective-permute-start | bytes 3145736 | tf_op jit(solution)/shard_map/ppermute | solution.py:46
  165.8 23.3 %collective-permute-start.6 = (bf16[256,2048]{1,0:T(8,128)(2,1)S(1)}, bf16[256,2048]{1,0:T(8,128)(2,1)S(1)}, u32[]{:S(2)}, u32[]{:S(2)}) collective-permute-start(bf16[256,2048]{1,0:T(8,128)(2,1)S(1)} %get-tuple-element.93), channel_id=1, source_target_pairs={{0,2},{1,3},{2,0},{3,1},{4,6},{5,7},{6,4},{7,5},{8,10},{9,11},{10,... | collective-permute-start | bytes 3145736 | tf_op jit(solution)/shard_map/ppermute | solution.py:46
  167.0 23.8 %collective-permute-start.5 = (bf16[256,2048]{1,0:T(8,128)(2,1)S(1)}, bf16[256,2048]{1,0:T(8,128)(2,1)S(1)}, u32[]{:S(2)}, u32[]{:S(2)}) collective-permute-start(bf16[256,2048]{1,0:T(8,128)(2,1)S(1)} %get-tuple-element.93), channel_id=1, source_target_pairs={{0,1},{1,0},{2,3},{3,2},{4,5},{5,4},{6,7},{7,6},{8,9},{9,8},{10,11... | collective-permute-start | bytes 3145736 | tf_op jit(solution)/shard_map/ppermute | solution.py:46
  297.9 26.0 %collective-permute-start.10 = (bf16[256,2048]{1,0:T(8,128)(2,1)S(1)}, bf16[256,2048]{1,0:T(8,128)(2,1)S(1)}, u32[]{:S(2)}, u32[]{:S(2)}) collective-permute-start(bf16[256,2048]{1,0:T(8,128)(2,1)S(1)} %pad_maximum_fusion.4), channel_id=1, source_target_pairs={{0,1},{1,0},{2,3},{3,2},{4,5},{5,4},{6,7},{7,6},{8,9},{9,8},{10,11... | collective-permute-start | bytes 3145736 | tf_op jit(solution)/shard_map/ppermute | solution.py:46
  302.7 23.3 %collective-permute-start.12 = (bf16[256,2048]{1,0:T(8,128)(2,1)S(1)}, bf16[256,2048]{1,0:T(8,128)(2,1)S(1)}, u32[]{:S(2)}, u32[]{:S(2)}) collective-permute-start(bf16[256,2048]{1,0:T(8,128)(2,1)S(1)} %pad_maximum_fusion.5), channel_id=1, source_target_pairs={{0,2},{1,3},{2,0},{3,1},{4,6},{5,7},{6,4},{7,5},{8,10},{9,11},{10,... | collective-permute-start | bytes 3145736 | tf_op jit(solution)/shard_map/ppermute | solution.py:46
  332.1 24.6 %collective-permute-start.13 = (bf16[256,2048]{1,0:T(8,128)(2,1)S(1)}, bf16[256,2048]{1,0:T(8,128)(2,1)S(1)}, u32[]{:S(2)}, u32[]{:S(2)}) collective-permute-start(bf16[256,2048]{1,0:T(8,128)(2,1)S(1)} %get-tuple-element.87), channel_id=1, source_target_pairs={{0,1},{1,0},{2,3},{3,2},{4,5},{5,4},{6,7},{7,6},{8,9},{9,8},{10,11... | collective-permute-start | bytes 3145736 | tf_op jit(solution)/shard_map/ppermute | solution.py:46
  406.3 28.3 %collective-permute-start.22 = (bf16[256,2048]{1,0:T(8,128)(2,1)S(1)}, bf16[256,2048]{1,0:T(8,128)(2,1)S(1)}, u32[]{:S(2)}, u32[]{:S(2)}) collective-permute-start(bf16[256,2048]{1,0:T(8,128)(2,1)S(1)} %pad_maximum_fusion.6), channel_id=1, source_target_pairs={{0,1},{1,0},{2,3},{3,2},{4,5},{5,4},{6,7},{7,6},{8,9},{9,8},{10,11... | collective-permute-start | bytes 3145736 | tf_op jit(solution)/shard_map/ppermute | solution.py:46
  438.7 23.9 %collective-permute-start.25 = (bf16[256,2048]{1,0:T(8,128)(2,1)S(1)}, bf16[256,2048]{1,0:T(8,128)(2,1)S(1)}, u32[]{:S(2)}, u32[]{:S(2)}) collective-permute-start(bf16[256,2048]{1,0:T(8,128)(2,1)S(1)} %get-tuple-element.82), channel_id=1, source_target_pairs={{0,1},{1,0},{2,3},{3,2},{4,5},{5,4},{6,7},{7,6},{8,9},{9,8},{10,11... | collective-permute-start | bytes 3145736 | tf_op jit(solution)/shard_map/ppermute | solution.py:46
  477.8 264.8 %reduce-scatter.11.cloned.1.call-start = ((), (), s32[]{:S(2)}) async-start(), calls=%async_computation.11 | async-start | bytes 9437184 | tf_op jit(solution)/shard_map/reduce_scatter | solution.py:260
  492.1 253.8 %reduce-scatter.5.cloned.1.call-start = ((), (), s32[]{:S(2)}) async-start(), calls=%async_computation.8 | async-start | bytes 7077888 | tf_op jit(solution)/shard_map/reduce_scatter | solution.py:284
  546.2 217.8 %reduce-scatter.9.cloned.1.call-start = ((), (), s32[]{:S(2)}) async-start(), calls=%async_computation.10 | async-start | bytes 9437184 | tf_op jit(solution)/shard_map/reduce_scatter | solution.py:268
  561.5 25.3 %collective-permute-start.18 = (bf16[256,2048]{1,0:T(8,128)(2,1)S(1)}, bf16[256,2048]{1,0:T(8,128)(2,1)S(1)}, u32[]{:S(2)}, u32[]{:S(2)}) collective-permute-start(bf16[256,2048]{1,0:T(8,128)(2,1)S(1)} %copy-done.9), channel_id=1, source_target_pairs={{0,2},{1,3},{2,0},{3,1},{4,6},{5,7},{6,4},{7,5},{8,10},{9,11},{10,... | collective-permute-start | bytes 3145736 | tf_op jit(solution)/shard_map/ppermute | solution.py:46
  561.5 26.8 %collective-permute-start.17 = (bf16[256,2048]{1,0:T(8,128)(2,1)S(1)}, bf16[256,2048]{1,0:T(8,128)(2,1)S(1)}, u32[]{:S(2)}, u32[]{:S(2)}) collective-permute-start(bf16[256,2048]{1,0:T(8,128)(2,1)S(1)} %copy-done.9), channel_id=1, source_target_pairs={{0,1},{1,0},{2,3},{3,2},{4,5},{5,4},{6,7},{7,6},{8,9},{9,8},{10,11... | collective-permute-start | bytes 3145736 | tf_op jit(solution)/shard_map/ppermute | solution.py:46
  587.6 47.5 %collective-permute-start.19 = (bf16[128,2048]{1,0:T(8,128)(2,1)}, bf16[128,2048]{1,0:T(8,128)(2,1)}, u32[]{:S(2)}, u32[]{:S(2)}) collective-permute-start(bf16[128,2048]{1,0:T(8,128)(2,1)} %slice.245), channel_id=1, source_target_pairs={{0,1},{1,0},{2,3},{3,2},{4,5},{5,4},{6,7},{7,6},{8,9},{9,8},{10,11... | collective-permute-start | bytes 1572872 | tf_op jit(solution)/shard_map/ppermute | solution.py:46
  588.3 76.5 %collective-permute-start.20 = (bf16[128,2048]{1,0:T(8,128)(2,1)S(1)}, bf16[128,2048]{1,0:T(8,128)(2,1)S(1)}, u32[]{:S(2)}, u32[]{:S(2)}) collective-permute-start(bf16[128,2048]{1,0:T(8,128)(2,1)S(1)} %slice.246), channel_id=1, source_target_pairs={{0,2},{1,3},{2,0},{3,1},{4,6},{5,7},{6,4},{7,5},{8,10},{9,11},{10,... | collective-permute-start | bytes 1572872 | tf_op jit(solution)/shard_map/ppermute | solution.py:46
  656.1 27.7 %collective-permute-start.32 = (bf16[256,2048]{1,0:T(8,128)(2,1)S(1)}, bf16[256,2048]{1,0:T(8,128)(2,1)S(1)}, u32[]{:S(2)}, u32[]{:S(2)}) collective-permute-start(bf16[256,2048]{1,0:T(8,128)(2,1)S(1)} %pad_maximum_fusion.8), channel_id=1, source_target_pairs={{0,1},{1,0},{2,3},{3,2},{4,5},{5,4},{6,7},{7,6},{8,9},{9,8},{10,11... | collective-permute-start | bytes 3145736 | tf_op jit(solution)/shard_map/ppermute | solution.py:46
  687.1 38.3 %collective-permute-start.35 = (bf16[256,2048]{1,0:T(8,128)(2,1)S(1)}, bf16[256,2048]{1,0:T(8,128)(2,1)S(1)}, u32[]{:S(2)}, u32[]{:S(2)}) collective-permute-start(bf16[256,2048]{1,0:T(8,128)(2,1)S(1)} %get-tuple-element.80), channel_id=1, source_target_pairs={{0,1},{1,0},{2,3},{3,2},{4,5},{5,4},{6,7},{7,6},{8,9},{9,8},{10,11... | collective-permute-start | bytes 3145736 | tf_op jit(solution)/shard_map/ppermute | solution.py:46
  688.3 34.3 %collective-permute-start.36 = (bf16[256,2048]{1,0:T(8,128)(2,1)S(1)}, bf16[256,2048]{1,0:T(8,128)(2,1)S(1)}, u32[]{:S(2)}, u32[]{:S(2)}) collective-permute-start(bf16[256,2048]{1,0:T(8,128)(2,1)S(1)} %get-tuple-element.80), channel_id=1, source_target_pairs={{0,2},{1,3},{2,0},{3,1},{4,6},{5,7},{6,4},{7,5},{8,10},{9,11},{10,... | collective-permute-start | bytes 3145736 | tf_op jit(solution)/shard_map/ppermute | solution.py:46
  (65 other events, 1296.6 us)
Sparse Core Ops, SparseCore 0:
  11.7 67.4 all-gather.4
  81.4 29.4 all-gather.6
  113.1 81.1 all-gather.8
  196.3 81.0 all-gather.10
  478.0 33.4 reduce-scatter.6
  513.6 88.3 reduce-scatter.10
  604.3 69.0 reduce-scatter.4
  675.7 88.2 reduce-scatter.8

commit v2 on v1

--- a/solution.py
+++ b/solution.py
@@ -48,6 +48,15 @@
 
 def after(value, *others):
     return lax.optimization_barrier((value, *others))[0]
+
+
+def everyone(value, axes):
+    for axis in axes:
+        flip = 1
+        while flip < lax.axis_size(axis):
+            value = value + swap(value, axis, flip)
+            flip *= 2
+    return value
 
 
 def gather_rows(block):
@@ -231,12 +240,11 @@
     in_here = my_block(tokens).astype(F32)
     grad_out = my_block(cotangent).astype(F32) * row_live[:, None]
 
-    low_qkv = jnp.concatenate([w_query, w_key, w_value], axis=1).astype(LOW)
-    low_out = w_out.T.astype(LOW)
+    low_attn = jnp.concatenate([w_query, w_key, w_value, w_out.T], axis=1).astype(LOW)
     low_inner = w_inner.astype(LOW)
     low_outer = w_outer.T.astype(LOW)
-    full_qkv = lax.all_gather(low_qkv, "dp", axis=0, tiled=True)
-    full_out = lax.all_gather(low_out, "dp", axis=0, tiled=True)
+    full_attn = lax.all_gather(low_attn, "dp", axis=0, tiled=True)
+    full_qkv, full_out = full_attn[:, : 3 * width_here], full_attn[:, 3 * width_here :]
     full_inner = lax.all_gather(low_inner, "dp", axis=0, tiled=True)
     full_outer = lax.all_gather(low_outer, "dp", axis=0, tiled=True)
 
@@ -257,46 +265,45 @@
     outer_low = gather_rows(grad_two.astype(LOW))
     output = reorder(gather_rows(after(output.astype(LOW), outer_low))).astype(F32)
 
-    grad_w_outer = lax.psum_scatter(
-        mat_first(outer_low, act_low).astype(LOW), "dp", scatter_dimension=0, tiled=True
-    )
-    grad_act = mat_bf(outer_low, full_outer)
+    grad_w_outer = mat_first(outer_low, act_low).astype(LOW)
+    grad_act = mat_bf(after(outer_low, grad_w_outer), full_outer)
     gelu_value, gelu_back = jax.vjp(gelu_tanh, inner)
     inner_low = gelu_back(grad_act)[0].astype(LOW)
     grad_b_inner = jnp.sum(inner_low.astype(F32), axis=0)
     grad_hidden = grad_two + scatter_rows(lambda a, b: mat_last(inner_low[a:b], full_inner), tok_rows)
-    grad_w_inner = lax.psum_scatter(
-        mat_first(hidden_low, inner_low).astype(LOW), "dp", scatter_dimension=0, tiled=True
-    )
+    grad_w_inner = mat_first(hidden_low, inner_low).astype(LOW)
+    grad_hidden = after(grad_hidden, grad_w_inner)
     grad_one, grad_ln1_gain, grad_ln1_bias = norm_one_back(grad_hidden)
     grad_b_out = jnp.sum(grad_one, axis=0)
     attn_low = gather_rows(grad_one.astype(LOW))
     mixed_low = mat_bf(attn_low, full_out).astype(LOW)
-    grad_w_out = lax.psum_scatter(
-        mat_first(attn_low, mixed).astype(LOW), "dp", scatter_dimension=0, tiled=True
-    )
+    grad_w_out = mat_first(attn_low, mixed).astype(LOW)
     query_low, own_key, own_value, far_key, far_value = attn_bwd(
         qkv, far_kv, mixed_low, mixed, lse, own_bias_wide, far_bias_wide, heads_here
     )
     key_low = (own_key + swap(far_key, "dp", 1).astype(F32)).astype(LOW)
     value_low = (own_value + swap(far_value, "dp", 1).astype(F32)).astype(LOW)
     qkv_low = jnp.concatenate([query_low, key_low, value_low], axis=1)
-    grad_w_qkv = lax.psum_scatter(
-        mat_first(rows_in, qkv_low).astype(LOW), "dp", scatter_dimension=0, tiled=True
+    grad_w_qkv = mat_first(rows_in, qkv_low).astype(LOW)
+    grad_w_attn = jnp.concatenate([grad_w_qkv, grad_w_out], axis=1)
+    grad_w_outer, grad_w_inner, grad_w_attn = (
+        lax.psum_scatter(grad, "dp", scatter_dimension=0, tiled=True).astype(F32)
+        for grad in (grad_w_outer, grad_w_inner, grad_w_attn)
     )
     grad_b_qkv = jnp.sum(qkv_low.astype(F32), axis=0)
     input_part = scatter_rows(lambda a, b: mat_last(qkv_low[a:b], full_qkv), tok_rows)
     grad_tokens = reorder(gather_rows((grad_one + input_part).astype(LOW))).astype(F32)
 
-    over_rows = lax.psum(
+    over_rows = everyone(
         jnp.stack(
             [grad_b_out, grad_b_outer, grad_ln1_gain, grad_ln1_bias, grad_ln2_gain, grad_ln2_bias]
         ),
-        ("dp", "tensor"),
-    )
-    grad_b_inner, grad_b_qkv = lax.psum((grad_b_inner, grad_b_qkv), "dp")
+        ("tensor", "dp"),
+    )
+    grad_b_inner = everyone(grad_b_inner, ("dp",))
+    grad_b_qkv = everyone(grad_b_qkv, ("dp",))
     grad_b_out, grad_b_outer, grad_ln1_gain, grad_ln1_bias, grad_ln2_gain, grad_ln2_bias = over_rows
-    grad_w_query, grad_w_key, grad_w_value = jnp.split(grad_w_qkv.astype(F32), 3, axis=1)
+    grad_w_query, grad_w_key, grad_w_value, grad_w_out = jnp.split(grad_w_attn, 4, axis=1)
     return (
         output,
         grad_tokens,
@@ -305,13 +312,13 @@
         grad_w_value,
         grad_b_qkv[:width_here],
         grad_b_qkv[2 * width_here :],
-        grad_w_out.T.astype(F32),
+        grad_w_out.T,
         grad_b_out,
         grad_ln1_gain,
         grad_ln1_bias,
-        grad_w_inner.astype(F32),
+        grad_w_inner,
         grad_b_inner,
-        grad_w_outer.T.astype(F32),
+        grad_w_outer.T,
         grad_b_outer,
         grad_ln2_gain,
         grad_ln2_bias,

time: 783 us -> 721 us (0.921)
  blocking collectives: 71.3 us -> 0 us
  waiting for transfers between devices: 359 us -> 345 us
  starting transfers between devices: 44.6 us -> 55.7 us
  matrix products: 149 us -> 159 us
    psum x2 -> x0, blocking collectives: 71.3 us -> none  [the longest x1 42.8 us: on_device(): lax.psum(jnp.stack([grad_b_out, grad_b_outer, grad_ln1_gain, grad_ln1_bia...]
    all_gather x1, waiting for transfers between devices: 56.9 us -> 21.3 us  [on_device(): full_outer = lax.all_gather(low_outer, 'dp', axis=0, tiled=True)]
    all_gather x2 -> x1, waiting for transfers between devices: 59.2 us -> 77.6 us  [on_device(): full_attn = lax.all_gather(low_attn, 'dp', axis=0, tiled=True)]
    ppermute x39 -> x50, waiting for transfers between devices: 228 us -> 246 us  [swap(): lax.ppermute(value, axis, [(source, source ^ flip) for source in range(co...]
    reduce_scatter x4 -> x3, waiting for transfers between devices: 15.8 us -> 0.01 us  [on_device(): lax.psum_scatter(grad, 'dp', scatter_dimension=0, tiled=True).astype(F32)]
    ppermute x39 -> x50, starting transfers between devices: 44.3 us -> 55.1 us  [swap(): lax.ppermute(value, axis, [(source, source ^ flip) for source in range(co...]
    dot_general x4, matrix products: 40.7 us -> 49.3 us  [mat_first(): return lax.dot_general(left, right, BOTH_FIRST, preferred_element_type=F32)]
    concatenate x1 -> x2, other arithmetic: 0.93 us -> 8.77 us  [the longest x1 7.73 us: on_device(): grad_w_attn = jnp.concatenate([grad_w_qkv, grad_w_out], axis=1)]
  transfers between devices with their start and end apart: 47 -> 56, of which waited for: 31 -> 37; matrix products, arithmetic and copies ran while one was open for 22% -> 27% of each run, Pallas kernels for 7% -> 7%
where the time goes in v2:
time: 721 us; the launch traced here: 712 us
  waiting for transfers between devices  345 us (48%)
  matrix products  159 us (22%)
  starting transfers between devices  55.7 us (8%)
  Pallas kernels  51.1 us (7%)
  local copies, waits for them, and re-layouts  43.7 us (6%)
  other arithmetic  42.2 us (6%)
  between operations  15.9 us (2%)
    ppermute x50, waiting for transfers between devices, swap(): lax.ppermute(value, axis, [(source, source ^ flip) for source in range(co...  246 us
    all_gather x1, waiting for transfers between devices, on_device(): full_attn = lax.all_gather(low_attn, 'dp', axis=0, tiled=True)  77.6 us
    ppermute x50, starting transfers between devices, swap(): lax.ppermute(value, axis, [(source, source ^ flip) for source in range(co...  55.1 us
    dot_general x4, matrix products, mat_bf(): return jnp.dot(left, right, preferred_element_type=F32)  55.1 us
    dot_general x16, matrix products, mat_last(): return lax.dot_general(left, right, BOTH_LAST, preferred_element_type=F32)  54.3 us
    dot_general x4, matrix products, mat_first(): return lax.dot_general(left, right, BOTH_FIRST, preferred_element_type=F32)  49.3 us
    pallas_call x1, Pallas kernels, attn_bwd(): pl.pallas_call(functools.partial(bwd_kernel, scale=scale, chunk=chunk), g...  30 us
    unnamed x119, local copies, waits for them, and re-layouts  26.9 us
  transfers between devices with their start and end apart: 56, of which 37 were waited for; matrix products, arithmetic and copies ran while one was open for 27% of the time, Pallas kernels for 7%

profile of v2, /device:TPU:0, one launch (start us, length us, event | category | flops | bytes accessed | tf_op | source)
XLA Modules:
  0.0 711.8 jit_solution(17271171941195478409)
XLA Ops:
  20.8 77.6 %all-gather.4.cloned.1.call-done = bf16[2048,2048]{0,1:T(8,128)(2,1)} async-done(((bf16[256,2048]{0,1:T(8,128)(2,1)}), bf16[2048,2048]{0,1:T(8,128)(2,1)}) %all-gather.4.cloned.1.call-update) | async-done | bytes 8388624 | tf_op jit(solution)/shard_map/all_gather | solution.py:246
  98.4 11.9 %add_convert_fusion.q_ref.ko_ref.vo_ref = bf16[1024,1536]{1,0:T(8,128)(2,1)S(1)} fusion(bf16[2048,2048]{0,1:T(8,128)(2,1)} %all-gather.4.cloned.1.call-done, f32[1536]{0:T(1024)S(1)} %pad_maximum_fusion.14, bf16[256,2048]{1,0:T(8,128)(2,1)S(1)} %get-tuple-element.105, bf16[256,2048]{1,0:T(8,128)(2,1)} %get-tuple-element.106, ...), kind=kOutput, calls=%fused_computation.17 | convolution fusion | flops 6462373888 | bytes 13637632 | tf_op jit(solution)/shard_map/dot_general | solution.py:33
  118.0 21.1 %attention_forward.1 = (bf16[1024,512]{1,0:T(8,128)(2,1)S(1)}, f32[4,1,1024]{2,1,0:T(1,128)S(1)}) custom-call(bf16[1024,1536]{1,0:T(8,128)(2,1)} %copy-done.15, bf16[1024,1536]{1,0:T(8,128)(2,1)} %copy-done.15, bf16[1024,1024]{1,0:T(8,128)(2,1)S(1)} %collective-permute-done.kf_ref.vf_ref, bf16[1024,1536]{1,0:T(8,128)(2,1)} %copy-done.15, ...), custom_call_target="tpu_custom_call" | custom-call | flops 4294967296 | bytes 6291456 | tf_op jit(solution)/shard_map/attention_forward/pallas_call | solution.py:119
  161.0 21.2 %collective-permute-done.2 = bf16[256,2048]{1,0:T(8,128)(2,1)S(1)} collective-permute-done((bf16[256,2048]{1,0:T(8,128)(2,1)S(1)}, bf16[256,2048]{1,0:T(8,128)(2,1)S(1)}, u32[]{:S(2)}, u32[]{:S(2)}) %collective-permute-start.2) | collective-permute-done | bytes 1048608 | tf_op jit(solution)/shard_map/ppermute | solution.py:46
  191.0 20.5 %collective-permute-done.6 = bf16[256,2048]{1,0:T(8,128)(2,1)S(1)} collective-permute-done((bf16[256,2048]{1,0:T(8,128)(2,1)S(1)}, bf16[256,2048]{1,0:T(8,128)(2,1)S(1)}, u32[]{:S(2)}, u32[]{:S(2)}) %collective-permute-start.6) | collective-permute-done | bytes 1048608 | tf_op jit(solution)/shard_map/ppermute | solution.py:46
  216.4 7.2 %collective-permute-done.7 = bf16[128,2048]{1,0:T(8,128)(2,1)S(1)} collective-permute-done((bf16[128,2048]{1,0:T(8,128)(2,1)S(1)}, bf16[128,2048]{1,0:T(8,128)(2,1)S(1)}, u32[]{:S(2)}, u32[]{:S(2)}) %collective-permute-start.7) | collective-permute-done | bytes 524320 | tf_op jit(solution)/shard_map/ppermute | solution.py:46
  225.2 17.0 %multiply_convert_fusion = (bf16[1024,2048]{1,0:T(8,128)(2,1)}, f32[1024,2048]{1,0:T(8,128)}) fusion(f32[2048]{0:T(1024)S(1)} %copy-done.38, bf16[1024,2048]{1,0:T(8,128)(2,1)} %constant_dynamic-update-slice_fusion, bf16[2048,2048]{1,0:T(8,128)(2,1)} %all-gather.6.cloned.1.call-done), kind=kOutput, calls=%fused_computation.12 | convolution fusion | flops 8610906112 | bytes 25174016 | tf_op jit(solution)/shard_map/dot_general | solution.py:33
  242.3 21.3 %all-gather.8.cloned.1.call-done = bf16[2048,2048]{0,1:T(8,128)(2,1)} async-done(((bf16[256,2048]{0,1:T(8,128)(2,1)}), bf16[2048,2048]{0,1:T(8,128)(2,1)}) %all-gather.8.cloned.1.call-update) | async-done | bytes 8388624 | tf_op jit(solution)/shard_map/all_gather | solution.py:249
  292.8 17.3 %collective-permute-done.10 = bf16[256,2048]{1,0:T(8,128)(2,1)S(1)} collective-permute-done((bf16[256,2048]{1,0:T(8,128)(2,1)S(1)}, bf16[256,2048]{1,0:T(8,128)(2,1)S(1)}, u32[]{:S(2)}, u32[]{:S(2)}) %collective-permute-start.10) | collective-permute-done | bytes 1048608 | tf_op jit(solution)/shard_map/ppermute | solution.py:46
  318.7 19.7 %collective-permute-done.14 = bf16[256,2048]{1,0:T(8,128)(2,1)S(1)} collective-permute-done((bf16[256,2048]{1,0:T(8,128)(2,1)S(1)}, bf16[256,2048]{1,0:T(8,128)(2,1)S(1)}, u32[]{:S(2)}, u32[]{:S(2)}) %collective-permute-start.14) | collective-permute-done | bytes 1048608 | tf_op jit(solution)/shard_map/ppermute | solution.py:46
  342.2 9.0 %collective-permute-done.15 = bf16[128,2048]{1,0:T(8,128)(2,1)S(1)} collective-permute-done((bf16[128,2048]{1,0:T(8,128)(2,1)S(1)}, bf16[128,2048]{1,0:T(8,128)(2,1)S(1)}, u32[]{:S(2)}, u32[]{:S(2)}) %collective-permute-start.15) | collective-permute-done | bytes 524320 | tf_op jit(solution)/shard_map/ppermute | solution.py:46
  353.3 22.1 %convolution_convert_fusion.2 = bf16[2048,2048]{1,0:T(8,128)(2,1)} fusion(bf16[1024,2048]{1,0:T(8,128)(2,1)S(1)} %constant_dynamic-update-slice_fusion.5, bf16[1024,2048]{1,0:T(8,128)(2,1)S(1)} %copy-done.43), kind=kOutput, calls=%fused_computation.15 | convolution fusion | flops 8594128896 | bytes 16777216 | tf_op jit(solution)/shard_map/dot_general | solution.py:41
  375.5 20.7 %convert_reduce_fusion = (f32[2048]{0:T(1024)S(1)}, bf16[1024,2048]{1,0:T(8,128)(2,1)S(1)}) fusion(f32[1024,2048]{1,0:T(8,128)} %get-tuple-element.132, f32[2048]{0:T(1024)S(1)} %copy-done.38, bf16[1024,2048]{1,0:T(8,128)(2,1)} %copy-done.26, bf16[2048,2048]{0,1:T(8,128)(2,1)} %all-gather.8.cloned.1.call-done), kind=kOutput, calls=%fused_computation.11 | convolution fusion | flops 8646555648 | bytes 25182208 | tf_op jit(solution)/shard_map/dot_general | solution.py:33
  398.2 13.5 %convolution_convert_fusion.1 = bf16[2048,2048]{1,0:T(8,128)(2,1)} fusion(bf16[1024,2048]{1,0:T(8,128)(2,1)} %constant_dynamic-update-slice_fusion, bf16[1024,2048]{1,0:T(8,128)(2,1)S(1)} %get-tuple-element.78), kind=kOutput, calls=%fused_computation.14 | convolution fusion | flops 8594128896 | bytes 16777216 | tf_op jit(solution)/shard_map/dot_general | solution.py:41
  431.4 9.7 %collective-permute-done.23 = bf16[128,2048]{1,0:T(8,128)(2,1)S(1)} collective-permute-done((bf16[128,2048]{1,0:T(8,128)(2,1)S(1)}, bf16[128,2048]{1,0:T(8,128)(2,1)S(1)}, u32[]{:S(2)}, u32[]{:S(2)}) %collective-permute-start.23) | collective-permute-done | bytes 524320 | tf_op jit(solution)/shard_map/ppermute | solution.py:46
  444.7 13.5 %collective-permute-done.22 = bf16[256,2048]{1,0:T(8,128)(2,1)S(1)} collective-permute-done((bf16[256,2048]{1,0:T(8,128)(2,1)S(1)}, bf16[256,2048]{1,0:T(8,128)(2,1)S(1)}, u32[]{:S(2)}, u32[]{:S(2)}) %collective-permute-start.22) | collective-permute-done | bytes 1048608 | tf_op jit(solution)/shard_map/ppermute | solution.py:46
  463.6 17.4 %collective-permute-done.26 = bf16[256,2048]{1,0:T(8,128)(2,1)S(1)} collective-permute-done((bf16[256,2048]{1,0:T(8,128)(2,1)S(1)}, bf16[256,2048]{1,0:T(8,128)(2,1)S(1)}, u32[]{:S(2)}, u32[]{:S(2)}) %collective-permute-start.26) | collective-permute-done | bytes 1048608 | tf_op jit(solution)/shard_map/ppermute | solution.py:46
  500.4 30.0 %attention_backward.1 = (bf16[1024,512]{1,0:T(8,128)(2,1)S(1)}, f32[1024,512]{1,0:T(8,128)}, f32[1024,512]{1,0:T(8,128)}, bf16[1024,512]{1,0:T(8,128)(2,1)S(1)}, bf16[1024,512]{1,0:T(8,128)(2,1)S(1)}) custom-call(bf16[1024,1536]{1,0:T(8,128)(2,1)} %copy-done.15, bf16[1024,512]{1,0:T(8,128)(2,1)S(1)} %convolution_convert_fusion.7.do_ref, ...), custom_call_target="tpu_custom_call" | custom-call | flops 10737418240 | bytes 12582912 | tf_op jit(solution)/shard_map/attention_backward/pallas_call | solution.py:170
  541.0 8.9 %convolution_convert_fusion = bf16[2048,1536]{0,1:T(8,128)(2,1)} fusion(bf16[1024,1536]{1,0:T(8,128)(2,1)S(1)} %get-tuple-element.80, bf16[256,2048]{1,0:T(8,128)(2,1)S(1)} %copy-done.22, bf16[256,2048]{1,0:T(8,128)(2,1)S(1)} %copy-done.23, bf16[256,2048]{1,0:T(8,128)(2,1)S(1)} %copy-done.20, bf16[256,2048]{1,0:T(8,128)(2,1)S(1)} %copy-done.18), kind=kOutput, calls=%fused_computation.13 | convolution fusion | flops 6462373888 | bytes 13631488 | tf_op jit(solution)/shard_map/dot_general | solution.py:41
  549.9 7.7 %pad_maximum_fusion = bf16[2048,2048]{0,1:T(8,128)(2,1)} fusion(bf16[2048,512]{0,1:T(8,128)(2,1)S(1)} %convolution_convert_fusion.3, bf16[2048,1536]{0,1:T(8,128)(2,1)} %convolution_convert_fusion), kind=kLoop, calls=%fused_computation.10 | loop fusion | flops 16777216 | bytes 16777216 | tf_op jit(solution)/shard_map/concatenate | solution.py:288
  570.6 12.3 %collective-permute-done.18 = bf16[256,2048]{1,0:T(8,128)(2,1)S(1)} collective-permute-done((bf16[256,2048]{1,0:T(8,128)(2,1)S(1)}, bf16[256,2048]{1,0:T(8,128)(2,1)S(1)}, u32[]{:S(2)}, u32[]{:S(2)}) %collective-permute-start.18) | collective-permute-done | bytes 1048608 | tf_op jit(solution)/shard_map/ppermute | solution.py:46
  590.5 8.0 %collective-permute-done.42 = f32[6,2048]{1,0:T(8,128)S(1)} collective-permute-done((f32[6,2048]{1,0:T(8,128)S(1)}, f32[6,2048]{1,0:T(8,128)S(1)}, u32[]{:S(2)}, u32[]{:S(2)}) %collective-permute-start.42) | collective-permute-done | bytes 49184 | tf_op jit(solution)/shard_map/ppermute | solution.py:46
  633.6 11.7 %collective-permute-done.32 = bf16[256,2048]{1,0:T(8,128)(2,1)S(1)} collective-permute-done((bf16[256,2048]{1,0:T(8,128)(2,1)S(1)}, bf16[256,2048]{1,0:T(8,128)(2,1)S(1)}, u32[]{:S(2)}, u32[]{:S(2)}) %collective-permute-start.32) | collective-permute-done | bytes 1048608 | tf_op jit(solution)/shard_map/ppermute | solution.py:46
  671.1 8.1 %collective-permute-done.35 = bf16[256,2048]{1,0:T(8,128)(2,1)S(1)} collective-permute-done((bf16[256,2048]{1,0:T(8,128)(2,1)S(1)}, bf16[256,2048]{1,0:T(8,128)(2,1)S(1)}, u32[]{:S(2)}, u32[]{:S(2)}) %collective-permute-start.35) | collective-permute-done | bytes 1048608 | tf_op jit(solution)/shard_map/ppermute | solution.py:46
  (348 shorter events, 268.4 us)
Async XLA Ops:
  7.2 91.2 %all-gather.4.cloned.1.call-start = ((), (), s32[]{:S(2)}) async-start(), calls=%async_computation.3 | async-start | bytes 9437184 | tf_op jit(solution)/shard_map/all_gather | solution.py:246
  13.1 212.2 %all-gather.6.cloned.1.call-start = ((), (), s32[]{:S(2)}) async-start(), calls=%async_computation.4 | async-start | bytes 9437184 | tf_op jit(solution)/shard_map/all_gather | solution.py:248
  14.3 249.3 %all-gather.8.cloned.1.call-start = ((), (), s32[]{:S(2)}) async-start(), calls=%async_computation.5 | async-start | bytes 9437184 | tf_op jit(solution)/shard_map/all_gather | solution.py:249
  17.0 676.0 %reduce-scatter.8.cloned.1.call-start = ((), (), s32[]{:S(2)}) async-start(), calls=%async_computation.8 | async-start | bytes 9437184 | tf_op jit(solution)/shard_map/reduce_scatter | solution.py:290
  156.3 25.9 %collective-permute-start.2 = (bf16[256,2048]{1,0:T(8,128)(2,1)S(1)}, bf16[256,2048]{1,0:T(8,128)(2,1)S(1)}, u32[]{:S(2)}, u32[]{:S(2)}) collective-permute-start(bf16[256,2048]{1,0:T(8,128)(2,1)S(1)} %pad_maximum_fusion.4), channel_id=1, source_target_pairs={{0,1},{1,0},{2,3},{3,2},{4,5},{5,4},{6,7},{7,6},{8,9},{9,8},{10,11... | collective-permute-start | bytes 3145736 | tf_op jit(solution)/shard_map/ppermute | solution.py:46
  160.9 23.5 %collective-permute-start.4 = (bf16[256,2048]{1,0:T(8,128)(2,1)S(1)}, bf16[256,2048]{1,0:T(8,128)(2,1)S(1)}, u32[]{:S(2)}, u32[]{:S(2)}) collective-permute-start(bf16[256,2048]{1,0:T(8,128)(2,1)S(1)} %pad_maximum_fusion.5), channel_id=1, source_target_pairs={{0,2},{1,3},{2,0},{3,1},{4,6},{5,7},{6,4},{7,5},{8,10},{9,11},{10,... | collective-permute-start | bytes 3145736 | tf_op jit(solution)/shard_map/ppermute | solution.py:46
  189.0 22.5 %collective-permute-start.6 = (bf16[256,2048]{1,0:T(8,128)(2,1)S(1)}, bf16[256,2048]{1,0:T(8,128)(2,1)S(1)}, u32[]{:S(2)}, u32[]{:S(2)}) collective-permute-start(bf16[256,2048]{1,0:T(8,128)(2,1)S(1)} %get-tuple-element.94), channel_id=1, source_target_pairs={{0,2},{1,3},{2,0},{3,1},{4,6},{5,7},{6,4},{7,5},{8,10},{9,11},{10,... | collective-permute-start | bytes 3145736 | tf_op jit(solution)/shard_map/ppermute | solution.py:46
  189.5 24.2 %collective-permute-start.5 = (bf16[256,2048]{1,0:T(8,128)(2,1)S(1)}, bf16[256,2048]{1,0:T(8,128)(2,1)S(1)}, u32[]{:S(2)}, u32[]{:S(2)}) collective-permute-start(bf16[256,2048]{1,0:T(8,128)(2,1)S(1)} %get-tuple-element.94), channel_id=1, source_target_pairs={{0,1},{1,0},{2,3},{3,2},{4,5},{5,4},{6,7},{7,6},{8,9},{9,8},{10,11... | collective-permute-start | bytes 3145736 | tf_op jit(solution)/shard_map/ppermute | solution.py:46
  284.2 25.9 %collective-permute-start.10 = (bf16[256,2048]{1,0:T(8,128)(2,1)S(1)}, bf16[256,2048]{1,0:T(8,128)(2,1)S(1)}, u32[]{:S(2)}, u32[]{:S(2)}) collective-permute-start(bf16[256,2048]{1,0:T(8,128)(2,1)S(1)} %pad_maximum_fusion.6), channel_id=1, source_target_pairs={{0,1},{1,0},{2,3},{3,2},{4,5},{5,4},{6,7},{7,6},{8,9},{9,8},{10,11... | collective-permute-start | bytes 3145736 | tf_op jit(solution)/shard_map/ppermute | solution.py:46
  288.9 23.3 %collective-permute-start.12 = (bf16[256,2048]{1,0:T(8,128)(2,1)S(1)}, bf16[256,2048]{1,0:T(8,128)(2,1)S(1)}, u32[]{:S(2)}, u32[]{:S(2)}) collective-permute-start(bf16[256,2048]{1,0:T(8,128)(2,1)S(1)} %pad_maximum_fusion.7), channel_id=1, source_target_pairs={{0,2},{1,3},{2,0},{3,1},{4,6},{5,7},{6,4},{7,5},{8,10},{9,11},{10,... | collective-permute-start | bytes 3145736 | tf_op jit(solution)/shard_map/ppermute | solution.py:46
  315.7 22.8 %collective-permute-start.14 = (bf16[256,2048]{1,0:T(8,128)(2,1)S(1)}, bf16[256,2048]{1,0:T(8,128)(2,1)S(1)}, u32[]{:S(2)}, u32[]{:S(2)}) collective-permute-start(bf16[256,2048]{1,0:T(8,128)(2,1)S(1)} %get-tuple-element.88), channel_id=1, source_target_pairs={{0,2},{1,3},{2,0},{3,1},{4,6},{5,7},{6,4},{7,5},{8,10},{9,11},{10,... | collective-permute-start | bytes 3145736 | tf_op jit(solution)/shard_map/ppermute | solution.py:46
  317.2 24.6 %collective-permute-start.13 = (bf16[256,2048]{1,0:T(8,128)(2,1)S(1)}, bf16[256,2048]{1,0:T(8,128)(2,1)S(1)}, u32[]{:S(2)}, u32[]{:S(2)}) collective-permute-start(bf16[256,2048]{1,0:T(8,128)(2,1)S(1)} %get-tuple-element.88), channel_id=1, source_target_pairs={{0,1},{1,0},{2,3},{3,2},{4,5},{5,4},{6,7},{7,6},{8,9},{9,8},{10,11... | collective-permute-start | bytes 3145736 | tf_op jit(solution)/shard_map/ppermute | solution.py:46
  375.4 320.9 %reduce-scatter.6.cloned.1.call-start = ((), (), s32[]{:S(2)}) async-start(), calls=%async_computation.7 | async-start | bytes 9437184 | tf_op jit(solution)/shard_map/reduce_scatter | solution.py:290
  411.7 287.4 %reduce-scatter.4.cloned.1.call-start = ((), (), s32[]{:S(2)}) async-start(), calls=%async_computation.6 | async-start | bytes 9437184 | tf_op jit(solution)/shard_map/reduce_scatter | solution.py:290
  429.9 28.4 %collective-permute-start.22 = (bf16[256,2048]{1,0:T(8,128)(2,1)S(1)}, bf16[256,2048]{1,0:T(8,128)(2,1)S(1)}, u32[]{:S(2)}, u32[]{:S(2)}) collective-permute-start(bf16[256,2048]{1,0:T(8,128)(2,1)S(1)} %pad_maximum_fusion.8), channel_id=1, source_target_pairs={{0,1},{1,0},{2,3},{3,2},{4,5},{5,4},{6,7},{7,6},{8,9},{9,8},{10,11... | collective-permute-start | bytes 3145736 | tf_op jit(solution)/shard_map/ppermute | solution.py:46
  462.1 23.1 %collective-permute-start.25 = (bf16[256,2048]{1,0:T(8,128)(2,1)S(1)}, bf16[256,2048]{1,0:T(8,128)(2,1)S(1)}, u32[]{:S(2)}, u32[]{:S(2)}) collective-permute-start(bf16[256,2048]{1,0:T(8,128)(2,1)S(1)} %get-tuple-element.84), channel_id=1, source_target_pairs={{0,1},{1,0},{2,3},{3,2},{4,5},{5,4},{6,7},{7,6},{8,9},{9,8},{10,11... | collective-permute-start | bytes 3145736 | tf_op jit(solution)/shard_map/ppermute | solution.py:46
  557.7 25.2 %collective-permute-start.18 = (bf16[256,2048]{1,0:T(8,128)(2,1)S(1)}, bf16[256,2048]{1,0:T(8,128)(2,1)S(1)}, u32[]{:S(2)}, u32[]{:S(2)}) collective-permute-start(bf16[256,2048]{1,0:T(8,128)(2,1)S(1)} %get-tuple-element.28), channel_id=1, source_target_pairs={{0,2},{1,3},{2,0},{3,1},{4,6},{5,7},{6,4},{7,5},{8,10},{9,11},{10,... | collective-permute-start | bytes 3145736 | tf_op jit(solution)/shard_map/ppermute | solution.py:46
  559.2 26.3 %collective-permute-start.17 = (bf16[256,2048]{1,0:T(8,128)(2,1)S(1)}, bf16[256,2048]{1,0:T(8,128)(2,1)S(1)}, u32[]{:S(2)}, u32[]{:S(2)}) collective-permute-start(bf16[256,2048]{1,0:T(8,128)(2,1)S(1)} %get-tuple-element.28), channel_id=1, source_target_pairs={{0,1},{1,0},{2,3},{3,2},{4,5},{5,4},{6,7},{7,6},{8,9},{9,8},{10,11... | collective-permute-start | bytes 3145736 | tf_op jit(solution)/shard_map/ppermute | solution.py:46
  583.8 43.5 %collective-permute-start.19 = (bf16[128,2048]{1,0:T(8,128)(2,1)}, bf16[128,2048]{1,0:T(8,128)(2,1)}, u32[]{:S(2)}, u32[]{:S(2)}) collective-permute-start(bf16[128,2048]{1,0:T(8,128)(2,1)} %slice.255), channel_id=1, source_target_pairs={{0,1},{1,0},{2,3},{3,2},{4,5},{5,4},{6,7},{7,6},{8,9},{9,8},{10,11... | collective-permute-start | bytes 1572872 | tf_op jit(solution)/shard_map/ppermute | solution.py:46
  586.3 42.9 %collective-permute-start.20 = (bf16[128,2048]{1,0:T(8,128)(2,1)}, bf16[128,2048]{1,0:T(8,128)(2,1)}, u32[]{:S(2)}, u32[]{:S(2)}) collective-permute-start(bf16[128,2048]{1,0:T(8,128)(2,1)} %slice.256), channel_id=1, source_target_pairs={{0,2},{1,3},{2,0},{3,1},{4,6},{5,7},{6,4},{7,5},{8,10},{9,11},{10,... | collective-permute-start | bytes 1572872 | tf_op jit(solution)/shard_map/ppermute | solution.py:46
  598.5 30.6 %collective-permute-start.43 = (f32[6,2048]{1,0:T(8,128)S(1)}, f32[6,2048]{1,0:T(8,128)S(1)}, u32[]{:S(2)}, u32[]{:S(2)}) collective-permute-start(f32[6,2048]{1,0:T(8,128)S(1)} %add.385), channel_id=1, source_target_pairs={{0,2},{1,3},{2,0},{3,1},{4,6},{5,7},{6,4},{7,5},{8,10},{9,11},{10,... | collective-permute-start | bytes 147464 | tf_op jit(solution)/shard_map/ppermute | solution.py:46
  617.5 27.7 %collective-permute-start.32 = (bf16[256,2048]{1,0:T(8,128)(2,1)S(1)}, bf16[256,2048]{1,0:T(8,128)(2,1)S(1)}, u32[]{:S(2)}, u32[]{:S(2)}) collective-permute-start(bf16[256,2048]{1,0:T(8,128)(2,1)S(1)} %pad_maximum_fusion.10), channel_id=1, source_target_pairs={{0,1},{1,0},{2,3},{3,2},{4,5},{5,4},{6,7},{7,6},{8,9},{9,8},{10,11... | collective-permute-start | bytes 3145736 | tf_op jit(solution)/shard_map/ppermute | solution.py:46
  646.0 22.1 %collective-permute-start.36 = (bf16[256,2048]{1,0:T(8,128)(2,1)S(1)}, bf16[256,2048]{1,0:T(8,128)(2,1)S(1)}, u32[]{:S(2)}, u32[]{:S(2)}) collective-permute-start(bf16[256,2048]{1,0:T(8,128)(2,1)S(1)} %get-tuple-element.82), channel_id=1, source_target_pairs={{0,2},{1,3},{2,0},{3,1},{4,6},{5,7},{6,4},{7,5},{8,10},{9,11},{10,... | collective-permute-start | bytes 3145736 | tf_op jit(solution)/shard_map/ppermute | solution.py:46
  653.1 26.1 %collective-permute-start.35 = (bf16[256,2048]{1,0:T(8,128)(2,1)S(1)}, bf16[256,2048]{1,0:T(8,128)(2,1)S(1)}, u32[]{:S(2)}, u32[]{:S(2)}) collective-permute-start(bf16[256,2048]{1,0:T(8,128)(2,1)S(1)} %get-tuple-element.82), channel_id=1, source_target_pairs={{0,1},{1,0},{2,3},{3,2},{4,5},{5,4},{6,7},{7,6},{8,9},{9,8},{10,11... | collective-permute-start | bytes 3145736 | tf_op jit(solution)/shard_map/ppermute | solution.py:46
  (80 other events, 1167.1 us)
Sparse Core Ops, SparseCore 0:
  13.2 85.1 all-gather.3
  100.6 80.2 all-gather.5
  182.5 81.0 all-gather.7
  375.5 86.8 reduce-scatter.7
  464.6 87.9 reduce-scatter.5
  557.8 89.7 reduce-scatter.3

commit v3 on v2

--- a/solution.py
+++ b/solution.py
@@ -17,12 +17,6 @@
 LOW = jnp.bfloat16
 BOTH_LAST = (((1,), (1,)), ((), ()))
 BOTH_FIRST = (((0,), (0,)), ((), ()))
-
-
-def layer_norm(resid, gain, shift):
-    center = resid - jnp.mean(resid, axis=-1, keepdims=True)
-    spread = jnp.mean(center * center, axis=-1, keepdims=True)
-    return center * lax.rsqrt(spread + norm_eps) * gain + shift
 
 
 def gelu_tanh(inner):
@@ -59,47 +53,157 @@
     return value
 
 
-def gather_rows(block):
+def gated(value, gate):
+    return value if gate is None else after(value, gate)
+
+
+def gather_near(block):
+    return swap(block, "tensor", 1), swap(block, "tensor", 2)
+
+
+def gather_rest(block, near):
+    one, two = near
     half = block.shape[0] // 2
-    one, two = swap(block, "tensor", 1), swap(block, "tensor", 2)
-    three_top = swap(two[:half], "tensor", 1)
-    three_low = swap(one[half:], "tensor", 2)
-    rows = [block, one, two, three_top, three_low]
+    rest = [swap(two[:half], "tensor", 1), swap(one[half:], "tensor", 2)]
     count, flip = lax.axis_size("tensor"), 4
     while flip < count:
-        rows.append(swap(jnp.concatenate(rows), "tensor", flip))
+        rest.append(swap(jnp.concatenate([block, one, two, *rest]), "tensor", flip))
         flip *= 2
-    return jnp.concatenate(rows)
-
-
-def scatter_rows(part, rows):
+    return rest
+
+
+def gather_rows(block):
+    near = gather_near(block)
+    return jnp.concatenate([block, *near, *gather_rest(block, near)])
+
+
+def scatter_rows(part, after_first=(), after_second=()):
     count = lax.axis_size("tensor")
-    block = rows // count
-    half = block // 2
     flip = count // 2
     extra = None
     while flip >= 4:
-        away = part(flip * block, 2 * flip * block)
+        away = jnp.concatenate([part(k, None) for k in range(flip, 2 * flip)])
+        split = away.shape[0]
         if extra is not None:
-            away = away + extra[flip * block :].astype(F32)
+            away = away + extra[split:].astype(F32)
         come = swap(away.astype(LOW), "tensor", flip)
-        extra = come if extra is None else extra[: flip * block].astype(F32) + come.astype(F32)
+        extra = come if extra is None else extra[:split].astype(F32) + come.astype(F32)
         flip //= 2
 
-    def piece(k):
-        value = part(k * block, (k + 1) * block)
+    def piece(k, gate=None):
+        value = part(k, gate)
         if extra is not None:
+            block = value.shape[0]
             value = value + extra[k * block : (k + 1) * block].astype(F32)
         return value
 
     three = piece(3).astype(LOW)
-    come_top = swap(three[:half], "tensor", 1)
-    come_low = swap(three[half:], "tensor", 2)
-    one, two = piece(1), piece(2)
+    half = three.shape[0] // 2
+    come_top, come_low = swap(three[:half], "tensor", 1), swap(three[half:], "tensor", 2)
+    one, two = piece(1, three), piece(2, three)
+    first = [make(three) for make in after_first]
+    come_top, come_low = after((come_top, come_low), *first)
     one = jnp.concatenate([one[:half].astype(LOW), (one[half:] + come_low.astype(F32)).astype(LOW)])
     two = jnp.concatenate([(two[:half] + come_top.astype(F32)).astype(LOW), two[half:].astype(LOW)])
-    come_one, come_two = swap(one, "tensor", 1), swap(two, "tensor", 2)
-    return piece(0) + come_one.astype(F32) + come_two.astype(F32)
+    from_one, from_two = swap(one, "tensor", 1), swap(two, "tensor", 2)
+    here = piece(0, (one, two))
+    second = [make((one, two)) for make in after_second]
+    from_one, from_two = after((from_one, from_two), here, *second)
+    return (here, from_one, from_two), first, second
+
+
+def normed(resid):
+    center = resid - jnp.mean(resid, axis=-1, keepdims=True)
+    spread = jnp.mean(center * center, axis=-1, keepdims=True)
+    scale = lax.rsqrt(spread + norm_eps)
+    return center * scale, scale
+
+
+def norm_grad(unit, scale, grad, gain):
+    inner = grad * gain
+    back = scale * (
+        inner
+        - jnp.mean(inner, axis=-1, keepdims=True)
+        - unit * jnp.mean(inner * unit, axis=-1, keepdims=True)
+    )
+    return back, grad * unit
+
+
+def add_sums(sum_ref, *terms):
+    @pl.when(pl.program_id(0) == 0)
+    def _():
+        sum_ref[...] = jnp.zeros_like(sum_ref)
+
+    for row, term in enumerate(terms):
+        sum_ref[row : row + 1, :] += jnp.sum(term, axis=0, keepdims=True)
+
+
+def received(here_ref, one_ref, two_ref):
+    return here_ref[...] + one_ref[...].astype(F32) + two_ref[...].astype(F32)
+
+
+def norm_one_kernel(
+    in_ref, h, one, two, b_ref, gain_ref, shift_ref, resid_ref, hidden_ref, low_ref
+):
+    resid = in_ref[...].astype(F32) + (received(h, one, two) + b_ref[...])
+    unit, _ = normed(resid)
+    hidden = unit * gain_ref[...] + shift_ref[...]
+    resid_ref[...] = resid
+    hidden_ref[...] = hidden
+    low_ref[...] = hidden.astype(LOW)
+
+
+def norm_two_kernel(
+    hidden_ref, h, one, two, b_ref, gain_ref, shift_ref, cot_ref, live_ref,
+    grad_ref, low_ref, out_ref, sum_ref,
+):
+    unit, scale = normed(hidden_ref[...] + (received(h, one, two) + b_ref[...]))
+    gain = gain_ref[...]
+    out_ref[...] = (unit * gain + shift_ref[...]).astype(LOW)
+    grad = cot_ref[...].astype(F32) * live_ref[:, 0:1]
+    back, to_gain = norm_grad(unit, scale, grad, gain)
+    grad_ref[...] = back
+    low_ref[...] = back.astype(LOW)
+    add_sums(sum_ref, back, to_gain, grad)
+
+
+def norm_one_back_kernel(
+    resid_ref, grad_ref, h, one, two, gain_ref, back_ref, low_ref, sum_ref
+):
+    grad = grad_ref[...] + received(h, one, two)
+    unit, scale = normed(resid_ref[...])
+    back, to_gain = norm_grad(unit, scale, grad, gain_ref[...])
+    back_ref[...] = back
+    low_ref[...] = back.astype(LOW)
+    add_sums(sum_ref, back, to_gain, grad)
+
+
+def on_rows(kernel, name, args, outs, sums, tile=64):
+    rows, model = args[0].shape
+    tile = min(tile, rows)
+
+    def spec(shape):
+        if shape[0] == 1:
+            return pl.BlockSpec(shape, lambda i: (0, 0))
+        return pl.BlockSpec((tile, shape[1]), lambda i: (i, 0))
+
+    out_shape = [jax.ShapeDtypeStruct((rows, model), dtype) for dtype in outs]
+    out_specs = [spec(out.shape) for out in out_shape]
+    if sums:
+        out_shape.append(jax.ShapeDtypeStruct((8, model), F32))
+        out_specs.append(pl.BlockSpec((8, model), lambda i: (0, 0)))
+    return pl.pallas_call(
+        kernel,
+        grid=(rows // tile,),
+        in_specs=[spec(arg.shape) for arg in args],
+        out_specs=out_specs,
+        out_shape=out_shape,
+        compiler_params=pltpu.CompilerParams(vmem_limit_bytes=32 << 20),
+        cost_estimate=pl.CostEstimate(
+            flops=20 * rows * model, transcendentals=rows, bytes_accessed=20 * rows * model
+        ),
+        name=name,
+    )(*args)
 
 
 def fwd_kernel(q_ref,ko_ref,kf_ref,vo_ref,vf_ref,bo_ref,bf_ref,o_ref,l_ref,*,scale):
@@ -129,10 +233,10 @@
         out_specs=[pl.BlockSpec((bq,HEAD_DIM),lambda h,i:(i,h)),pl.BlockSpec((1,1,bq),lambda h,i:(h,0,i))],
         out_shape=[jax.ShapeDtypeStruct((rows,heads*HEAD_DIM),LOW),jax.ShapeDtypeStruct((heads,1,rows),F32)],
         compiler_params=pltpu.CompilerParams(vmem_limit_bytes=48<<20),
-        cost_estimate=pl.CostEstimate(flops=4*rows*2*rows*HEAD_DIM*heads,transcendentals=heads*rows*2*rows,bytes_accessed=heads*HEAD_DIM*rows*2*6),
+        cost_estimate=pl.CostEstimate(flops=12*rows*2*rows*HEAD_DIM*heads,transcendentals=heads*rows*2*rows,bytes_accessed=heads*HEAD_DIM*rows*2*6),
         name='attention_forward')(qkv,qkv,kv_far,qkv,kv_far,bias_own,bias_far)
 
-def bwd_kernel(q_ref,do_ref,o_ref,l_ref,ko_ref,kf_ref,vo_ref,vf_ref,bo_ref,bf_ref,dq_ref,dko_ref,dvo_ref,dkf_ref,dvf_ref,
+def bwd_kernel(q_ref,do_ref,o_ref,l_ref,ko_ref,kf_ref,vo_ref,vf_ref,bo_ref,bf_ref,dq_ref,dko_ref,dvo_ref,dkf_ref,
                ako,avo,akf,avf,kto,ktf,*,scale,chunk):
     i=pl.program_id(1); last=pl.num_programs(1)-1
     @pl.when(i==0)
@@ -161,7 +265,7 @@
     @pl.when(i==last)
     def _():
         dko_ref[...]=ako[...]*s; dvo_ref[...]=avo[...]
-        dkf_ref[...]=(akf[...]*s).astype(LOW); dvf_ref[...]=avf[...].astype(LOW)
+        dkf_ref[0]=(akf[...]*s).astype(LOW); dkf_ref[1]=avf[...].astype(LOW)
 def attn_bwd(qkv,kv_far,do,o,lse,bias_own,bias_far,heads,bq=256,chunk=512):
     rows=qkv.shape[0]
     scale=LOG2E*HEAD_DIM**-0.5
@@ -173,11 +277,11 @@
         in_specs=[qb,qb,qb,pl.BlockSpec((1,1,bq),lambda h,i:(h,0,i)),
           full(heads),full(0),full(2*heads),full(heads),
           pl.BlockSpec((rows,HEAD_DIM),lambda h,i:(0,0)),pl.BlockSpec((rows,HEAD_DIM),lambda h,i:(0,0))],
-        out_specs=[qb,full(0),full(0),full(0),full(0)],
-        out_shape=[jax.ShapeDtypeStruct((rows,heads*HEAD_DIM),LOW)]+[jax.ShapeDtypeStruct((rows,heads*HEAD_DIM),F32)]*2+[jax.ShapeDtypeStruct((rows,heads*HEAD_DIM),LOW)]*2,
+        out_specs=[qb,full(0),full(0),pl.BlockSpec((2,rows,HEAD_DIM),lambda h,i:(0,0,h))],
+        out_shape=[jax.ShapeDtypeStruct((rows,heads*HEAD_DIM),LOW)]+[jax.ShapeDtypeStruct((rows,heads*HEAD_DIM),F32)]*2+[jax.ShapeDtypeStruct((2,rows,heads*HEAD_DIM),LOW)],
         scratch_shapes=[pltpu.VMEM((rows,HEAD_DIM),F32)]*4+[pltpu.VMEM((HEAD_DIM,rows),LOW)]*2,
         compiler_params=pltpu.CompilerParams(vmem_limit_bytes=48<<20),
-        cost_estimate=pl.CostEstimate(flops=10*rows*2*rows*HEAD_DIM*heads,transcendentals=heads*rows*2*rows,bytes_accessed=heads*HEAD_DIM*rows*2*12),
+        cost_estimate=pl.CostEstimate(flops=20*rows*2*rows*HEAD_DIM*heads,transcendentals=heads*rows*2*rows,bytes_accessed=heads*HEAD_DIM*rows*2*12),
         name='attention_backward')(qkv,do,o,lse,qkv,kv_far,qkv,kv_far,bias_own,bias_far)
 
 
@@ -237,72 +341,183 @@
 
     row_live = (my_spot * tok_rows + place[:block] < my_length).astype(F32)
     rows_in = reorder(tokens)
-    in_here = my_block(tokens).astype(F32)
-    grad_out = my_block(cotangent).astype(F32) * row_live[:, None]
+    in_here = my_block(tokens)
+    grad_out = my_block(cotangent)
+    live_wide = jnp.broadcast_to(row_live[:, None], (block, HEAD_DIM))
+
+    dp_count = lax.axis_size("dp")
+    column = model // dp_count
+
+    def columns_of(value, core):
+        return jnp.concatenate(
+            [
+                jnp.where(
+                    core == 0,
+                    value[:, first : first + column],
+                    value[:, first + column : first + 2 * column],
+                )
+                for first in range(0, model, 2 * column)
+            ],
+            axis=1,
+        )
+
+    def shared_columns(value):
+        return columns_of(value, my_spot), swap(columns_of(value, 1 - my_spot), "dp", 1)
+
+    def weight_grad(pairs):
+        total = None
+        for left, right in pairs:
+            term = mat_first(left, right)
+            total = term if total is None else total + term
+        return total
+
+    core_groups = [[core + 2 * step for step in range(dp_count // 2)] for core in range(2)]
+
+    def to_owner(grad):
+        return lax.psum_scatter(
+            grad, "dp", scatter_dimension=0, tiled=True, axis_index_groups=core_groups
+        )
+
+    def split_rows(value):
+        return [value[k * block : (k + 1) * block] for k in range(value.shape[0] // block)]
 
     low_attn = jnp.concatenate([w_query, w_key, w_value, w_out.T], axis=1).astype(LOW)
-    low_inner = w_inner.astype(LOW)
-    low_outer = w_outer.T.astype(LOW)
+    low_inner = w_inner.T.astype(LOW)
+    low_outer = w_outer.astype(LOW)
     full_attn = lax.all_gather(low_attn, "dp", axis=0, tiled=True)
-    full_qkv, full_out = full_attn[:, : 3 * width_here], full_attn[:, 3 * width_here :]
-    full_inner = lax.all_gather(low_inner, "dp", axis=0, tiled=True)
-    full_outer = lax.all_gather(low_outer, "dp", axis=0, tiled=True)
-
+    full_qkv, full_out = full_attn[:, : 3 * width_here], full_attn[:, 3 * width_here :].T
+    full_inner = lax.all_gather(low_inner, "dp", axis=1, tiled=True)
+    full_outer = lax.all_gather(low_outer, "dp", axis=1, tiled=True)
+
+    rows_pair = shared_columns(rows_in)
     b_qkv = jnp.concatenate([b_query, jnp.zeros_like(b_query), b_value])
-    qkv = (mat_bf(rows_in, full_qkv) + b_qkv).astype(LOW)
+    qkv = (mat_bf(after(rows_in, rows_pair), full_qkv) + b_qkv).astype(LOW)
     far_kv = swap(qkv[:, width_here:], "dp", 1)
     mixed, lse = attn_fwd(qkv, far_kv, own_bias[None], far_bias[None], heads_here)
 
-    attn = scatter_rows(lambda a, b: mat_last(mixed[a:b], full_out), tok_rows)
-    hidden, norm_one_back = jax.vjp(layer_norm, in_here + (attn + b_out), ln1_gain, ln1_bias)
-    hidden_low = gather_rows(hidden.astype(LOW))
-    inner = mat_bf(hidden_low, full_inner) + b_inner
-    act_low = gelu_tanh(inner).astype(LOW)
-    outer = scatter_rows(lambda a, b: mat_last(act_low[a:b], full_outer), tok_rows)
-    output, norm_two_back = jax.vjp(layer_norm, hidden + (outer + b_outer), ln2_gain, ln2_bias)
-    grad_two, grad_ln2_gain, grad_ln2_bias = norm_two_back(grad_out)
-    grad_b_outer = jnp.sum(grad_two, axis=0)
-    outer_low = gather_rows(grad_two.astype(LOW))
-    output = reorder(gather_rows(after(output.astype(LOW), outer_low))).astype(F32)
-
-    grad_w_outer = mat_first(outer_low, act_low).astype(LOW)
-    grad_act = mat_bf(after(outer_low, grad_w_outer), full_outer)
-    gelu_value, gelu_back = jax.vjp(gelu_tanh, inner)
-    inner_low = gelu_back(grad_act)[0].astype(LOW)
-    grad_b_inner = jnp.sum(inner_low.astype(F32), axis=0)
-    grad_hidden = grad_two + scatter_rows(lambda a, b: mat_last(inner_low[a:b], full_inner), tok_rows)
-    grad_w_inner = mat_first(hidden_low, inner_low).astype(LOW)
-    grad_hidden = after(grad_hidden, grad_w_inner)
-    grad_one, grad_ln1_gain, grad_ln1_bias = norm_one_back(grad_hidden)
-    grad_b_out = jnp.sum(grad_one, axis=0)
-    attn_low = gather_rows(grad_one.astype(LOW))
-    mixed_low = mat_bf(attn_low, full_out).astype(LOW)
-    grad_w_out = mat_first(attn_low, mixed).astype(LOW)
-    query_low, own_key, own_value, far_key, far_value = attn_bwd(
-        qkv, far_kv, mixed_low, mixed, lse, own_bias_wide, far_bias_wide, heads_here
-    )
-    key_low = (own_key + swap(far_key, "dp", 1).astype(F32)).astype(LOW)
-    value_low = (own_value + swap(far_value, "dp", 1).astype(F32)).astype(LOW)
+    mixed_blocks = split_rows(mixed)
+    attn_parts, _, _ = scatter_rows(lambda k, gate: mat_bf(gated(mixed_blocks[k], gate), full_out))
+    resid_one, hidden, hidden_here = on_rows(
+        norm_one_kernel,
+        "norm_one",
+        (in_here, *attn_parts, b_out[None], ln1_gain[None], ln1_bias[None]),
+        (F32, F32, LOW),
+        False,
+    )
+    hidden_low = gather_rows(hidden_here)
+    inner = mat_last(hidden_low, full_inner) + b_inner
+    act, act_slope = jax.jvp(gelu_tanh, (inner,), (jnp.ones_like(inner),))
+    act_low, act_slope = act.astype(LOW), act_slope.astype(LOW)
+    mixed_far = swap(after(mixed, hidden_low), "dp", 1)
+    hidden_pair = shared_columns(after(hidden_low, act_low))
+    act_far = swap(act_low, "dp", 1)
+    act_low, act_slope = after((act_low, act_slope), mixed_far, act_far, hidden_pair)
+
+    act_blocks = split_rows(act_low)
+    outer_parts, _, _ = scatter_rows(lambda k, gate: mat_bf(gated(act_blocks[k], gate), full_outer))
+    grad_two, outer_here, output, sums_two = on_rows(
+        norm_two_kernel,
+        "norm_two",
+        (
+            hidden,
+            *outer_parts,
+            b_outer[None],
+            ln2_gain[None],
+            ln2_bias[None],
+            grad_out,
+            live_wide,
+        ),
+        (F32, LOW, LOW),
+        True,
+    )
+    near = 3 * block
+    outer_near = gather_near(outer_here)
+
+    def act_grad(rows, first):
+        slope = act_slope[first * block : first * block + rows.shape[0]]
+        return (mat_last(rows, full_outer) * slope.astype(F32)).astype(LOW)
+
+    inner_here = act_grad(outer_here, 0)
+    outer_near = after(outer_near, inner_here)
+    outer_rest = gather_rest(outer_here, outer_near)
+    near_mine, near_far = shared_columns(jnp.concatenate([outer_here, *outer_near]))
+    grad_near = weight_grad([(near_mine, act_low[:near]), (near_far, act_far[:near])])
+    outer_rest = after(outer_rest, grad_near)
+    outer_rest = jnp.concatenate(outer_rest)
+    rest_mine, rest_far = shared_columns(outer_rest)
+    grad_w_outer = (
+        grad_near + weight_grad([(rest_mine, act_low[near:]), (rest_far, act_far[near:])])
+    ).astype(LOW)
+    owner_outer = to_owner(grad_w_outer)
+    away_rows = jnp.concatenate([*outer_near, after(outer_rest, grad_w_outer)])
+    inner_away = act_grad(away_rows, 1)
+    inner_low = jnp.concatenate([inner_here, inner_away])
+    inner_far = swap(inner_low, "dp", 1)
+    inner_blocks = [inner_here, *split_rows(inner_away)]
+
+
+    def inner_part(k, gate):
+        return mat_bf(gated(inner_blocks[k], gate), full_inner)
+
+    def inner_weight(sent):
+        mine, far = after((inner_low, inner_far), sent)
+        return weight_grad([(hidden_pair[0], mine), (hidden_pair[1], far)]).astype(LOW)
+
+    hidden_parts, _, (grad_w_inner,) = scatter_rows(inner_part, (), [inner_weight])
+    grad_one, attn_here, sums_one = on_rows(
+        norm_one_back_kernel,
+        "norm_one_back",
+        (resid_one, grad_two, *hidden_parts, ln1_gain[None]),
+        (F32, LOW),
+        True,
+    )
+    owner_inner = to_owner(after(grad_w_inner, owner_outer, attn_here))
+    attn_low = gather_rows(attn_here)
+    mixed_low = mat_last(attn_low, full_out).astype(LOW)
+    output = after(output, attn_low)
+    query_low, own_key, own_value, far_pair = attn_bwd(
+        qkv, far_kv, mixed_low, mixed, lse, own_bias_wide, far_bias_wide, heads_here, 512, 256
+    )
+    output_near = after(gather_near(output), query_low)
+    output_rest = gather_rest(output, output_near)
+    attn_pair = shared_columns(after(attn_low, query_low))
+    far_key, far_value = after(swap(far_pair, "dp", 1), attn_pair).astype(F32)
+    key_low = (own_key + far_key).astype(LOW)
+    value_low = (own_value + far_value).astype(LOW)
     qkv_low = jnp.concatenate([query_low, key_low, value_low], axis=1)
-    grad_w_qkv = mat_first(rows_in, qkv_low).astype(LOW)
-    grad_w_attn = jnp.concatenate([grad_w_qkv, grad_w_out], axis=1)
+    qkv_far = swap(qkv_low, "dp", 1)
+    qkv_blocks = split_rows(qkv_low)
+
+    def attn_weight(sent):
+        mine, far = after((qkv_low, qkv_far), sent, owner_inner)
+        grad_w_qkv = weight_grad([(rows_pair[0], mine), (rows_pair[1], far)]).astype(LOW)
+        attn_mine, attn_far = after(attn_pair, grad_w_qkv)
+        grad_w_out = weight_grad([(attn_mine, mixed), (attn_far, mixed_far)]).astype(LOW)
+        return jnp.concatenate([grad_w_qkv, grad_w_out], axis=1)
+
+    (here, one, two), (grad_w_attn, output_rest), _ = scatter_rows(
+        lambda k, gate: mat_last(gated(qkv_blocks[k], gate), full_qkv), after_first=[attn_weight, lambda sent: output_rest]
+    )
+    owner_attn = to_owner(after(grad_w_attn, owner_inner))
+    tokens_here = (grad_one + (here + one.astype(F32) + two.astype(F32))).astype(LOW)
+    grad_tokens = gather_rows(tokens_here)
+    output = jnp.concatenate([output, *output_near, *output_rest])
+    output, grad_tokens = (reorder(rows).astype(F32) for rows in (output, grad_tokens))
+
+    over_rows = jnp.concatenate([sums_one[:3], sums_two[:3]])
+    over_rows = everyone(after(over_rows, tokens_here), ("tensor",)).reshape(-1)
+    inner_sum = jnp.sum(inner_low.astype(F32), axis=0)
+    qkv_sum = jnp.sum(qkv_low.astype(F32), axis=0)
+    sums = everyone(jnp.concatenate([over_rows, inner_sum, qkv_sum]), ("dp",))
+    grad_b_out, grad_ln1_gain, grad_ln1_bias, grad_b_outer, grad_ln2_gain, grad_ln2_bias = sums[
+        : 6 * model
+    ].reshape(6, model)
+    grad_b_inner = sums[6 * model : -3 * width_here]
+    grad_b_qkv = sums[-3 * width_here :]
+
     grad_w_outer, grad_w_inner, grad_w_attn = (
-        lax.psum_scatter(grad, "dp", scatter_dimension=0, tiled=True).astype(F32)
-        for grad in (grad_w_outer, grad_w_inner, grad_w_attn)
-    )
-    grad_b_qkv = jnp.sum(qkv_low.astype(F32), axis=0)
-    input_part = scatter_rows(lambda a, b: mat_last(qkv_low[a:b], full_qkv), tok_rows)
-    grad_tokens = reorder(gather_rows((grad_one + input_part).astype(LOW))).astype(F32)
-
-    over_rows = everyone(
-        jnp.stack(
-            [grad_b_out, grad_b_outer, grad_ln1_gain, grad_ln1_bias, grad_ln2_gain, grad_ln2_bias]
-        ),
-        ("tensor", "dp"),
-    )
-    grad_b_inner = everyone(grad_b_inner, ("dp",))
-    grad_b_qkv = everyone(grad_b_qkv, ("dp",))
-    grad_b_out, grad_b_outer, grad_ln1_gain, grad_ln1_bias, grad_ln2_gain, grad_ln2_bias = over_rows
+        grad.astype(F32) for grad in (owner_outer, owner_inner, owner_attn)
+    )
     grad_w_query, grad_w_key, grad_w_value, grad_w_out = jnp.split(grad_w_attn, 4, axis=1)
     return (
         output,

time: 721 us -> 677 us (0.939)
  waiting for transfers between devices: 345 us -> 302 us
  matrix products: 159 us -> 137 us
  local copies, waits for them, and re-layouts: 43.7 us -> 61.4 us
    ppermute x50 -> x52, waiting for transfers between devices: 246 us -> 218 us  [swap(): lax.ppermute(value, axis, [(source, source ^ flip) for source in range(co...]
    all_gather x2, waiting for transfers between devices: 21.3 us -> 7.27 us  [the longest x1 7.27 us: on_device(): full_outer = lax.all_gather(low_outer, 'dp', axis=1, tiled=True)]
    unnamed x119 -> x189, local copies, waits for them, and re-layouts: 26.9 us -> 38.5 us
    dot_general x4 -> x13, matrix products: 55.1 us -> 43.6 us  [mat_bf(): return jnp.dot(left, right, preferred_element_type=F32)]
    pallas_call x0 -> x3, Pallas kernels: none -> 8.38 us  [on_rows(): pl.pallas_call(kernel, grid=(rows // tile,), in_specs=[spec(arg.shape) fo...]
    select_n x0 -> x5, other arithmetic: none -> 7.55 us  [columns_of(): jnp.where(core == 0, value[:, first:first + column], value[:, first + col...]
    dot_general x16 -> x8, matrix products: 54.3 us -> 47.7 us  [mat_last(): return lax.dot_general(left, right, BOTH_LAST, preferred_element_type=F32)]
    ppermute x50 -> x52, starting transfers between devices: 55.1 us -> 51 us  [swap(): lax.ppermute(value, axis, [(source, source ^ flip) for source in range(co...]
  transfers between devices with their start and end apart: 56 -> 58, of which waited for: 37 -> 40; matrix products, arithmetic and copies ran while one was open for 27% -> 30% of each run, Pallas kernels for 7% -> 8%
where the time goes in v3:
time: 677 us; the launch traced here: 672 us
  waiting for transfers between devices  302 us (45%)
  matrix products  137 us (20%)
  local copies, waits for them, and re-layouts  61.4 us (9%)
  Pallas kernels  57.9 us (9%)
  starting transfers between devices  51.5 us (8%)
  other arithmetic  45.4 us (7%)
  between operations  16.3 us (2%)
    ppermute x52, waiting for transfers between devices, swap(): lax.ppermute(value, axis, [(source, source ^ flip) for source in range(co...  218 us
    all_gather x1, waiting for transfers between devices, on_device(): full_attn = lax.all_gather(low_attn, 'dp', axis=0, tiled=True)  73.4 us
    ppermute x52, starting transfers between devices, swap(): lax.ppermute(value, axis, [(source, source ^ flip) for source in range(co...  51 us
    dot_general x8, matrix products, mat_last(): return lax.dot_general(left, right, BOTH_LAST, preferred_element_type=F32)  47.7 us
    dot_general x10, matrix products, mat_first(): return lax.dot_general(left, right, BOTH_FIRST, preferred_element_type=F32)  45.7 us
    dot_general x13, matrix products, mat_bf(): return jnp.dot(left, right, preferred_element_type=F32)  43.6 us
    unnamed x189, local copies, waits for them, and re-layouts  38.5 us
    pallas_call x1, Pallas kernels, attn_bwd(): pl.pallas_call(functools.partial(bwd_kernel, scale=scale, chunk=chunk), g...  28 us
  transfers between devices with their start and end apart: 58, of which 40 were waited for; matrix products, arithmetic and copies ran while one was open for 30% of the time, Pallas kernels for 8%

profile of v3, /device:TPU:0, one launch (start us, length us, event | category | flops | bytes accessed | tf_op | source)
XLA Modules:
  0.0 671.7 jit_solution(17714665410200451307)
XLA Ops:
  25.0 73.4 %all-gather.4.cloned.1.call-done = bf16[2048,2048]{0,1:T(8,128)(2,1)} async-done(((bf16[256,2048]{0,1:T(8,128)(2,1)}), bf16[2048,2048]{0,1:T(8,128)(2,1)}) %all-gather.4.cloned.1.call-update) | async-done | bytes 8388624 | tf_op jit(solution)/shard_map/all_gather | solution.py:387
  98.4 10.1 %add_convert_fusion.3.q_ref.ko_ref.vo_ref = bf16[1024,1536]{1,0:T(8,128)(2,1)S(1)} fusion(bf16[1024,2048]{1,0:T(8,128)(2,1)} %copy-done.22, bf16[2048,2048]{0,1:T(8,128)(2,1)} %all-gather.4.cloned.1.call-done, f32[1536]{0:T(1024)S(1)} %pad_maximum_fusion.23), kind=kOutput, calls=%fused_computation.21 | convolution fusion | flops 6445596672 | bytes 13637632 | tf_op jit(solution)/shard_map/dot_general | solution.py:27
  116.1 21.5 %attention_forward.1 = (bf16[1024,512]{1,0:T(8,128)(2,1)S(1)}, f32[4,1,1024]{2,1,0:T(1,128)S(1)}) custom-call(bf16[1024,1536]{1,0:T(8,128)(2,1)} %copy-done.44, bf16[1024,1536]{1,0:T(8,128)(2,1)} %copy-done.44, bf16[1024,1024]{1,0:T(8,128)(2,1)S(1)} %collective-permute-done.1.kf_ref.vf_ref, bf16[1024,1536]{1,0:T(8,128)(2,1)} %copy-done.44, ...), custom_call_target="tpu_custom_call" | custom-call | flops 12884901888 | bytes 6291456 | tf_op jit(solution)/shard_map/attention_forward/pallas_call | solution.py:223
  145.1 9.5 %collective-permute-done.2 = bf16[128,2048]{1,0:T(8,128)(2,1)S(1)} collective-permute-done((bf16[128,2048]{1,0:T(8,128)(2,1)S(1)}, bf16[128,2048]{1,0:T(8,128)(2,1)S(1)}, u32[]{:S(2)}, u32[]{:S(2)}) %collective-permute-start.2) | collective-permute-done | bytes 524320 | tf_op jit(solution)/shard_map/ppermute | solution.py:40
  159.2 21.2 %collective-permute-done.4.one = bf16[256,2048]{1,0:T(8,128)(2,1)S(1)} collective-permute-done((bf16[256,2048]{1,0:T(8,128)(2,1)S(1)}, bf16[256,2048]{1,0:T(8,128)(2,1)S(1)}, u32[]{:S(2)}, u32[]{:S(2)}) %collective-permute-start.4) | collective-permute-done | bytes 1048608 | tf_op jit(solution)/shard_map/ppermute | solution.py:40
  185.5 20.3 %collective-permute-done.7 = bf16[256,2048]{1,0:T(8,128)(2,1)S(1)} collective-permute-done((bf16[256,2048]{1,0:T(8,128)(2,1)S(1)}, bf16[256,2048]{1,0:T(8,128)(2,1)S(1)}, u32[]{:S(2)}, u32[]{:S(2)}) %collective-permute-start.7) | collective-permute-done | bytes 1048608 | tf_op jit(solution)/shard_map/ppermute | solution.py:40
  212.0 6.2 collective-permute-done.8
  220.1 19.0 %fusion.7 = (bf16[1024,2048]{1,0:T(8,128)(2,1)}, bf16[1024,2048]{1,0:T(8,128)(2,1)S(1)}) fusion(f32[2048]{0:T(1024)S(1)} %copy-done.72, bf16[1024,2048]{1,0:T(8,128)(2,1)} %constant_dynamic-update-slice_fusion, bf16[2048,2048]{0,1:T(8,128)(2,1)} %all-gather.6.cloned.1.call-done), kind=kOutput, calls=%fused_computation.10 | convolution fusion | flops 8636071936 | bytes 20979712 | tf_op jit(solution)/shard_map/dot_general | solution.py:31
  256.3 7.3 %all-gather.8.cloned.1.call-done = bf16[2048,2048]{1,0:T(8,128)(2,1)} async-done(((bf16[2048,256]{1,0:T(8,128)(2,1)}), bf16[2048,2048]{1,0:T(8,128)(2,1)}) %all-gather.8.cloned.1.call-update) | async-done | bytes 8388624 | tf_op jit(solution)/shard_map/all_gather | solution.py:390
  263.5 6.2 convolution_convert_fusion.2
  277.7 6.3 collective-permute-done.13
  292.1 17.7 %collective-permute-done.15.one = bf16[256,2048]{1,0:T(8,128)(2,1)S(1)} collective-permute-done((bf16[256,2048]{1,0:T(8,128)(2,1)S(1)}, bf16[256,2048]{1,0:T(8,128)(2,1)S(1)}, u32[]{:S(2)}, u32[]{:S(2)}) %collective-permute-start.15) | collective-permute-done | bytes 1048608 | tf_op jit(solution)/shard_map/ppermute | solution.py:40
  321.4 16.4 %collective-permute-done.17 = bf16[256,2048]{1,0:T(8,128)(2,1)S(1)} collective-permute-done((bf16[256,2048]{1,0:T(8,128)(2,1)S(1)}, bf16[256,2048]{1,0:T(8,128)(2,1)S(1)}, u32[]{:S(2)}, u32[]{:S(2)}) %collective-permute-start.17) | collective-permute-done | bytes 1048608 | tf_op jit(solution)/shard_map/ppermute | solution.py:40
  364.4 10.9 %multiply_convert_fusion = bf16[768,2048]{1,0:T(8,128)(2,1)S(1)} fusion(bf16[2048,2048]{1,0:T(8,128)(2,1)} %all-gather.8.cloned.1.call-done, bf16[256,2048]{1,0:T(8,128)(2,1)} %copy-done.38, bf16[256,2048]{1,0:T(8,128)(2,1)} %copy-done.37, bf16[256,2048]{1,0:T(8,128)(2,1)} %copy-done.36, bf16[1024,2048]{1,0:T(8,128)(2,1)} %get-tuple-element.110), kind=kOutput, calls=%fused_computation.20 | convolution fusion | flops 6456606720 | bytes 17825792 | tf_op jit(solution)/shard_map/dot_general | solution.py:31
  376.2 7.2 %convolution_convert_fusion.1 = bf16[256,2048]{1,0:T(8,128)(2,1)S(1)} fusion(bf16[2048,2048]{0,1:T(8,128)(2,1)} %all-gather.6.cloned.1.call-done, bf16[768,2048]{1,0:T(8,128)(2,1)S(1)} %multiply_convert_fusion), kind=kOutput, calls=%fused_computation.49 | convolution fusion | flops 2148007936 | bytes 10485760 | tf_op jit(solution)/shard_map/dot_general | solution.py:27
  391.0 6.6 collective-permute-done.23
  407.0 6.9 %fusion.112 = f32[1024,2048]{1,0:T(8,128)S(1)} fusion(bf16[1024,1024]{1,0:T(8,128)(2,1)S(1)} %copy-done.67, bf16[1024,2048]{1,0:T(8,128)(2,1)} %collective-permute-done.27), kind=kOutput, calls=%fused_computation.270 | convolution fusion | flops 4294967296 | bytes 14680064 | tf_op jit(solution)/shard_map/dot_general | solution.py:35
  413.9 6.9 %add_convert_fusion = bf16[1024,2048]{1,0:T(8,128)(2,1)} fusion(f32[1024,2048]{1,0:T(8,128)S(1)} %fusion.112, bf16[1024,2048]{1,0:T(8,128)(2,1)S(1)} %pad_maximum_fusion.1, bf16[1024,256]{1,0:T(8,128)(2,1)S(1)} %copy-done.59, bf16[1024,256]{1,0:T(8,128)(2,1)S(1)} %copy-done.58, bf16[1024,256]{1,0:T(8,128)(2,1)S(1)} %copy-done.57, ...), kind=kOutput, calls=%fused_computation.14 | convolution fusion | flops 4307550208 | bytes 18874368 | tf_op jit(solution)/shard_map/dot_general | solution.py:35
  436.3 19.8 %collective-permute-done.29 = bf16[256,2048]{1,0:T(8,128)(2,1)S(1)} collective-permute-done((bf16[256,2048]{1,0:T(8,128)(2,1)S(1)}, bf16[256,2048]{1,0:T(8,128)(2,1)S(1)}, u32[]{:S(2)}, u32[]{:S(2)}) %collective-permute-start.29) | collective-permute-done | bytes 1048608 | tf_op jit(solution)/shard_map/ppermute | solution.py:40
  459.1 9.3 %collective-permute-done.30 = bf16[128,2048]{1,0:T(8,128)(2,1)S(1)} collective-permute-done((bf16[128,2048]{1,0:T(8,128)(2,1)S(1)}, bf16[128,2048]{1,0:T(8,128)(2,1)S(1)}, u32[]{:S(2)}, u32[]{:S(2)}) %collective-permute-start.30) | collective-permute-done | bytes 524320 | tf_op jit(solution)/shard_map/ppermute | solution.py:40
  475.8 28.0 %attention_backward.1 = (bf16[1024,512]{1,0:T(8,128)(2,1)S(1)}, f32[1024,512]{1,0:T(8,128)}, f32[1024,512]{1,0:T(8,128)}, bf16[2,1024,512]{2,1,0:T(8,128)(2,1)}) custom-call(bf16[1024,1536]{1,0:T(8,128)(2,1)} %copy-done.44, bf16[1024,512]{1,0:T(8,128)(2,1)S(1)} %convolution_convert_fusion.3.do_ref, bf16[1024,512]{1,0:T(8,128)(2,1)S(1)} %copy-done.11, ...), custom_call_target="tpu_custom_call" | custom-call | flops 21474836480 | bytes 12582912 | tf_op jit(solution)/shard_map/attention_backward/pallas_call | solution.py:274
  518.3 12.7 %collective-permute-done.32 = bf16[256,2048]{1,0:T(8,128)(2,1)S(1)} collective-permute-done((bf16[256,2048]{1,0:T(8,128)(2,1)S(1)}, bf16[256,2048]{1,0:T(8,128)(2,1)S(1)}, u32[]{:S(2)}, u32[]{:S(2)}) %collective-permute-start.32) | collective-permute-done | bytes 1048608 | tf_op jit(solution)/shard_map/ppermute | solution.py:40
  580.9 16.7 %collective-permute-done.41 = bf16[256,2048]{1,0:T(8,128)(2,1)S(1)} collective-permute-done((bf16[256,2048]{1,0:T(8,128)(2,1)S(1)}, bf16[256,2048]{1,0:T(8,128)(2,1)S(1)}, u32[]{:S(2)}, u32[]{:S(2)}) %collective-permute-start.41) | collective-permute-done | bytes 1048608 | tf_op jit(solution)/shard_map/ppermute | solution.py:40
  646.1 8.8 %collective-permute-done.45 = bf16[128,2048]{1,0:T(8,128)(2,1)S(1)} collective-permute-done((bf16[128,2048]{1,0:T(8,128)(2,1)S(1)}, bf16[128,2048]{1,0:T(8,128)(2,1)S(1)}, u32[]{:S(2)}, u32[]{:S(2)}) %collective-permute-start.45) | collective-permute-done | bytes 524320 | tf_op jit(solution)/shard_map/ppermute | solution.py:40
  (433 shorter events, 286.7 us)
Async XLA Ops:
  7.2 91.2 %all-gather.4.cloned.1.call-start = ((), (), s32[]{:S(2)}) async-start(), calls=%async_computation.3 | async-start | bytes 9437184 | tf_op jit(solution)/shard_map/all_gather | solution.py:387
  13.1 207.1 %all-gather.6.cloned.1.call-start = ((), (), s32[]{:S(2)}) async-start(), calls=%async_computation.4 | async-start | bytes 9437184 | tf_op jit(solution)/shard_map/all_gather | solution.py:389
  14.3 249.3 %all-gather.8.cloned.1.call-start = ((), (), s32[]{:S(2)}) async-start(), calls=%async_computation.5 | async-start | bytes 9437184 | tf_op jit(solution)/shard_map/all_gather | solution.py:390
  113.6 361.1 %reduce-scatter.4.cloned.1.call-start = ((), (), s32[]{:S(2)}) async-start(), calls=%async_computation.6 | async-start | bytes 5242880 | tf_op jit(solution)/shard_map/reduce_scatter | solution.py:377
  156.0 24.3 %collective-permute-start.4 = (bf16[256,2048]{1,0:T(8,128)(2,1)S(1)}, bf16[256,2048]{1,0:T(8,128)(2,1)S(1)}, u32[]{:S(2)}, u32[]{:S(2)}) collective-permute-start(bf16[256,2048]{1,0:T(8,128)(2,1)S(1)} %pad_maximum_fusion.12), channel_id=1, source_target_pairs={{0,1},{1,0},{2,3},{3,2},{4,5},{5,4},{6,7},{7,6},{8,9},{9,8},{10,11... | collective-permute-start | bytes 3145736 | tf_op jit(solution)/shard_map/ppermute | solution.py:40
  184.1 24.3 %collective-permute-start.6 = (bf16[256,2048]{1,0:T(8,128)(2,1)S(1)}, bf16[256,2048]{1,0:T(8,128)(2,1)S(1)}, u32[]{:S(2)}, u32[]{:S(2)}) collective-permute-start(bf16[256,2048]{1,0:T(8,128)(2,1)S(1)} %get-tuple-element.95), channel_id=1, source_target_pairs={{0,1},{1,0},{2,3},{3,2},{4,5},{5,4},{6,7},{7,6},{8,9},{9,8},{10,11... | collective-permute-start | bytes 3145736 | tf_op jit(solution)/shard_map/ppermute | solution.py:40
  285.4 24.3 %collective-permute-start.15 = (bf16[256,2048]{1,0:T(8,128)(2,1)S(1)}, bf16[256,2048]{1,0:T(8,128)(2,1)S(1)}, u32[]{:S(2)}, u32[]{:S(2)}) collective-permute-start(bf16[256,2048]{1,0:T(8,128)(2,1)S(1)} %pad_maximum_fusion.14), channel_id=1, source_target_pairs={{0,1},{1,0},{2,3},{3,2},{4,5},{5,4},{6,7},{7,6},{8,9},{9,8},{10,11... | collective-permute-start | bytes 3145736 | tf_op jit(solution)/shard_map/ppermute | solution.py:40
  364.4 184.6 %reduce-scatter.6.cloned.1.call-start = ((), (), s32[]{:S(2)}) async-start(), calls=%async_computation.7 | async-start | bytes 5242880 | tf_op jit(solution)/shard_map/reduce_scatter | solution.py:377
  376.0 31.0 %collective-permute-start.27 = (bf16[1024,2048]{1,0:T(8,128)(2,1)S(1)}, bf16[1024,2048]{1,0:T(8,128)(2,1)}, u32[]{:S(2)}, u32[]{:S(2)}) collective-permute-start(bf16[1024,2048]{1,0:T(8,128)(2,1)S(1)} %pad_maximum_fusion.1), channel_id=1, source_target_pairs={{0,4},{4,0},{8,12},{12,8},{16,20},{20,16},{24,28},{28,24},{1,5},{5... | collective-permute-start | bytes 12582920 | tf_op jit(solution)/shard_map/ppermute | solution.py:40
  399.6 24.4 %collective-permute-start.25 = (bf16[256,2048]{1,0:T(8,128)(2,1)}, bf16[256,2048]{1,0:T(8,128)(2,1)S(1)}, u32[]{:S(2)}, u32[]{:S(2)}) collective-permute-start(bf16[256,2048]{1,0:T(8,128)(2,1)} %pad_maximum_fusion.16), channel_id=1, source_target_pairs={{0,1},{1,0},{2,3},{3,2},{4,5},{5,4},{6,7},{7,6},{8,9},{9,8},{10,11... | collective-permute-start | bytes 3145736 | tf_op jit(solution)/shard_map/ppermute | solution.py:40
  401.8 24.2 %collective-permute-start.26 = (bf16[256,2048]{1,0:T(8,128)(2,1)}, bf16[256,2048]{1,0:T(8,128)(2,1)}, u32[]{:S(2)}, u32[]{:S(2)}) collective-permute-start(bf16[256,2048]{1,0:T(8,128)(2,1)} %pad_maximum_fusion.17), channel_id=1, source_target_pairs={{0,2},{1,3},{2,0},{3,1},{4,6},{5,7},{6,4},{7,5},{8,10},{9,11},{10,... | collective-permute-start | bytes 3145736 | tf_op jit(solution)/shard_map/ppermute | solution.py:40
  434.5 24.1 %collective-permute-start.28 = (bf16[256,2048]{1,0:T(8,128)(2,1)S(1)}, bf16[256,2048]{1,0:T(8,128)(2,1)S(1)}, u32[]{:S(2)}, u32[]{:S(2)}) collective-permute-start(bf16[256,2048]{1,0:T(8,128)(2,1)S(1)} %get-tuple-element.125), channel_id=1, source_target_pairs={{0,1},{1,0},{2,3},{3,2},{4,5},{5,4},{6,7},{7,6},{8,9},{9,8},{10,11... | collective-permute-start | bytes 3145736 | tf_op jit(solution)/shard_map/ppermute | solution.py:40
  474.7 186.0 %reduce-scatter.8.cloned.1.call-start = ((), (), s32[]{:S(2)}) async-start(), calls=%async_computation.8 | async-start | bytes 5242880 | tf_op jit(solution)/shard_map/reduce_scatter | solution.py:377
  505.4 25.6 %collective-permute-start.32 = (bf16[256,2048]{1,0:T(8,128)(2,1)S(1)}, bf16[256,2048]{1,0:T(8,128)(2,1)S(1)}, u32[]{:S(2)}, u32[]{:S(2)}) collective-permute-start(bf16[256,2048]{1,0:T(8,128)(2,1)S(1)} %copy-done.8), channel_id=1, source_target_pairs={{0,1},{1,0},{2,3},{3,2},{4,5},{5,4},{6,7},{7,6},{8,9},{9,8},{10,11... | collective-permute-start | bytes 3145736 | tf_op jit(solution)/shard_map/ppermute | solution.py:40
  506.4 25.3 %collective-permute-start.33 = (bf16[256,2048]{1,0:T(8,128)(2,1)S(1)}, bf16[256,2048]{1,0:T(8,128)(2,1)S(1)}, u32[]{:S(2)}, u32[]{:S(2)}) collective-permute-start(bf16[256,2048]{1,0:T(8,128)(2,1)S(1)} %copy-done.8), channel_id=1, source_target_pairs={{0,2},{1,3},{2,0},{3,1},{4,6},{5,7},{6,4},{7,5},{8,10},{9,11},{10,... | collective-permute-start | bytes 3145736 | tf_op jit(solution)/shard_map/ppermute | solution.py:40
  514.3 30.8 %collective-permute-start.40 = (bf16[1024,1536]{1,0:T(8,128)(2,1)S(1)}, bf16[1024,1536]{1,0:T(8,128)(2,1)}, u32[]{:S(2)}, u32[]{:S(2)}) collective-permute-start(bf16[1024,1536]{1,0:T(8,128)(2,1)S(1)} %get-tuple-element.139), channel_id=1, source_target_pairs={{0,4},{4,0},{8,12},{12,8},{16,20},{20,16},{24,28},{28,24},{1,5},{5... | collective-permute-start | bytes 9437192 | tf_op jit(solution)/shard_map/ppermute | solution.py:40
  532.6 38.3 %collective-permute-start.34 = (bf16[128,2048]{1,0:T(8,128)(2,1)}, bf16[128,2048]{1,0:T(8,128)(2,1)}, u32[]{:S(2)}, u32[]{:S(2)}) collective-permute-start(bf16[128,2048]{1,0:T(8,128)(2,1)} %slice.450), channel_id=1, source_target_pairs={{0,1},{1,0},{2,3},{3,2},{4,5},{5,4},{6,7},{7,6},{8,9},{9,8},{10,11... | collective-permute-start | bytes 1572872 | tf_op jit(solution)/shard_map/ppermute | solution.py:40
  534.5 36.5 %collective-permute-start.35 = (bf16[128,2048]{1,0:T(8,128)(2,1)}, bf16[128,2048]{1,0:T(8,128)(2,1)}, u32[]{:S(2)}, u32[]{:S(2)}) collective-permute-start(bf16[128,2048]{1,0:T(8,128)(2,1)} %slice.451), channel_id=1, source_target_pairs={{0,2},{1,3},{2,0},{3,1},{4,6},{5,7},{6,4},{7,5},{8,10},{9,11},{10,... | collective-permute-start | bytes 1572872 | tf_op jit(solution)/shard_map/ppermute | solution.py:40
  539.6 31.5 %collective-permute-start.38 = (bf16[128,2048]{1,0:T(8,128)(2,1)}, bf16[128,2048]{1,0:T(8,128)(2,1)}, u32[]{:S(2)}, u32[]{:S(2)}) collective-permute-start(bf16[128,2048]{1,0:T(8,128)(2,1)} %get-tuple-element.251), channel_id=1, source_target_pairs={{0,1},{1,0},{2,3},{3,2},{4,5},{5,4},{6,7},{7,6},{8,9},{9,8},{10,11... | collective-permute-start | bytes 1572872 | tf_op jit(solution)/shard_map/ppermute | solution.py:40
  540.6 30.4 %collective-permute-start.39 = (bf16[128,2048]{1,0:T(8,128)(2,1)}, bf16[128,2048]{1,0:T(8,128)(2,1)}, u32[]{:S(2)}, u32[]{:S(2)}) collective-permute-start(bf16[128,2048]{1,0:T(8,128)(2,1)} %get-tuple-element.250), channel_id=1, source_target_pairs={{0,2},{1,3},{2,0},{3,1},{4,6},{5,7},{6,4},{7,5},{8,10},{9,11},{10,... | collective-permute-start | bytes 1572872 | tf_op jit(solution)/shard_map/ppermute | solution.py:40
  572.7 24.8 %collective-permute-start.41 = (bf16[256,2048]{1,0:T(8,128)(2,1)S(1)}, bf16[256,2048]{1,0:T(8,128)(2,1)S(1)}, u32[]{:S(2)}, u32[]{:S(2)}) collective-permute-start(bf16[256,2048]{1,0:T(8,128)(2,1)S(1)} %pad_maximum_fusion.18), channel_id=1, source_target_pairs={{0,1},{1,0},{2,3},{3,2},{4,5},{5,4},{6,7},{7,6},{8,9},{9,8},{10,11... | collective-permute-start | bytes 3145736 | tf_op jit(solution)/shard_map/ppermute | solution.py:40
  575.4 24.6 %collective-permute-start.42 = (bf16[256,2048]{1,0:T(8,128)(2,1)S(1)}, bf16[256,2048]{1,0:T(8,128)(2,1)S(1)}, u32[]{:S(2)}, u32[]{:S(2)}) collective-permute-start(bf16[256,2048]{1,0:T(8,128)(2,1)S(1)} %pad_maximum_fusion.19), channel_id=1, source_target_pairs={{0,2},{1,3},{2,0},{3,1},{4,6},{5,7},{6,4},{7,5},{8,10},{9,11},{10,... | collective-permute-start | bytes 3145736 | tf_op jit(solution)/shard_map/ppermute | solution.py:40
  613.6 29.4 %collective-permute-start.43 = (bf16[256,2048]{1,0:T(8,128)(2,1)}, bf16[256,2048]{1,0:T(8,128)(2,1)S(1)}, u32[]{:S(2)}, u32[]{:S(2)}) collective-permute-start(bf16[256,2048]{1,0:T(8,128)(2,1)} %get-tuple-element.190), channel_id=1, source_target_pairs={{0,1},{1,0},{2,3},{3,2},{4,5},{5,4},{6,7},{7,6},{8,9},{9,8},{10,11... | collective-permute-start | bytes 3145736 | tf_op jit(solution)/shard_map/ppermute | solution.py:40
  614.8 25.7 %collective-permute-start.44 = (bf16[256,2048]{1,0:T(8,128)(2,1)}, bf16[256,2048]{1,0:T(8,128)(2,1)}, u32[]{:S(2)}, u32[]{:S(2)}) collective-permute-start(bf16[256,2048]{1,0:T(8,128)(2,1)} %get-tuple-element.190), channel_id=1, source_target_pairs={{0,2},{1,3},{2,0},{3,1},{4,6},{5,7},{6,4},{7,5},{8,10},{9,11},{10,... | collective-permute-start | bytes 3145736 | tf_op jit(solution)/shard_map/ppermute | solution.py:40
  (117 other events, 1285.8 us)
Sparse Core Ops, SparseCore 0:
  13.2 85.1 all-gather.3
  100.6 80.2 all-gather.5
  182.5 81.0 all-gather.7
  364.5 74.4 reduce-scatter.3
  474.8 74.1 reduce-scatter.5
  565.2 80.0 reduce-scatter.7

commit v4 on v3

--- a/solution.py
+++ b/solution.py
@@ -100,15 +100,15 @@
     three = piece(3).astype(LOW)
     half = three.shape[0] // 2
     come_top, come_low = swap(three[:half], "tensor", 1), swap(three[half:], "tensor", 2)
-    one, two = piece(1, three), piece(2, three)
     first = [make(three) for make in after_first]
+    one, two = piece(1, (three, *first)), piece(2, (three, *first))
     come_top, come_low = after((come_top, come_low), *first)
     one = jnp.concatenate([one[:half].astype(LOW), (one[half:] + come_low.astype(F32)).astype(LOW)])
     two = jnp.concatenate([(two[:half] + come_top.astype(F32)).astype(LOW), two[half:].astype(LOW)])
     from_one, from_two = swap(one, "tensor", 1), swap(two, "tensor", 2)
     here = piece(0, (one, two))
     second = [make((one, two)) for make in after_second]
-    from_one, from_two = after((from_one, from_two), here, *second)
+    from_one, from_two = after((from_one, from_two), here, *jax.tree.leaves(second))
     return (here, from_one, from_two), first, second
 
 
@@ -281,7 +281,7 @@
         out_shape=[jax.ShapeDtypeStruct((rows,heads*HEAD_DIM),LOW)]+[jax.ShapeDtypeStruct((rows,heads*HEAD_DIM),F32)]*2+[jax.ShapeDtypeStruct((2,rows,heads*HEAD_DIM),LOW)],
         scratch_shapes=[pltpu.VMEM((rows,HEAD_DIM),F32)]*4+[pltpu.VMEM((HEAD_DIM,rows),LOW)]*2,
         compiler_params=pltpu.CompilerParams(vmem_limit_bytes=48<<20),
-        cost_estimate=pl.CostEstimate(flops=20*rows*2*rows*HEAD_DIM*heads,transcendentals=heads*rows*2*rows,bytes_accessed=heads*HEAD_DIM*rows*2*12),
+        cost_estimate=pl.CostEstimate(flops=rows*heads,transcendentals=0,bytes_accessed=heads*HEAD_DIM*rows*2),
         name='attention_backward')(qkv,do,o,lse,qkv,kv_far,qkv,kv_far,bias_own,bias_far)
 
 
@@ -378,8 +378,8 @@
             grad, "dp", scatter_dimension=0, tiled=True, axis_index_groups=core_groups
         )
 
-    def split_rows(value):
-        return [value[k * block : (k + 1) * block] for k in range(value.shape[0] // block)]
+    def rows_of(value, k):
+        return value[k * block : (k + 1) * block]
 
     low_attn = jnp.concatenate([w_query, w_key, w_value, w_out.T], axis=1).astype(LOW)
     low_inner = w_inner.T.astype(LOW)
@@ -395,8 +395,7 @@
     far_kv = swap(qkv[:, width_here:], "dp", 1)
     mixed, lse = attn_fwd(qkv, far_kv, own_bias[None], far_bias[None], heads_here)
 
-    mixed_blocks = split_rows(mixed)
-    attn_parts, _, _ = scatter_rows(lambda k, gate: mat_bf(gated(mixed_blocks[k], gate), full_out))
+    attn_parts, _, _ = scatter_rows(lambda k, gate: mat_bf(rows_of(gated(mixed, gate), k), full_out))
     resid_one, hidden, hidden_here = on_rows(
         norm_one_kernel,
         "norm_one",
@@ -413,8 +412,7 @@
     act_far = swap(act_low, "dp", 1)
     act_low, act_slope = after((act_low, act_slope), mixed_far, act_far, hidden_pair)
 
-    act_blocks = split_rows(act_low)
-    outer_parts, _, _ = scatter_rows(lambda k, gate: mat_bf(gated(act_blocks[k], gate), full_outer))
+    outer_parts, _, _ = scatter_rows(lambda k, gate: mat_bf(rows_of(gated(act_low, gate), k), full_outer))
     grad_two, outer_here, output, sums_two = on_rows(
         norm_two_kernel,
         "norm_two",
@@ -443,6 +441,7 @@
     near_mine, near_far = shared_columns(jnp.concatenate([outer_here, *outer_near]))
     grad_near = weight_grad([(near_mine, act_low[:near]), (near_far, act_far[:near])])
     outer_rest = after(outer_rest, grad_near)
+    output_near = gather_near(after(output, *outer_rest))
     outer_rest = jnp.concatenate(outer_rest)
     rest_mine, rest_far = shared_columns(outer_rest)
     grad_w_outer = (
@@ -453,11 +452,16 @@
     inner_away = act_grad(away_rows, 1)
     inner_low = jnp.concatenate([inner_here, inner_away])
     inner_far = swap(inner_low, "dp", 1)
-    inner_blocks = [inner_here, *split_rows(inner_away)]
-
+
+    inner_three, output_near = lax.optimization_barrier(
+        (mat_bf(rows_of(inner_away, 2), full_inner), output_near)
+    )
 
     def inner_part(k, gate):
-        return mat_bf(gated(inner_blocks[k], gate), full_inner)
+        if k == 3:
+            return inner_three
+        rows = inner_here if k == 0 else inner_away
+        return mat_bf(rows_of(gated(rows, gate), max(k - 1, 0)), full_inner)
 
     def inner_weight(sent):
         mine, far = after((inner_low, inner_far), sent)
@@ -472,21 +476,18 @@
         True,
     )
     owner_inner = to_owner(after(grad_w_inner, owner_outer, attn_here))
-    attn_low = gather_rows(attn_here)
+    output_rest = gather_rest(output, after(output_near, *hidden_parts))
+    attn_low = gather_rows(after(attn_here, output_rest))
     mixed_low = mat_last(attn_low, full_out).astype(LOW)
-    output = after(output, attn_low)
     query_low, own_key, own_value, far_pair = attn_bwd(
         qkv, far_kv, mixed_low, mixed, lse, own_bias_wide, far_bias_wide, heads_here, 512, 256
     )
-    output_near = after(gather_near(output), query_low)
-    output_rest = gather_rest(output, output_near)
     attn_pair = shared_columns(after(attn_low, query_low))
     far_key, far_value = after(swap(far_pair, "dp", 1), attn_pair).astype(F32)
     key_low = (own_key + far_key).astype(LOW)
     value_low = (own_value + far_value).astype(LOW)
     qkv_low = jnp.concatenate([query_low, key_low, value_low], axis=1)
     qkv_far = swap(qkv_low, "dp", 1)
-    qkv_blocks = split_rows(qkv_low)
 
     def attn_weight(sent):
         mine, far = after((qkv_low, qkv_far), sent, owner_inner)
@@ -495,29 +496,35 @@
         grad_w_out = weight_grad([(attn_mine, mixed), (attn_far, mixed_far)]).astype(LOW)
         return jnp.concatenate([grad_w_qkv, grad_w_out], axis=1)
 
-    (here, one, two), (grad_w_attn, output_rest), _ = scatter_rows(
-        lambda k, gate: mat_last(gated(qkv_blocks[k], gate), full_qkv), after_first=[attn_weight, lambda sent: output_rest]
+    def total_sums(sent):
+        rows = jnp.concatenate([sums_one[:3], sums_two[:3]]).reshape(-1)
+        inner_sum = jnp.sum(inner_low.astype(F32), axis=0)
+        qkv_sum = jnp.sum(qkv_low.astype(F32), axis=0)
+        return everyone(after(jnp.concatenate([rows, inner_sum, qkv_sum]), sent), ("dp",))
+
+    def owned(sent):
+        outer, inner = after((owner_outer, owner_inner), sent)
+        return outer.T.astype(F32), inner.astype(F32)
+
+    (here, one, two), (grad_w_attn,), (sums, (grad_w_outer, grad_w_inner)) = scatter_rows(
+        lambda k, gate: mat_last(rows_of(gated(qkv_low, gate), k), full_qkv),
+        after_first=[attn_weight],
+        after_second=[total_sums, owned],
     )
     owner_attn = to_owner(after(grad_w_attn, owner_inner))
     tokens_here = (grad_one + (here + one.astype(F32) + two.astype(F32))).astype(LOW)
-    grad_tokens = gather_rows(tokens_here)
-    output = jnp.concatenate([output, *output_near, *output_rest])
+    tokens_near = gather_near(tokens_here)
+    output = jnp.concatenate(after((output, *output_near, *output_rest), tokens_near))
+    tokens_rest = gather_rest(tokens_here, tokens_near)
+    grad_tokens = jnp.concatenate([tokens_here, *tokens_near, *tokens_rest])
     output, grad_tokens = (reorder(rows).astype(F32) for rows in (output, grad_tokens))
 
-    over_rows = jnp.concatenate([sums_one[:3], sums_two[:3]])
-    over_rows = everyone(after(over_rows, tokens_here), ("tensor",)).reshape(-1)
-    inner_sum = jnp.sum(inner_low.astype(F32), axis=0)
-    qkv_sum = jnp.sum(qkv_low.astype(F32), axis=0)
-    sums = everyone(jnp.concatenate([over_rows, inner_sum, qkv_sum]), ("dp",))
-    grad_b_out, grad_ln1_gain, grad_ln1_bias, grad_b_outer, grad_ln2_gain, grad_ln2_bias = sums[
-        : 6 * model
-    ].reshape(6, model)
     grad_b_inner = sums[6 * model : -3 * width_here]
     grad_b_qkv = sums[-3 * width_here :]
-
-    grad_w_outer, grad_w_inner, grad_w_attn = (
-        grad.astype(F32) for grad in (owner_outer, owner_inner, owner_attn)
-    )
+    sums = everyone(after(sums[: 6 * model], tokens_rest), ("tensor",)).reshape(6, model)
+    grad_b_out, grad_ln1_gain, grad_ln1_bias, grad_b_outer, grad_ln2_gain, grad_ln2_bias = sums
+
+    grad_w_attn = owner_attn.astype(F32)
     grad_w_query, grad_w_key, grad_w_value, grad_w_out = jnp.split(grad_w_attn, 4, axis=1)
     return (
         output,
@@ -533,7 +540,7 @@
         grad_ln1_bias,
         grad_w_inner,
         grad_b_inner,
-        grad_w_outer.T,
+        grad_w_outer,
         grad_b_outer,
         grad_ln2_gain,
         grad_ln2_bias,

time: 677 us -> 656 us (0.969)
  waiting for transfers between devices: 302 us -> 271 us
  matrix products: 137 us -> 167 us
  starting transfers between devices: 51.5 us -> 40.3 us
  local copies, waits for them, and re-layouts: 61.4 us -> 52.6 us
    ppermute x52, waiting for transfers between devices: 218 us -> 188 us  [swap(): lax.ppermute(value, axis, [(source, source ^ flip) for source in range(co...]
    dot_general x13, matrix products: 43.6 us -> 58 us  [mat_bf(): return jnp.dot(left, right, preferred_element_type=F32)]
    dot_general x8, matrix products: 47.7 us -> 59 us  [mat_last(): return lax.dot_general(left, right, BOTH_LAST, preferred_element_type=F32)]
    ppermute x52, starting transfers between devices: 51 us -> 39.9 us  [swap(): lax.ppermute(value, axis, [(source, source ^ flip) for source in range(co...]
    unnamed x189 -> x155, local copies, waits for them, and re-layouts: 38.5 us -> 35.8 us
  transfers between devices with their start and end apart: 58 -> 58, of which waited for: 40 -> 37; matrix products, arithmetic and copies ran while one was open for 30% -> 35% of each run, Pallas kernels for 8% -> 8%
where the time goes in v4:
time: 656 us; the launch traced here: 650 us
  waiting for transfers between devices  271 us (41%)
  matrix products  167 us (25%)
  Pallas kernels  58.8 us (9%)
  local copies, waits for them, and re-layouts  52.6 us (8%)
  other arithmetic  44.4 us (7%)
  starting transfers between devices  40.3 us (6%)
  between operations  16.2 us (2%)
    ppermute x52, waiting for transfers between devices, swap(): lax.ppermute(value, axis, [(source, source ^ flip) for source in range(co...  188 us
    all_gather x1, waiting for transfers between devices, on_device(): full_attn = lax.all_gather(low_attn, 'dp', axis=0, tiled=True)  73.3 us
    dot_general x8, matrix products, mat_last(): return lax.dot_general(left, right, BOTH_LAST, preferred_element_type=F32)  59 us
    dot_general x13, matrix products, mat_bf(): return jnp.dot(left, right, preferred_element_type=F32)  58 us
    dot_general x10, matrix products, mat_first(): return lax.dot_general(left, right, BOTH_FIRST, preferred_element_type=F32)  50 us
    ppermute x52, starting transfers between devices, swap(): lax.ppermute(value, axis, [(source, source ^ flip) for source in range(co...  39.9 us
    unnamed x155, local copies, waits for them, and re-layouts  35.8 us
    pallas_call x1, Pallas kernels, attn_bwd(): pl.pallas_call(functools.partial(bwd_kernel, scale=scale, chunk=chunk), g...  27.9 us
  transfers between devices with their start and end apart: 58, of which 37 were waited for; matrix products, arithmetic and copies ran while one was open for 35% of the time, Pallas kernels for 8%

profile of v4, /device:TPU:0, one launch (start us, length us, event | category | flops | bytes accessed | tf_op | source)
XLA Modules:
  0.0 650.1 jit_solution(16287191694539951572)
XLA Ops:
  25.1 73.3 %all-gather.4.cloned.1.call-done = bf16[2048,2048]{0,1:T(8,128)(2,1)} async-done(((bf16[256,2048]{0,1:T(8,128)(2,1)}), bf16[2048,2048]{0,1:T(8,128)(2,1)}) %all-gather.4.cloned.1.call-update) | async-done | bytes 8388624 | tf_op jit(solution)/shard_map/all_gather | solution.py:387
  98.4 10.1 %add_convert_fusion.3.q_ref.ko_ref.vo_ref = bf16[1024,1536]{1,0:T(8,128)(2,1)S(1)} fusion(bf16[1024,2048]{1,0:T(8,128)(2,1)} %copy-done.18, bf16[2048,2048]{0,1:T(8,128)(2,1)} %all-gather.4.cloned.1.call-done, f32[1536]{0:T(1024)S(1)} %pad_maximum_fusion.23), kind=kOutput, calls=%fused_computation.21 | convolution fusion | flops 6445596672 | bytes 13637632 | tf_op jit(solution)/shard_map/dot_general | solution.py:27
  116.2 21.1 %attention_forward.1 = (bf16[1024,512]{1,0:T(8,128)(2,1)S(1)}, f32[4,1,1024]{2,1,0:T(1,128)S(1)}) custom-call(bf16[1024,1536]{1,0:T(8,128)(2,1)} %copy-done.17, bf16[1024,1536]{1,0:T(8,128)(2,1)} %copy-done.17, bf16[1024,1024]{1,0:T(8,128)(2,1)S(1)} %collective-permute-done.1.kf_ref.vf_ref, bf16[1024,1536]{1,0:T(8,128)(2,1)} %copy-done.17, ...), custom_call_target="tpu_custom_call" | custom-call | flops 12884901888 | bytes 6291456 | tf_op jit(solution)/shard_map/attention_forward/pallas_call | solution.py:223
  147.9 6.4 collective-permute-done.2
  160.4 19.6 %collective-permute-done.5.two = bf16[256,2048]{1,0:T(8,128)(2,1)S(1)} collective-permute-done((bf16[256,2048]{1,0:T(8,128)(2,1)S(1)}, bf16[256,2048]{1,0:T(8,128)(2,1)S(1)}, u32[]{:S(2)}, u32[]{:S(2)}) %collective-permute-start.5) | collective-permute-done | bytes 1048608 | tf_op jit(solution)/shard_map/ppermute | solution.py:40
  184.2 21.9 %collective-permute-done.7 = bf16[256,2048]{1,0:T(8,128)(2,1)S(1)} collective-permute-done((bf16[256,2048]{1,0:T(8,128)(2,1)S(1)}, bf16[256,2048]{1,0:T(8,128)(2,1)S(1)}, u32[]{:S(2)}, u32[]{:S(2)}) %collective-permute-start.7) | collective-permute-done | bytes 1048608 | tf_op jit(solution)/shard_map/ppermute | solution.py:40
  211.1 6.7 %collective-permute-done.8 = bf16[128,2048]{1,0:T(8,128)(2,1)S(1)} collective-permute-done((bf16[128,2048]{1,0:T(8,128)(2,1)S(1)}, bf16[128,2048]{1,0:T(8,128)(2,1)S(1)}, u32[]{:S(2)}, u32[]{:S(2)}) %collective-permute-start.8) | collective-permute-done | bytes 524320 | tf_op jit(solution)/shard_map/ppermute | solution.py:40
  219.9 19.0 %fusion.7 = (bf16[1024,2048]{1,0:T(8,128)(2,1)}, bf16[1024,2048]{1,0:T(8,128)(2,1)S(1)}) fusion(f32[2048]{0:T(1024)S(1)} %copy-done.61, bf16[1024,2048]{1,0:T(8,128)(2,1)} %constant_dynamic-update-slice_fusion, bf16[2048,2048]{0,1:T(8,128)(2,1)} %all-gather.6.cloned.1.call-done), kind=kOutput, calls=%fused_computation.10 | convolution fusion | flops 8636071936 | bytes 20979712 | tf_op jit(solution)/shard_map/dot_general | solution.py:31
  255.1 9.0 %all-gather.8.cloned.1.call-done = bf16[2048,2048]{1,0:T(8,128)(2,1)} async-done(((bf16[2048,256]{1,0:T(8,128)(2,1)}), bf16[2048,2048]{1,0:T(8,128)(2,1)}) %all-gather.8.cloned.1.call-update) | async-done | bytes 8388624 | tf_op jit(solution)/shard_map/all_gather | solution.py:390
  264.1 6.2 convolution_convert_fusion.1
  292.8 17.6 %collective-permute-done.16.two = bf16[256,2048]{1,0:T(8,128)(2,1)S(1)} collective-permute-done((bf16[256,2048]{1,0:T(8,128)(2,1)S(1)}, bf16[256,2048]{1,0:T(8,128)(2,1)S(1)}, u32[]{:S(2)}, u32[]{:S(2)}) %collective-permute-start.16) | collective-permute-done | bytes 1048608 | tf_op jit(solution)/shard_map/ppermute | solution.py:40
  318.1 7.1 %multiply_convert_fusion.1 = bf16[256,2048]{1,0:T(8,128)(2,1)} fusion(bf16[1024,2048]{1,0:T(8,128)(2,1)} %get-tuple-element.114, bf16[256,2048]{1,0:T(8,128)(2,1)S(1)} %get-tuple-element.113, bf16[2048,2048]{1,0:T(8,128)(2,1)} %all-gather.8.cloned.1.call-done), kind=kOutput, calls=%fused_computation.65 | convolution fusion | flops 2149056512 | bytes 11534336 | tf_op jit(solution)/shard_map/dot_general | solution.py:31
  325.2 14.7 %collective-permute-done.17 = bf16[256,2048]{1,0:T(8,128)(2,1)S(1)} collective-permute-done((bf16[256,2048]{1,0:T(8,128)(2,1)S(1)}, bf16[256,2048]{1,0:T(8,128)(2,1)S(1)}, u32[]{:S(2)}, u32[]{:S(2)}) %collective-permute-start.17) | collective-permute-done | bytes 1048608 | tf_op jit(solution)/shard_map/ppermute | solution.py:40
  366.1 11.2 %multiply_convert_fusion = bf16[768,2048]{1,0:T(8,128)(2,1)S(1)} fusion(bf16[2048,2048]{1,0:T(8,128)(2,1)} %all-gather.8.cloned.1.call-done, bf16[256,2048]{1,0:T(8,128)(2,1)} %copy-done.27, bf16[256,2048]{1,0:T(8,128)(2,1)} %copy-done.26, bf16[256,2048]{1,0:T(8,128)(2,1)} %copy-done.25, bf16[1024,2048]{1,0:T(8,128)(2,1)} %get-tuple-element.114), kind=kOutput, calls=%fused_computation.20 | convolution fusion | flops 6456606720 | bytes 17825792 | tf_op jit(solution)/shard_map/dot_general | solution.py:31
  377.9 6.2 fusion.57
  403.5 7.1 %fusion.118.h = f32[256,2048]{1,0:T(8,128)} fusion(bf16[256,2048]{1,0:T(8,128)(2,1)S(1)} %copy-done.23, bf16[2048,2048]{0,1:T(8,128)(2,1)} %all-gather.6.cloned.1.call-done), kind=kOutput, calls=%fused_computation.275 | convolution fusion | flops 2147483648 | bytes 11534336 | tf_op jit(solution)/shard_map/dot_general | solution.py:27
  410.7 7.0 %fusion.119 = f32[1024,2048]{1,0:T(8,128)} fusion(bf16[1024,1024]{1,0:T(8,128)(2,1)S(1)} %copy-done.55, bf16[1024,2048]{1,0:T(8,128)(2,1)S(1)} %collective-permute-done.29), kind=kOutput, calls=%fused_computation.276 | convolution fusion | flops 4294967296 | bytes 14680064 | tf_op jit(solution)/shard_map/dot_general | solution.py:35
  417.7 9.1 %add_convert_fusion = bf16[1024,2048]{1,0:T(8,128)(2,1)} fusion(f32[1024,2048]{1,0:T(8,128)} %fusion.119, bf16[1024,2048]{1,0:T(8,128)(2,1)S(1)} %pad_maximum_fusion.1, bf16[1024,256]{1,0:T(8,128)(2,1)S(1)} %copy-done.42, bf16[1024,256]{1,0:T(8,128)(2,1)S(1)} %copy-done.41, bf16[1024,256]{1,0:T(8,128)(2,1)S(1)} %copy-done.40, ...), kind=kOutput, calls=%fused_computation.14 | convolution fusion | flops 4307550208 | bytes 18874368 | tf_op jit(solution)/shard_map/dot_general | solution.py:35
  444.7 19.8 %collective-permute-done.33 = bf16[256,2048]{1,0:T(8,128)(2,1)S(1)} collective-permute-done((bf16[256,2048]{1,0:T(8,128)(2,1)}, bf16[256,2048]{1,0:T(8,128)(2,1)S(1)}, u32[]{:S(2)}, u32[]{:S(2)}) %collective-permute-start.33) | collective-permute-done | bytes 1048608 | tf_op jit(solution)/shard_map/ppermute | solution.py:40
  468.2 8.4 %collective-permute-done.34 = bf16[128,2048]{1,0:T(8,128)(2,1)S(1)} collective-permute-done((bf16[128,2048]{1,0:T(8,128)(2,1)S(1)}, bf16[128,2048]{1,0:T(8,128)(2,1)S(1)}, u32[]{:S(2)}, u32[]{:S(2)}) %collective-permute-start.34) | collective-permute-done | bytes 524320 | tf_op jit(solution)/shard_map/ppermute | solution.py:40
  481.8 27.9 %attention_backward.1 = (bf16[1024,512]{1,0:T(8,128)(2,1)S(1)}, f32[1024,512]{1,0:T(8,128)}, f32[1024,512]{1,0:T(8,128)}, bf16[2,1024,512]{2,1,0:T(8,128)(2,1)}) custom-call(bf16[1024,1536]{1,0:T(8,128)(2,1)} %copy-done.17, bf16[1024,512]{1,0:T(8,128)(2,1)S(1)} %convolution_convert_fusion.2.do_ref, bf16[1024,512]{1,0:T(8,128)(2,1)S(1)} %copy-done.2, ...), custom_call_target="tpu_custom_call" | custom-call | flops 4096 | bytes 1048576 | tf_op jit(solution)/shard_map/attention_backward/pallas_call | solution.py:274
  537.5 6.2 add_convert_fusion.2
  575.2 6.7 %collective-permute-done.45 = f32[15872]{0:T(1024)S(1)} collective-permute-done((f32[15872]{0:T(1024)S(1)}, f32[15872]{0:T(1024)S(1)}, u32[]{:S(2)}, u32[]{:S(2)}) %collective-permute-start.45) | collective-permute-done | bytes 63520 | tf_op jit(solution)/shard_map/ppermute | solution.py:40
  595.1 19.7 %collective-permute-done.47 = bf16[256,2048]{1,0:T(8,128)(2,1)S(1)} collective-permute-done((bf16[256,2048]{1,0:T(8,128)(2,1)}, bf16[256,2048]{1,0:T(8,128)(2,1)S(1)}, u32[]{:S(2)}, u32[]{:S(2)}) %collective-permute-start.47) | collective-permute-done | bytes 1048608 | tf_op jit(solution)/shard_map/ppermute | solution.py:40
  (394 shorter events, 272.0 us)
Async XLA Ops:
  7.2 91.2 %all-gather.4.cloned.1.call-start = ((), (), s32[]{:S(2)}) async-start(), calls=%async_computation.3 | async-start | bytes 9437184 | tf_op jit(solution)/shard_map/all_gather | solution.py:387
  13.1 206.9 %all-gather.6.cloned.1.call-start = ((), (), s32[]{:S(2)}) async-start(), calls=%async_computation.4 | async-start | bytes 9437184 | tf_op jit(solution)/shard_map/all_gather | solution.py:389
  14.3 249.8 %all-gather.8.cloned.1.call-start = ((), (), s32[]{:S(2)}) async-start(), calls=%async_computation.5 | async-start | bytes 9437184 | tf_op jit(solution)/shard_map/all_gather | solution.py:390
  113.6 330.3 %reduce-scatter.4.cloned.1.call-start = ((), (), s32[]{:S(2)}) async-start(), calls=%async_computation.6 | async-start | bytes 5242880 | tf_op jit(solution)/shard_map/reduce_scatter | solution.py:377
  155.7 24.4 %collective-permute-start.5 = (bf16[256,2048]{1,0:T(8,128)(2,1)S(1)}, bf16[256,2048]{1,0:T(8,128)(2,1)S(1)}, u32[]{:S(2)}, u32[]{:S(2)}) collective-permute-start(bf16[256,2048]{1,0:T(8,128)(2,1)S(1)} %pad_maximum_fusion.13), channel_id=1, source_target_pairs={{0,2},{1,3},{2,0},{3,1},{4,6},{5,7},{6,4},{7,5},{8,10},{9,11},{10,... | collective-permute-start | bytes 3145736 | tf_op jit(solution)/shard_map/ppermute | solution.py:40
  157.4 24.1 %collective-permute-start.4 = (bf16[256,2048]{1,0:T(8,128)(2,1)S(1)}, bf16[256,2048]{1,0:T(8,128)(2,1)S(1)}, u32[]{:S(2)}, u32[]{:S(2)}) collective-permute-start(bf16[256,2048]{1,0:T(8,128)(2,1)S(1)} %pad_maximum_fusion.12), channel_id=1, source_target_pairs={{0,1},{1,0},{2,3},{3,2},{4,5},{5,4},{6,7},{7,6},{8,9},{9,8},{10,11... | collective-permute-start | bytes 3145736 | tf_op jit(solution)/shard_map/ppermute | solution.py:40
  183.0 23.2 %collective-permute-start.7 = (bf16[256,2048]{1,0:T(8,128)(2,1)S(1)}, bf16[256,2048]{1,0:T(8,128)(2,1)S(1)}, u32[]{:S(2)}, u32[]{:S(2)}) collective-permute-start(bf16[256,2048]{1,0:T(8,128)(2,1)S(1)} %get-tuple-element.102), channel_id=1, source_target_pairs={{0,2},{1,3},{2,0},{3,1},{4,6},{5,7},{6,4},{7,5},{8,10},{9,11},{10,... | collective-permute-start | bytes 3145736 | tf_op jit(solution)/shard_map/ppermute | solution.py:40
  183.6 24.4 %collective-permute-start.6 = (bf16[256,2048]{1,0:T(8,128)(2,1)S(1)}, bf16[256,2048]{1,0:T(8,128)(2,1)S(1)}, u32[]{:S(2)}, u32[]{:S(2)}) collective-permute-start(bf16[256,2048]{1,0:T(8,128)(2,1)S(1)} %get-tuple-element.102), channel_id=1, source_target_pairs={{0,1},{1,0},{2,3},{3,2},{4,5},{5,4},{6,7},{7,6},{8,9},{9,8},{10,11... | collective-permute-start | bytes 3145736 | tf_op jit(solution)/shard_map/ppermute | solution.py:40
  286.1 24.3 %collective-permute-start.16 = (bf16[256,2048]{1,0:T(8,128)(2,1)S(1)}, bf16[256,2048]{1,0:T(8,128)(2,1)S(1)}, u32[]{:S(2)}, u32[]{:S(2)}) collective-permute-start(bf16[256,2048]{1,0:T(8,128)(2,1)S(1)} %pad_maximum_fusion.15), channel_id=1, source_target_pairs={{0,2},{1,3},{2,0},{3,1},{4,6},{5,7},{6,4},{7,5},{8,10},{9,11},{10,... | collective-permute-start | bytes 3145736 | tf_op jit(solution)/shard_map/ppermute | solution.py:40
  287.7 24.0 %collective-permute-start.15 = (bf16[256,2048]{1,0:T(8,128)(2,1)S(1)}, bf16[256,2048]{1,0:T(8,128)(2,1)S(1)}, u32[]{:S(2)}, u32[]{:S(2)}) collective-permute-start(bf16[256,2048]{1,0:T(8,128)(2,1)S(1)} %pad_maximum_fusion.14), channel_id=1, source_target_pairs={{0,1},{1,0},{2,3},{3,2},{4,5},{5,4},{6,7},{7,6},{8,9},{9,8},{10,11... | collective-permute-start | bytes 3145736 | tf_op jit(solution)/shard_map/ppermute | solution.py:40
  356.9 27.3 %collective-permute-start.23 = (bf16[256,2048]{1,0:T(8,128)(2,1)}, bf16[256,2048]{1,0:T(8,128)(2,1)}, u32[]{:S(2)}, u32[]{:S(2)}) collective-permute-start(bf16[256,2048]{1,0:T(8,128)(2,1)} %get-tuple-element.162), channel_id=1, source_target_pairs={{0,1},{1,0},{2,3},{3,2},{4,5},{5,4},{6,7},{7,6},{8,9},{9,8},{10,11... | collective-permute-start | bytes 3145736 | tf_op jit(solution)/shard_map/ppermute | solution.py:40
  358.1 26.0 %collective-permute-start.24 = (bf16[256,2048]{1,0:T(8,128)(2,1)}, bf16[256,2048]{1,0:T(8,128)(2,1)}, u32[]{:S(2)}, u32[]{:S(2)}) collective-permute-start(bf16[256,2048]{1,0:T(8,128)(2,1)} %get-tuple-element.162), channel_id=1, source_target_pairs={{0,2},{1,3},{2,0},{3,1},{4,6},{5,7},{6,4},{7,5},{8,10},{9,11},{10,... | collective-permute-start | bytes 3145736 | tf_op jit(solution)/shard_map/ppermute | solution.py:40
  366.0 165.3 %reduce-scatter.6.cloned.1.call-start = ((), (), s32[]{:S(2)}) async-start(), calls=%async_computation.7 | async-start | bytes 5242880 | tf_op jit(solution)/shard_map/reduce_scatter | solution.py:377
  377.9 32.8 %collective-permute-start.29 = (bf16[1024,2048]{1,0:T(8,128)(2,1)S(1)}, bf16[1024,2048]{1,0:T(8,128)(2,1)S(1)}, u32[]{:S(2)}, u32[]{:S(2)}) collective-permute-start(bf16[1024,2048]{1,0:T(8,128)(2,1)S(1)} %pad_maximum_fusion.1), channel_id=1, source_target_pairs={{0,4},{4,0},{8,12},{12,8},{16,20},{20,16},{24,28},{28,24},{1,5},{5... | collective-permute-start | bytes 12582920 | tf_op jit(solution)/shard_map/ppermute | solution.py:40
  400.2 26.7 %collective-permute-start.28 = (bf16[256,2048]{1,0:T(8,128)(2,1)}, bf16[256,2048]{1,0:T(8,128)(2,1)}, u32[]{:S(2)}, u32[]{:S(2)}) collective-permute-start(bf16[256,2048]{1,0:T(8,128)(2,1)} %pad_maximum_fusion.17), channel_id=1, source_target_pairs={{0,2},{1,3},{2,0},{3,1},{4,6},{5,7},{6,4},{7,5},{8,10},{9,11},{10,... | collective-permute-start | bytes 3145736 | tf_op jit(solution)/shard_map/ppermute | solution.py:40
  402.4 24.4 %collective-permute-start.27 = (bf16[256,2048]{1,0:T(8,128)(2,1)}, bf16[256,2048]{1,0:T(8,128)(2,1)}, u32[]{:S(2)}, u32[]{:S(2)}) collective-permute-start(bf16[256,2048]{1,0:T(8,128)(2,1)} %pad_maximum_fusion.16), channel_id=1, source_target_pairs={{0,1},{1,0},{2,3},{3,2},{4,5},{5,4},{6,7},{7,6},{8,9},{9,8},{10,11... | collective-permute-start | bytes 3145736 | tf_op jit(solution)/shard_map/ppermute | solution.py:40
  443.0 24.2 %collective-permute-start.32 = (bf16[256,2048]{1,0:T(8,128)(2,1)}, bf16[256,2048]{1,0:T(8,128)(2,1)S(1)}, u32[]{:S(2)}, u32[]{:S(2)}) collective-permute-start(bf16[256,2048]{1,0:T(8,128)(2,1)} %get-tuple-element.138), channel_id=1, source_target_pairs={{0,1},{1,0},{2,3},{3,2},{4,5},{5,4},{6,7},{7,6},{8,9},{9,8},{10,11... | collective-permute-start | bytes 3145736 | tf_op jit(solution)/shard_map/ppermute | solution.py:40
  444.0 195.1 %reduce-scatter.8.cloned.1.call-start = ((), (), s32[]{:S(2)}) async-start(), calls=%async_computation.8 | async-start | bytes 5242880 | tf_op jit(solution)/shard_map/reduce_scatter | solution.py:377
  529.3 30.0 %collective-permute-start.39 = (bf16[128,2048]{1,0:T(8,128)(2,1)}, bf16[128,2048]{1,0:T(8,128)(2,1)}, u32[]{:S(2)}, u32[]{:S(2)}) collective-permute-start(bf16[128,2048]{1,0:T(8,128)(2,1)} %get-tuple-element.259), channel_id=1, source_target_pairs={{0,1},{1,0},{2,3},{3,2},{4,5},{5,4},{6,7},{7,6},{8,9},{9,8},{10,11... | collective-permute-start | bytes 1572872 | tf_op jit(solution)/shard_map/ppermute | solution.py:40
  530.0 29.3 %collective-permute-start.40 = (bf16[128,2048]{1,0:T(8,128)(2,1)}, bf16[128,2048]{1,0:T(8,128)(2,1)}, u32[]{:S(2)}, u32[]{:S(2)}) collective-permute-start(bf16[128,2048]{1,0:T(8,128)(2,1)} %get-tuple-element.258), channel_id=1, source_target_pairs={{0,2},{1,3},{2,0},{3,1},{4,6},{5,7},{6,4},{7,5},{8,10},{9,11},{10,... | collective-permute-start | bytes 1572872 | tf_op jit(solution)/shard_map/ppermute | solution.py:40
  562.0 25.6 %collective-permute-start.42 = (bf16[256,2048]{1,0:T(8,128)(2,1)S(1)}, bf16[256,2048]{1,0:T(8,128)(2,1)S(1)}, u32[]{:S(2)}, u32[]{:S(2)}) collective-permute-start(bf16[256,2048]{1,0:T(8,128)(2,1)S(1)} %pad_maximum_fusion.19), channel_id=1, source_target_pairs={{0,2},{1,3},{2,0},{3,1},{4,6},{5,7},{6,4},{7,5},{8,10},{9,11},{10,... | collective-permute-start | bytes 3145736 | tf_op jit(solution)/shard_map/ppermute | solution.py:40
  563.0 25.2 %collective-permute-start.41 = (bf16[256,2048]{1,0:T(8,128)(2,1)S(1)}, bf16[256,2048]{1,0:T(8,128)(2,1)S(1)}, u32[]{:S(2)}, u32[]{:S(2)}) collective-permute-start(bf16[256,2048]{1,0:T(8,128)(2,1)S(1)} %pad_maximum_fusion.18), channel_id=1, source_target_pairs={{0,1},{1,0},{2,3},{3,2},{4,5},{5,4},{6,7},{7,6},{8,9},{9,8},{10,11... | collective-permute-start | bytes 3145736 | tf_op jit(solution)/shard_map/ppermute | solution.py:40
  590.2 24.7 %collective-permute-start.47 = (bf16[256,2048]{1,0:T(8,128)(2,1)}, bf16[256,2048]{1,0:T(8,128)(2,1)S(1)}, u32[]{:S(2)}, u32[]{:S(2)}) collective-permute-start(bf16[256,2048]{1,0:T(8,128)(2,1)} %get-tuple-element.204), channel_id=1, source_target_pairs={{0,2},{1,3},{2,0},{3,1},{4,6},{5,7},{6,4},{7,5},{8,10},{9,11},{10,... | collective-permute-start | bytes 3145736 | tf_op jit(solution)/shard_map/ppermute | solution.py:40
  591.2 25.2 %collective-permute-start.46 = (bf16[256,2048]{1,0:T(8,128)(2,1)}, bf16[256,2048]{1,0:T(8,128)(2,1)}, u32[]{:S(2)}, u32[]{:S(2)}) collective-permute-start(bf16[256,2048]{1,0:T(8,128)(2,1)} %get-tuple-element.204), channel_id=1, source_target_pairs={{0,1},{1,0},{2,3},{3,2},{4,5},{5,4},{6,7},{7,6},{8,9},{9,8},{10,11... | collective-permute-start | bytes 3145736 | tf_op jit(solution)/shard_map/ppermute | solution.py:40
  (100 other events, 918.0 us)
Sparse Core Ops, SparseCore 0:
  13.2 85.1 all-gather.3
  100.6 80.2 all-gather.5
  183.0 81.0 all-gather.7
  366.1 74.2 reduce-scatter.3
  444.1 76.3 reduce-scatter.5
  549.4 77.2 reduce-scatter.7

commit v5 on v4

--- a/solution.py
+++ b/solution.py
@@ -82,7 +82,7 @@
     flip = count // 2
     extra = None
     while flip >= 4:
-        away = jnp.concatenate([part(k, None) for k in range(flip, 2 * flip)])
+        away = part(flip, 2 * flip, None)
         split = away.shape[0]
         if extra is not None:
             away = away + extra[split:].astype(F32)
@@ -90,23 +90,23 @@
         extra = come if extra is None else extra[:split].astype(F32) + come.astype(F32)
         flip //= 2
 
-    def piece(k, gate=None):
-        value = part(k, gate)
+    def piece(first, last, gate=None):
+        value = part(first, last, gate)
         if extra is not None:
-            block = value.shape[0]
-            value = value + extra[k * block : (k + 1) * block].astype(F32)
+            block = extra.shape[0] // 4
+            value = value + extra[first * block : last * block].astype(F32)
         return value
 
-    three = piece(3).astype(LOW)
+    three = piece(3, 4).astype(LOW)
     half = three.shape[0] // 2
     come_top, come_low = swap(three[:half], "tensor", 1), swap(three[half:], "tensor", 2)
     first = [make(three) for make in after_first]
-    one, two = piece(1, (three, *first)), piece(2, (three, *first))
+    one, two = jnp.split(piece(1, 3, (three, *first)), 2)
     come_top, come_low = after((come_top, come_low), *first)
     one = jnp.concatenate([one[:half].astype(LOW), (one[half:] + come_low.astype(F32)).astype(LOW)])
     two = jnp.concatenate([(two[:half] + come_top.astype(F32)).astype(LOW), two[half:].astype(LOW)])
     from_one, from_two = swap(one, "tensor", 1), swap(two, "tensor", 2)
-    here = piece(0, (one, two))
+    here = piece(0, 1, (one, two))
     second = [make((one, two)) for make in after_second]
     from_one, from_two = after((from_one, from_two), here, *jax.tree.leaves(second))
     return (here, from_one, from_two), first, second
@@ -378,8 +378,8 @@
             grad, "dp", scatter_dimension=0, tiled=True, axis_index_groups=core_groups
         )
 
-    def rows_of(value, k):
-        return value[k * block : (k + 1) * block]
+    def rows_of(value, first, last):
+        return value[first * block : last * block]
 
     low_attn = jnp.concatenate([w_query, w_key, w_value, w_out.T], axis=1).astype(LOW)
     low_inner = w_inner.T.astype(LOW)
@@ -395,7 +395,7 @@
     far_kv = swap(qkv[:, width_here:], "dp", 1)
     mixed, lse = attn_fwd(qkv, far_kv, own_bias[None], far_bias[None], heads_here)
 
-    attn_parts, _, _ = scatter_rows(lambda k, gate: mat_bf(rows_of(gated(mixed, gate), k), full_out))
+    attn_parts, _, _ = scatter_rows(lambda a, b, gate: mat_bf(rows_of(gated(mixed, gate), a, b), full_out))
     resid_one, hidden, hidden_here = on_rows(
         norm_one_kernel,
         "norm_one",
@@ -412,7 +412,7 @@
     act_far = swap(act_low, "dp", 1)
     act_low, act_slope = after((act_low, act_slope), mixed_far, act_far, hidden_pair)
 
-    outer_parts, _, _ = scatter_rows(lambda k, gate: mat_bf(rows_of(gated(act_low, gate), k), full_outer))
+    outer_parts, _, _ = scatter_rows(lambda a, b, gate: mat_bf(rows_of(gated(act_low, gate), a, b), full_outer))
     grad_two, outer_here, output, sums_two = on_rows(
         norm_two_kernel,
         "norm_two",
@@ -454,14 +454,15 @@
     inner_far = swap(inner_low, "dp", 1)
 
     inner_three, output_near = lax.optimization_barrier(
-        (mat_bf(rows_of(inner_away, 2), full_inner), output_near)
-    )
-
-    def inner_part(k, gate):
-        if k == 3:
+        (mat_bf(rows_of(inner_away, 2, 3), full_inner), output_near)
+    )
+
+    def inner_part(first, last, gate):
+        if first == 3:
             return inner_three
-        rows = inner_here if k == 0 else inner_away
-        return mat_bf(rows_of(gated(rows, gate), max(k - 1, 0)), full_inner)
+        if first == 0:
+            return mat_bf(gated(inner_here, gate), full_inner)
+        return mat_bf(rows_of(gated(inner_away, gate), first - 1, last - 1), full_inner)
 
     def inner_weight(sent):
         mine, far = after((inner_low, inner_far), sent)
@@ -507,7 +508,7 @@
         return outer.T.astype(F32), inner.astype(F32)
 
     (here, one, two), (grad_w_attn,), (sums, (grad_w_outer, grad_w_inner)) = scatter_rows(
-        lambda k, gate: mat_last(rows_of(gated(qkv_low, gate), k), full_qkv),
+        lambda a, b, gate: mat_last(rows_of(gated(qkv_low, gate), a, b), full_qkv),
         after_first=[attn_weight],
         after_second=[total_sums, owned],
     )

time: 656 us -> 650 us (level)
  matrix products: 167 us -> 156 us
    dot_general x13 -> x10, matrix products: 58 us -> 51.5 us  [mat_bf(): return jnp.dot(left, right, preferred_element_type=F32)]
    dot_general x8 -> x7, matrix products: 59 us -> 56.8 us  [mat_last(): return lax.dot_general(left, right, BOTH_LAST, preferred_element_type=F32)]
    unnamed x155 -> x151, local copies, waits for them, and re-layouts: 35.8 us -> 35.6 us
  transfers between devices with their start and end apart: 58 -> 58, of which waited for: 37 -> 38; matrix products, arithmetic and copies ran while one was open for 35% -> 34% of each run, Pallas kernels for 8% -> 9%
where the time goes in v5:
time: 650 us; the launch traced here: 644 us
  waiting for transfers between devices  276 us (42%)
  matrix products  156 us (24%)
  Pallas kernels  59.5 us (9%)
  local copies, waits for them, and re-layouts  52.2 us (8%)
  other arithmetic  44.1 us (7%)
  starting transfers between devices  41 us (6%)
  between operations  15.9 us (2%)
    ppermute x52, waiting for transfers between devices, swap(): lax.ppermute(value, axis, [(source, source ^ flip) for source in range(co...  193 us
    all_gather x1, waiting for transfers between devices, on_device(): full_attn = lax.all_gather(low_attn, 'dp', axis=0, tiled=True)  73.3 us
    dot_general x7, matrix products, mat_last(): return lax.dot_general(left, right, BOTH_LAST, preferred_element_type=F32)  56.8 us
    dot_general x10, matrix products, mat_bf(): return jnp.dot(left, right, preferred_element_type=F32)  51.5 us
    dot_general x10, matrix products, mat_first(): return lax.dot_general(left, right, BOTH_FIRST, preferred_element_type=F32)  47.6 us
    ppermute x52, starting transfers between devices, swap(): lax.ppermute(value, axis, [(source, source ^ flip) for source in range(co...  40.6 us
    unnamed x151, local copies, waits for them, and re-layouts  35.6 us
    pallas_call x1, Pallas kernels, attn_bwd(): pl.pallas_call(functools.partial(bwd_kernel, scale=scale, chunk=chunk), g...  28.3 us
  transfers between devices with their start and end apart: 58, of which 38 were waited for; matrix products, arithmetic and copies ran while one was open for 34% of the time, Pallas kernels for 9%

profile of v5, /device:TPU:0, one launch (start us, length us, event | category | flops | bytes accessed | tf_op | source)
XLA Modules:
  0.0 644.4 jit_solution(9282596592480771560)
XLA Ops:
  25.1 73.3 %all-gather.4.cloned.1.call-done = bf16[2048,2048]{0,1:T(8,128)(2,1)} async-done(((bf16[256,2048]{0,1:T(8,128)(2,1)}), bf16[2048,2048]{0,1:T(8,128)(2,1)}) %all-gather.4.cloned.1.call-update) | async-done | bytes 8388624 | tf_op jit(solution)/shard_map/all_gather | solution.py:387
  98.4 10.1 %add_convert_fusion.3.q_ref.ko_ref.vo_ref = bf16[1024,1536]{1,0:T(8,128)(2,1)S(1)} fusion(bf16[1024,2048]{1,0:T(8,128)(2,1)} %copy-done.18, bf16[2048,2048]{0,1:T(8,128)(2,1)} %all-gather.4.cloned.1.call-done, f32[1536]{0:T(1024)S(1)} %pad_maximum_fusion.23), kind=kOutput, calls=%fused_computation.21 | convolution fusion | flops 6445596672 | bytes 13637632 | tf_op jit(solution)/shard_map/dot_general | solution.py:27
  116.2 21.1 %attention_forward.1 = (bf16[1024,512]{1,0:T(8,128)(2,1)S(1)}, f32[4,1,1024]{2,1,0:T(1,128)S(1)}) custom-call(bf16[1024,1536]{1,0:T(8,128)(2,1)} %copy-done.17, bf16[1024,1536]{1,0:T(8,128)(2,1)} %copy-done.17, bf16[1024,1024]{1,0:T(8,128)(2,1)S(1)} %collective-permute-done.1.kf_ref.vf_ref, bf16[1024,1536]{1,0:T(8,128)(2,1)} %copy-done.17, ...), custom_call_target="tpu_custom_call" | custom-call | flops 12884901888 | bytes 6291456 | tf_op jit(solution)/shard_map/attention_forward/pallas_call | solution.py:223
  146.1 8.2 %collective-permute-done.2 = bf16[128,2048]{1,0:T(8,128)(2,1)S(1)} collective-permute-done((bf16[128,2048]{1,0:T(8,128)(2,1)S(1)}, bf16[128,2048]{1,0:T(8,128)(2,1)S(1)}, u32[]{:S(2)}, u32[]{:S(2)}) %collective-permute-start.2) | collective-permute-done | bytes 524320 | tf_op jit(solution)/shard_map/ppermute | solution.py:40
  160.5 19.7 %collective-permute-done.5.two = bf16[256,2048]{1,0:T(8,128)(2,1)S(1)} collective-permute-done((bf16[256,2048]{1,0:T(8,128)(2,1)S(1)}, bf16[256,2048]{1,0:T(8,128)(2,1)S(1)}, u32[]{:S(2)}, u32[]{:S(2)}) %collective-permute-start.5) | collective-permute-done | bytes 1048608 | tf_op jit(solution)/shard_map/ppermute | solution.py:40
  184.3 21.9 %collective-permute-done.7 = bf16[256,2048]{1,0:T(8,128)(2,1)S(1)} collective-permute-done((bf16[256,2048]{1,0:T(8,128)(2,1)S(1)}, bf16[256,2048]{1,0:T(8,128)(2,1)S(1)}, u32[]{:S(2)}, u32[]{:S(2)}) %collective-permute-start.7) | collective-permute-done | bytes 1048608 | tf_op jit(solution)/shard_map/ppermute | solution.py:40
  211.1 6.7 %collective-permute-done.8 = bf16[128,2048]{1,0:T(8,128)(2,1)S(1)} collective-permute-done((bf16[128,2048]{1,0:T(8,128)(2,1)S(1)}, bf16[128,2048]{1,0:T(8,128)(2,1)S(1)}, u32[]{:S(2)}, u32[]{:S(2)}) %collective-permute-start.8) | collective-permute-done | bytes 524320 | tf_op jit(solution)/shard_map/ppermute | solution.py:40
  220.0 18.9 %fusion.7 = (bf16[1024,2048]{1,0:T(8,128)(2,1)}, bf16[1024,2048]{1,0:T(8,128)(2,1)S(1)}) fusion(f32[2048]{0:T(1024)S(1)} %copy-done.61, bf16[1024,2048]{1,0:T(8,128)(2,1)} %constant_dynamic-update-slice_fusion, bf16[2048,2048]{0,1:T(8,128)(2,1)} %all-gather.6.cloned.1.call-done), kind=kOutput, calls=%fused_computation.10 | convolution fusion | flops 8636071936 | bytes 20979712 | tf_op jit(solution)/shard_map/dot_general | solution.py:31
  255.1 9.0 %all-gather.8.cloned.1.call-done = bf16[2048,2048]{1,0:T(8,128)(2,1)} async-done(((bf16[2048,256]{1,0:T(8,128)(2,1)}), bf16[2048,2048]{1,0:T(8,128)(2,1)}) %all-gather.8.cloned.1.call-update) | async-done | bytes 8388624 | tf_op jit(solution)/shard_map/all_gather | solution.py:390
  278.1 6.5 %collective-permute-done.13 = bf16[128,2048]{1,0:T(8,128)(2,1)S(1)} collective-permute-done((bf16[128,2048]{1,0:T(8,128)(2,1)S(1)}, bf16[128,2048]{1,0:T(8,128)(2,1)S(1)}, u32[]{:S(2)}, u32[]{:S(2)}) %collective-permute-start.13) | collective-permute-done | bytes 524320 | tf_op jit(solution)/shard_map/ppermute | solution.py:40
  292.8 17.6 %collective-permute-done.16.two = bf16[256,2048]{1,0:T(8,128)(2,1)S(1)} collective-permute-done((bf16[256,2048]{1,0:T(8,128)(2,1)S(1)}, bf16[256,2048]{1,0:T(8,128)(2,1)S(1)}, u32[]{:S(2)}, u32[]{:S(2)}) %collective-permute-start.16) | collective-permute-done | bytes 1048608 | tf_op jit(solution)/shard_map/ppermute | solution.py:40
  318.5 7.0 %multiply_convert_fusion.1 = bf16[256,2048]{1,0:T(8,128)(2,1)} fusion(bf16[1024,2048]{1,0:T(8,128)(2,1)} %get-tuple-element.114, bf16[256,2048]{1,0:T(8,128)(2,1)S(1)} %get-tuple-element.113, bf16[2048,2048]{1,0:T(8,128)(2,1)} %all-gather.8.cloned.1.call-done), kind=kOutput, calls=%fused_computation.65 | convolution fusion | flops 2149056512 | bytes 11534336 | tf_op jit(solution)/shard_map/dot_general | solution.py:31
  325.5 14.7 %collective-permute-done.17 = bf16[256,2048]{1,0:T(8,128)(2,1)S(1)} collective-permute-done((bf16[256,2048]{1,0:T(8,128)(2,1)S(1)}, bf16[256,2048]{1,0:T(8,128)(2,1)S(1)}, u32[]{:S(2)}, u32[]{:S(2)}) %collective-permute-start.17) | collective-permute-done | bytes 1048608 | tf_op jit(solution)/shard_map/ppermute | solution.py:40
  366.4 11.2 %multiply_convert_fusion = bf16[768,2048]{1,0:T(8,128)(2,1)S(1)} fusion(bf16[2048,2048]{1,0:T(8,128)(2,1)} %all-gather.8.cloned.1.call-done, bf16[256,2048]{1,0:T(8,128)(2,1)} %copy-done.27, bf16[256,2048]{1,0:T(8,128)(2,1)} %copy-done.26, bf16[256,2048]{1,0:T(8,128)(2,1)} %copy-done.25, bf16[1024,2048]{1,0:T(8,128)(2,1)} %get-tuple-element.114), kind=kOutput, calls=%fused_computation.20 | convolution fusion | flops 6456606720 | bytes 17825792 | tf_op jit(solution)/shard_map/dot_general | solution.py:31
  378.3 6.2 fusion.58
  386.6 7.0 %fusion.114 = (bf16[512,2048]{1,0:T(8,128)(2,1)S(1)}, f32[512,2048]{1,0:T(8,128)S(1)}) fusion(bf16[2048,2048]{0,1:T(8,128)(2,1)} %all-gather.6.cloned.1.call-done, bf16[768,2048]{1,0:T(8,128)(2,1)S(1)} %multiply_convert_fusion), kind=kOutput, calls=%fused_computation.263 | convolution fusion | flops 4296015872 | bytes 16777216 | tf_op jit(solution)/shard_map/dot_general | solution.py:27
  403.8 7.2 %fusion.116.h = f32[256,2048]{1,0:T(8,128)} fusion(bf16[256,2048]{1,0:T(8,128)(2,1)S(1)} %copy-done.23, bf16[2048,2048]{0,1:T(8,128)(2,1)} %all-gather.6.cloned.1.call-done), kind=kOutput, calls=%fused_computation.265 | convolution fusion | flops 2147483648 | bytes 11534336 | tf_op jit(solution)/shard_map/dot_general | solution.py:27
  410.9 6.8 %fusion.117 = f32[1024,2048]{1,0:T(8,128)S(1)} fusion(bf16[1024,1024]{1,0:T(8,128)(2,1)S(1)} %copy-done.55, bf16[1024,2048]{1,0:T(8,128)(2,1)} %collective-permute-done.29), kind=kOutput, calls=%fused_computation.266 | convolution fusion | flops 4294967296 | bytes 14680064 | tf_op jit(solution)/shard_map/dot_general | solution.py:35
  417.8 6.9 %add_convert_fusion = bf16[1024,2048]{1,0:T(8,128)(2,1)} fusion(f32[1024,2048]{1,0:T(8,128)S(1)} %fusion.117, bf16[1024,2048]{1,0:T(8,128)(2,1)S(1)} %pad_maximum_fusion.1, bf16[1024,256]{1,0:T(8,128)(2,1)S(1)} %copy-done.42, bf16[1024,256]{1,0:T(8,128)(2,1)S(1)} %copy-done.41, bf16[1024,256]{1,0:T(8,128)(2,1)S(1)} %copy-done.40, ...), kind=kOutput, calls=%fused_computation.14 | convolution fusion | flops 4307550208 | bytes 18874368 | tf_op jit(solution)/shard_map/dot_general | solution.py:35
  444.5 19.4 %collective-permute-done.33 = bf16[256,2048]{1,0:T(8,128)(2,1)S(1)} collective-permute-done((bf16[256,2048]{1,0:T(8,128)(2,1)}, bf16[256,2048]{1,0:T(8,128)(2,1)S(1)}, u32[]{:S(2)}, u32[]{:S(2)}) %collective-permute-start.33) | collective-permute-done | bytes 1048608 | tf_op jit(solution)/shard_map/ppermute | solution.py:40
  467.7 7.8 %collective-permute-done.34 = bf16[128,2048]{1,0:T(8,128)(2,1)S(1)} collective-permute-done((bf16[128,2048]{1,0:T(8,128)(2,1)S(1)}, bf16[128,2048]{1,0:T(8,128)(2,1)S(1)}, u32[]{:S(2)}, u32[]{:S(2)}) %collective-permute-start.34) | collective-permute-done | bytes 524320 | tf_op jit(solution)/shard_map/ppermute | solution.py:40
  480.4 28.3 %attention_backward.1 = (bf16[1024,512]{1,0:T(8,128)(2,1)S(1)}, f32[1024,512]{1,0:T(8,128)}, f32[1024,512]{1,0:T(8,128)}, bf16[2,1024,512]{2,1,0:T(8,128)(2,1)}) custom-call(bf16[1024,1536]{1,0:T(8,128)(2,1)} %copy-done.17, bf16[1024,512]{1,0:T(8,128)(2,1)S(1)} %convolution_convert_fusion.2.do_ref, bf16[1024,512]{1,0:T(8,128)(2,1)S(1)} %copy-done.2, ...), custom_call_target="tpu_custom_call" | custom-call | flops 4096 | bytes 1048576 | tf_op jit(solution)/shard_map/attention_backward/pallas_call | solution.py:274
  569.0 6.8 %collective-permute-done.45 = f32[15872]{0:T(1024)S(1)} collective-permute-done((f32[15872]{0:T(1024)S(1)}, f32[15872]{0:T(1024)S(1)}, u32[]{:S(2)}, u32[]{:S(2)}) %collective-permute-start.45) | collective-permute-done | bytes 63520 | tf_op jit(solution)/shard_map/ppermute | solution.py:40
  589.7 19.8 %collective-permute-done.47 = bf16[256,2048]{1,0:T(8,128)(2,1)S(1)} collective-permute-done((bf16[256,2048]{1,0:T(8,128)(2,1)}, bf16[256,2048]{1,0:T(8,128)(2,1)S(1)}, u32[]{:S(2)}, u32[]{:S(2)}) %collective-permute-start.47) | collective-permute-done | bytes 1048608 | tf_op jit(solution)/shard_map/ppermute | solution.py:40
  (377 shorter events, 266.5 us)
Async XLA Ops:
  7.2 91.2 %all-gather.4.cloned.1.call-start = ((), (), s32[]{:S(2)}) async-start(), calls=%async_computation.3 | async-start | bytes 9437184 | tf_op jit(solution)/shard_map/all_gather | solution.py:387
  13.1 206.9 %all-gather.6.cloned.1.call-start = ((), (), s32[]{:S(2)}) async-start(), calls=%async_computation.4 | async-start | bytes 9437184 | tf_op jit(solution)/shard_map/all_gather | solution.py:389
  14.3 249.8 %all-gather.8.cloned.1.call-start = ((), (), s32[]{:S(2)}) async-start(), calls=%async_computation.5 | async-start | bytes 9437184 | tf_op jit(solution)/shard_map/all_gather | solution.py:390
  113.6 330.2 %reduce-scatter.4.cloned.1.call-start = ((), (), s32[]{:S(2)}) async-start(), calls=%async_computation.6 | async-start | bytes 5242880 | tf_op jit(solution)/shard_map/reduce_scatter | solution.py:377
  155.9 24.4 %collective-permute-start.5 = (bf16[256,2048]{1,0:T(8,128)(2,1)S(1)}, bf16[256,2048]{1,0:T(8,128)(2,1)S(1)}, u32[]{:S(2)}, u32[]{:S(2)}) collective-permute-start(bf16[256,2048]{1,0:T(8,128)(2,1)S(1)} %pad_maximum_fusion.13), channel_id=1, source_target_pairs={{0,2},{1,3},{2,0},{3,1},{4,6},{5,7},{6,4},{7,5},{8,10},{9,11},{10,... | collective-permute-start | bytes 3145736 | tf_op jit(solution)/shard_map/ppermute | solution.py:40
  157.5 24.1 %collective-permute-start.4 = (bf16[256,2048]{1,0:T(8,128)(2,1)S(1)}, bf16[256,2048]{1,0:T(8,128)(2,1)S(1)}, u32[]{:S(2)}, u32[]{:S(2)}) collective-permute-start(bf16[256,2048]{1,0:T(8,128)(2,1)S(1)} %pad_maximum_fusion.12), channel_id=1, source_target_pairs={{0,1},{1,0},{2,3},{3,2},{4,5},{5,4},{6,7},{7,6},{8,9},{9,8},{10,11... | collective-permute-start | bytes 3145736 | tf_op jit(solution)/shard_map/ppermute | solution.py:40
  183.1 23.2 %collective-permute-start.7 = (bf16[256,2048]{1,0:T(8,128)(2,1)S(1)}, bf16[256,2048]{1,0:T(8,128)(2,1)S(1)}, u32[]{:S(2)}, u32[]{:S(2)}) collective-permute-start(bf16[256,2048]{1,0:T(8,128)(2,1)S(1)} %get-tuple-element.102), channel_id=1, source_target_pairs={{0,2},{1,3},{2,0},{3,1},{4,6},{5,7},{6,4},{7,5},{8,10},{9,11},{10,... | collective-permute-start | bytes 3145736 | tf_op jit(solution)/shard_map/ppermute | solution.py:40
  183.7 24.4 %collective-permute-start.6 = (bf16[256,2048]{1,0:T(8,128)(2,1)S(1)}, bf16[256,2048]{1,0:T(8,128)(2,1)S(1)}, u32[]{:S(2)}, u32[]{:S(2)}) collective-permute-start(bf16[256,2048]{1,0:T(8,128)(2,1)S(1)} %get-tuple-element.102), channel_id=1, source_target_pairs={{0,1},{1,0},{2,3},{3,2},{4,5},{5,4},{6,7},{7,6},{8,9},{9,8},{10,11... | collective-permute-start | bytes 3145736 | tf_op jit(solution)/shard_map/ppermute | solution.py:40
  286.1 24.3 %collective-permute-start.16 = (bf16[256,2048]{1,0:T(8,128)(2,1)S(1)}, bf16[256,2048]{1,0:T(8,128)(2,1)S(1)}, u32[]{:S(2)}, u32[]{:S(2)}) collective-permute-start(bf16[256,2048]{1,0:T(8,128)(2,1)S(1)} %pad_maximum_fusion.15), channel_id=1, source_target_pairs={{0,2},{1,3},{2,0},{3,1},{4,6},{5,7},{6,4},{7,5},{8,10},{9,11},{10,... | collective-permute-start | bytes 3145736 | tf_op jit(solution)/shard_map/ppermute | solution.py:40
  287.7 24.0 %collective-permute-start.15 = (bf16[256,2048]{1,0:T(8,128)(2,1)S(1)}, bf16[256,2048]{1,0:T(8,128)(2,1)S(1)}, u32[]{:S(2)}, u32[]{:S(2)}) collective-permute-start(bf16[256,2048]{1,0:T(8,128)(2,1)S(1)} %pad_maximum_fusion.14), channel_id=1, source_target_pairs={{0,1},{1,0},{2,3},{3,2},{4,5},{5,4},{6,7},{7,6},{8,9},{9,8},{10,11... | collective-permute-start | bytes 3145736 | tf_op jit(solution)/shard_map/ppermute | solution.py:40
  357.2 27.3 %collective-permute-start.23 = (bf16[256,2048]{1,0:T(8,128)(2,1)}, bf16[256,2048]{1,0:T(8,128)(2,1)}, u32[]{:S(2)}, u32[]{:S(2)}) collective-permute-start(bf16[256,2048]{1,0:T(8,128)(2,1)} %get-tuple-element.162), channel_id=1, source_target_pairs={{0,1},{1,0},{2,3},{3,2},{4,5},{5,4},{6,7},{7,6},{8,9},{9,8},{10,11... | collective-permute-start | bytes 3145736 | tf_op jit(solution)/shard_map/ppermute | solution.py:40
  358.5 26.0 %collective-permute-start.24 = (bf16[256,2048]{1,0:T(8,128)(2,1)}, bf16[256,2048]{1,0:T(8,128)(2,1)}, u32[]{:S(2)}, u32[]{:S(2)}) collective-permute-start(bf16[256,2048]{1,0:T(8,128)(2,1)} %get-tuple-element.162), channel_id=1, source_target_pairs={{0,2},{1,3},{2,0},{3,1},{4,6},{5,7},{6,4},{7,5},{8,10},{9,11},{10,... | collective-permute-start | bytes 3145736 | tf_op jit(solution)/shard_map/ppermute | solution.py:40
  366.4 164.1 %reduce-scatter.6.cloned.1.call-start = ((), (), s32[]{:S(2)}) async-start(), calls=%async_computation.7 | async-start | bytes 5242880 | tf_op jit(solution)/shard_map/reduce_scatter | solution.py:377
  378.2 32.7 %collective-permute-start.29 = (bf16[1024,2048]{1,0:T(8,128)(2,1)S(1)}, bf16[1024,2048]{1,0:T(8,128)(2,1)}, u32[]{:S(2)}, u32[]{:S(2)}) collective-permute-start(bf16[1024,2048]{1,0:T(8,128)(2,1)S(1)} %pad_maximum_fusion.1), channel_id=1, source_target_pairs={{0,4},{4,0},{8,12},{12,8},{16,20},{20,16},{24,28},{28,24},{1,5},{5... | collective-permute-start | bytes 12582920 | tf_op jit(solution)/shard_map/ppermute | solution.py:40
  400.5 24.4 %collective-permute-start.28 = (bf16[256,2048]{1,0:T(8,128)(2,1)}, bf16[256,2048]{1,0:T(8,128)(2,1)}, u32[]{:S(2)}, u32[]{:S(2)}) collective-permute-start(bf16[256,2048]{1,0:T(8,128)(2,1)} %pad_maximum_fusion.17), channel_id=1, source_target_pairs={{0,2},{1,3},{2,0},{3,1},{4,6},{5,7},{6,4},{7,5},{8,10},{9,11},{10,... | collective-permute-start | bytes 3145736 | tf_op jit(solution)/shard_map/ppermute | solution.py:40
  402.6 24.1 %collective-permute-start.27 = (bf16[256,2048]{1,0:T(8,128)(2,1)}, bf16[256,2048]{1,0:T(8,128)(2,1)}, u32[]{:S(2)}, u32[]{:S(2)}) collective-permute-start(bf16[256,2048]{1,0:T(8,128)(2,1)} %pad_maximum_fusion.16), channel_id=1, source_target_pairs={{0,1},{1,0},{2,3},{3,2},{4,5},{5,4},{6,7},{7,6},{8,9},{9,8},{10,11... | collective-permute-start | bytes 3145736 | tf_op jit(solution)/shard_map/ppermute | solution.py:40
  442.8 23.6 %collective-permute-start.32 = (bf16[256,2048]{1,0:T(8,128)(2,1)}, bf16[256,2048]{1,0:T(8,128)(2,1)S(1)}, u32[]{:S(2)}, u32[]{:S(2)}) collective-permute-start(bf16[256,2048]{1,0:T(8,128)(2,1)} %get-tuple-element.138), channel_id=1, source_target_pairs={{0,1},{1,0},{2,3},{3,2},{4,5},{5,4},{6,7},{7,6},{8,9},{9,8},{10,11... | collective-permute-start | bytes 3145736 | tf_op jit(solution)/shard_map/ppermute | solution.py:40
  443.8 189.7 %reduce-scatter.8.cloned.1.call-start = ((), (), s32[]{:S(2)}) async-start(), calls=%async_computation.8 | async-start | bytes 5242880 | tf_op jit(solution)/shard_map/reduce_scatter | solution.py:377
  528.3 26.1 %collective-permute-start.39 = (bf16[128,2048]{1,0:T(8,128)(2,1)}, bf16[128,2048]{1,0:T(8,128)(2,1)}, u32[]{:S(2)}, u32[]{:S(2)}) collective-permute-start(bf16[128,2048]{1,0:T(8,128)(2,1)} %get-tuple-element.275), channel_id=1, source_target_pairs={{0,1},{1,0},{2,3},{3,2},{4,5},{5,4},{6,7},{7,6},{8,9},{9,8},{10,11... | collective-permute-start | bytes 1572872 | tf_op jit(solution)/shard_map/ppermute | solution.py:40
  529.4 25.0 %collective-permute-start.40 = (bf16[128,2048]{1,0:T(8,128)(2,1)}, bf16[128,2048]{1,0:T(8,128)(2,1)}, u32[]{:S(2)}, u32[]{:S(2)}) collective-permute-start(bf16[128,2048]{1,0:T(8,128)(2,1)} %get-tuple-element.274), channel_id=1, source_target_pairs={{0,2},{1,3},{2,0},{3,1},{4,6},{5,7},{6,4},{7,5},{8,10},{9,11},{10,... | collective-permute-start | bytes 1572872 | tf_op jit(solution)/shard_map/ppermute | solution.py:40
  556.3 25.6 %collective-permute-start.42 = (bf16[256,2048]{1,0:T(8,128)(2,1)S(1)}, bf16[256,2048]{1,0:T(8,128)(2,1)S(1)}, u32[]{:S(2)}, u32[]{:S(2)}) collective-permute-start(bf16[256,2048]{1,0:T(8,128)(2,1)S(1)} %pad_maximum_fusion.19), channel_id=1, source_target_pairs={{0,2},{1,3},{2,0},{3,1},{4,6},{5,7},{6,4},{7,5},{8,10},{9,11},{10,... | collective-permute-start | bytes 3145736 | tf_op jit(solution)/shard_map/ppermute | solution.py:40
  557.5 25.2 %collective-permute-start.41 = (bf16[256,2048]{1,0:T(8,128)(2,1)S(1)}, bf16[256,2048]{1,0:T(8,128)(2,1)S(1)}, u32[]{:S(2)}, u32[]{:S(2)}) collective-permute-start(bf16[256,2048]{1,0:T(8,128)(2,1)S(1)} %pad_maximum_fusion.18), channel_id=1, source_target_pairs={{0,1},{1,0},{2,3},{3,2},{4,5},{5,4},{6,7},{7,6},{8,9},{9,8},{10,11... | collective-permute-start | bytes 3145736 | tf_op jit(solution)/shard_map/ppermute | solution.py:40
  584.7 24.7 %collective-permute-start.47 = (bf16[256,2048]{1,0:T(8,128)(2,1)}, bf16[256,2048]{1,0:T(8,128)(2,1)S(1)}, u32[]{:S(2)}, u32[]{:S(2)}) collective-permute-start(bf16[256,2048]{1,0:T(8,128)(2,1)} %get-tuple-element.204), channel_id=1, source_target_pairs={{0,2},{1,3},{2,0},{3,1},{4,6},{5,7},{6,4},{7,5},{8,10},{9,11},{10,... | collective-permute-start | bytes 3145736 | tf_op jit(solution)/shard_map/ppermute | solution.py:40
  585.7 24.8 %collective-permute-start.46 = (bf16[256,2048]{1,0:T(8,128)(2,1)}, bf16[256,2048]{1,0:T(8,128)(2,1)}, u32[]{:S(2)}, u32[]{:S(2)}) collective-permute-start(bf16[256,2048]{1,0:T(8,128)(2,1)} %get-tuple-element.204), channel_id=1, source_target_pairs={{0,1},{1,0},{2,3},{3,2},{4,5},{5,4},{6,7},{7,6},{8,9},{9,8},{10,11... | collective-permute-start | bytes 3145736 | tf_op jit(solution)/shard_map/ppermute | solution.py:40
  (98 other events, 881.8 us)
Sparse Core Ops, SparseCore 0:
  13.2 85.1 all-gather.3
  100.6 80.2 all-gather.5
  183.0 81.0 all-gather.7
  366.5 74.2 reduce-scatter.3
  443.9 76.8 reduce-scatter.5
  548.6 76.9 reduce-scatter.7

commit v6 on v5

--- a/solution.py
+++ b/solution.py
@@ -61,15 +61,23 @@
     return swap(block, "tensor", 1), swap(block, "tensor", 2)
 
 
-def gather_rest(block, near):
+def sent_on(near):
     one, two = near
-    half = block.shape[0] // 2
-    rest = [swap(two[:half], "tensor", 1), swap(one[half:], "tensor", 2)]
+    half = one.shape[0] // 2
+    return two[:half], one[half:]
+
+
+def gather_sent(sent, block, near):
+    rest = [swap(sent[0], "tensor", 1), swap(sent[1], "tensor", 2)]
     count, flip = lax.axis_size("tensor"), 4
     while flip < count:
-        rest.append(swap(jnp.concatenate([block, one, two, *rest]), "tensor", flip))
+        rest.append(swap(jnp.concatenate([block, *near, *rest]), "tensor", flip))
         flip *= 2
     return rest
+
+
+def gather_rest(block, near):
+    return gather_sent(sent_on(near), block, near)
 
 
 def gather_rows(block):
@@ -204,6 +212,23 @@
         ),
         name=name,
     )(*args)
+
+
+def joined_weights_kernel(query_ref, key_ref, value_ref, out_ref, low_ref):
+    width = query_ref.shape[1]
+    for place, ref in enumerate((query_ref, key_ref, value_ref)):
+        low_ref[place * width : (place + 1) * width, :] = jnp.transpose(ref[...]).astype(LOW)
+    low_ref[3 * width :, :] = out_ref[...].astype(LOW)
+
+
+def joined_weights(query, key, value, out):
+    rows, width = query.shape
+    return pl.pallas_call(
+        joined_weights_kernel,
+        out_shape=jax.ShapeDtypeStruct((4 * width, rows), LOW),
+        compiler_params=pltpu.CompilerParams(vmem_limit_bytes=32 << 20),
+        name="joined_weights",
+    )(query, key, value, out)
 
 
 def fwd_kernel(q_ref,ko_ref,kf_ref,vo_ref,vf_ref,bo_ref,bf_ref,o_ref,l_ref,*,scale):
@@ -381,17 +406,17 @@
     def rows_of(value, first, last):
         return value[first * block : last * block]
 
-    low_attn = jnp.concatenate([w_query, w_key, w_value, w_out.T], axis=1).astype(LOW)
+    low_attn = joined_weights(w_query, w_key, w_value, w_out)
     low_inner = w_inner.T.astype(LOW)
     low_outer = w_outer.astype(LOW)
-    full_attn = lax.all_gather(low_attn, "dp", axis=0, tiled=True)
-    full_qkv, full_out = full_attn[:, : 3 * width_here], full_attn[:, 3 * width_here :].T
+    full_attn = lax.all_gather(low_attn, "dp", axis=1, tiled=True)
+    full_qkv, full_out = full_attn[: 3 * width_here], full_attn[3 * width_here :]
     full_inner = lax.all_gather(low_inner, "dp", axis=1, tiled=True)
     full_outer = lax.all_gather(low_outer, "dp", axis=1, tiled=True)
 
     rows_pair = shared_columns(rows_in)
     b_qkv = jnp.concatenate([b_query, jnp.zeros_like(b_query), b_value])
-    qkv = (mat_bf(after(rows_in, rows_pair), full_qkv) + b_qkv).astype(LOW)
+    qkv = (mat_last(after(rows_in, rows_pair), full_qkv) + b_qkv).astype(LOW)
     far_kv = swap(qkv[:, width_here:], "dp", 1)
     mixed, lse = attn_fwd(qkv, far_kv, own_bias[None], far_bias[None], heads_here)
 
@@ -468,7 +493,9 @@
         mine, far = after((inner_low, inner_far), sent)
         return weight_grad([(hidden_pair[0], mine), (hidden_pair[1], far)]).astype(LOW)
 
-    hidden_parts, _, (grad_w_inner,) = scatter_rows(inner_part, (), [inner_weight])
+    hidden_parts, (output_sent,), (grad_w_inner,) = scatter_rows(
+        inner_part, [lambda sent: sent_on(after(output_near, sent))], [inner_weight]
+    )
     grad_one, attn_here, sums_one = on_rows(
         norm_one_back_kernel,
         "norm_one_back",
@@ -477,7 +504,7 @@
         True,
     )
     owner_inner = to_owner(after(grad_w_inner, owner_outer, attn_here))
-    output_rest = gather_rest(output, after(output_near, *hidden_parts))
+    output_rest = gather_sent(after(output_sent, *hidden_parts), output, output_near)
     attn_low = gather_rows(after(attn_here, output_rest))
     mixed_low = mat_last(attn_low, full_out).astype(LOW)
     query_low, own_key, own_value, far_pair = attn_bwd(
@@ -508,7 +535,7 @@
         return outer.T.astype(F32), inner.astype(F32)
 
     (here, one, two), (grad_w_attn,), (sums, (grad_w_outer, grad_w_inner)) = scatter_rows(
-        lambda a, b, gate: mat_last(rows_of(gated(qkv_low, gate), a, b), full_qkv),
+        lambda a, b, gate: mat_bf(rows_of(gated(qkv_low, gate), a, b), full_qkv),
         after_first=[attn_weight],
         after_second=[total_sums, owned],
     )

time: 650 us -> 648 us (level)
    dot_general x10 -> x12, matrix products: 51.5 us -> 57.2 us  [mat_bf(): return jnp.dot(left, right, preferred_element_type=F32)]
    dot_general x7 -> x5, matrix products: 56.8 us -> 51.1 us  [mat_last(): return lax.dot_general(left, right, BOTH_LAST, preferred_element_type=F32)]
    unnamed x151 -> x156, local copies, waits for them, and re-layouts: 35.6 us -> 36.8 us
  transfers between devices with their start and end apart: 58 -> 58, of which waited for: 38 -> 39; matrix products, arithmetic and copies ran while one was open for 34% -> 34% of each run, Pallas kernels for 9% -> 9%
where the time goes in v6:
time: 648 us; the launch traced here: 642 us
  waiting for transfers between devices  272 us (42%)
  matrix products  156 us (24%)
  Pallas kernels  60.7 us (9%)
  local copies, waits for them, and re-layouts  55 us (8%)
  other arithmetic  41.7 us (6%)
  starting transfers between devices  41.1 us (6%)
  between operations  15.9 us (2%)
    ppermute x52, waiting for transfers between devices, swap(): lax.ppermute(value, axis, [(source, source ^ flip) for source in range(co...  190 us
    all_gather x1, waiting for transfers between devices, on_device(): full_attn = lax.all_gather(low_attn, 'dp', axis=1, tiled=True)  72.7 us
    dot_general x12, matrix products, mat_bf(): return jnp.dot(left, right, preferred_element_type=F32)  57.2 us
    dot_general x5, matrix products, mat_last(): return lax.dot_general(left, right, BOTH_LAST, preferred_element_type=F32)  51.1 us
    dot_general x10, matrix products, mat_first(): return lax.dot_general(left, right, BOTH_FIRST, preferred_element_type=F32)  47.6 us
    ppermute x52, starting transfers between devices, swap(): lax.ppermute(value, axis, [(source, source ^ flip) for source in range(co...  40.6 us
    unnamed x156, local copies, waits for them, and re-layouts  36.8 us
    pallas_call x1, Pallas kernels, attn_bwd(): pl.pallas_call(functools.partial(bwd_kernel, scale=scale, chunk=chunk), g...  28.3 us
  transfers between devices with their start and end apart: 58, of which 39 were waited for; matrix products, arithmetic and copies ran while one was open for 34% of the time, Pallas kernels for 9%

profile of v6, /device:TPU:0, one launch (start us, length us, event | category | flops | bytes accessed | tf_op | source)
XLA Modules:
  0.0 642.2 jit_solution(11816156553878684768)
XLA Ops:
  25.3 72.7 %all-gather.4.cloned.1.call-done = bf16[2048,2048]{1,0:T(8,128)(2,1)} async-done(((bf16[2048,256]{1,0:T(8,128)(2,1)}), bf16[2048,2048]{1,0:T(8,128)(2,1)}) %all-gather.4.cloned.1.call-update) | async-done | bytes 8388624 | tf_op jit(solution)/shard_map/all_gather | solution.py:412
  98.0 10.1 %add_convert_fusion.3.q_ref.ko_ref.vo_ref = bf16[1024,1536]{1,0:T(8,128)(2,1)S(1)} fusion(bf16[1024,2048]{1,0:T(8,128)(2,1)} %copy-done.22, bf16[2048,2048]{1,0:T(8,128)(2,1)} %all-gather.4.cloned.1.call-done, f32[1536]{0:T(1024)S(1)} %pad_maximum_fusion.22), kind=kOutput, calls=%fused_computation.21 | convolution fusion | flops 6445596672 | bytes 13637632 | tf_op jit(solution)/shard_map/dot_general | solution.py:31
  115.8 21.1 %attention_forward.1 = (bf16[1024,512]{1,0:T(8,128)(2,1)S(1)}, f32[4,1,1024]{2,1,0:T(1,128)S(1)}) custom-call(bf16[1024,1536]{1,0:T(8,128)(2,1)} %copy-done.21, bf16[1024,1536]{1,0:T(8,128)(2,1)} %copy-done.21, bf16[1024,1024]{1,0:T(8,128)(2,1)S(1)} %collective-permute-done.1.kf_ref.vf_ref, bf16[1024,1536]{1,0:T(8,128)(2,1)} %copy-done.21, ...), custom_call_target="tpu_custom_call" | custom-call | flops 12884901888 | bytes 6291456 | tf_op jit(solution)/shard_map/attention_forward/pallas_call | solution.py:248
  145.7 8.2 %collective-permute-done.2 = bf16[128,2048]{1,0:T(8,128)(2,1)S(1)} collective-permute-done((bf16[128,2048]{1,0:T(8,128)(2,1)S(1)}, bf16[128,2048]{1,0:T(8,128)(2,1)S(1)}, u32[]{:S(2)}, u32[]{:S(2)}) %collective-permute-start.2) | collective-permute-done | bytes 524320 | tf_op jit(solution)/shard_map/ppermute | solution.py:40
  160.1 19.7 %collective-permute-done.5.two = bf16[256,2048]{1,0:T(8,128)(2,1)S(1)} collective-permute-done((bf16[256,2048]{1,0:T(8,128)(2,1)S(1)}, bf16[256,2048]{1,0:T(8,128)(2,1)S(1)}, u32[]{:S(2)}, u32[]{:S(2)}) %collective-permute-start.5) | collective-permute-done | bytes 1048608 | tf_op jit(solution)/shard_map/ppermute | solution.py:40
  183.9 21.9 %collective-permute-done.7 = bf16[256,2048]{1,0:T(8,128)(2,1)S(1)} collective-permute-done((bf16[256,2048]{1,0:T(8,128)(2,1)S(1)}, bf16[256,2048]{1,0:T(8,128)(2,1)S(1)}, u32[]{:S(2)}, u32[]{:S(2)}) %collective-permute-start.7) | collective-permute-done | bytes 1048608 | tf_op jit(solution)/shard_map/ppermute | solution.py:40
  210.7 6.7 %collective-permute-done.8 = bf16[128,2048]{1,0:T(8,128)(2,1)S(1)} collective-permute-done((bf16[128,2048]{1,0:T(8,128)(2,1)S(1)}, bf16[128,2048]{1,0:T(8,128)(2,1)S(1)}, u32[]{:S(2)}, u32[]{:S(2)}) %collective-permute-start.8) | collective-permute-done | bytes 524320 | tf_op jit(solution)/shard_map/ppermute | solution.py:40
  219.6 18.9 %fusion.7 = (bf16[1024,2048]{1,0:T(8,128)(2,1)}, bf16[1024,2048]{1,0:T(8,128)(2,1)S(1)}) fusion(f32[2048]{0:T(1024)S(1)} %copy-done.65, bf16[1024,2048]{1,0:T(8,128)(2,1)} %constant_dynamic-update-slice_fusion, bf16[2048,2048]{0,1:T(8,128)(2,1)} %all-gather.6.cloned.1.call-done), kind=kOutput, calls=%fused_computation.10 | convolution fusion | flops 8636071936 | bytes 20979712 | tf_op jit(solution)/shard_map/dot_general | solution.py:31
  254.6 9.1 %all-gather.8.cloned.1.call-done = bf16[2048,2048]{1,0:T(8,128)(2,1)} async-done(((bf16[2048,256]{1,0:T(8,128)(2,1)}), bf16[2048,2048]{1,0:T(8,128)(2,1)}) %all-gather.8.cloned.1.call-update) | async-done | bytes 8388624 | tf_op jit(solution)/shard_map/all_gather | solution.py:415
  277.7 6.5 %collective-permute-done.13 = bf16[128,2048]{1,0:T(8,128)(2,1)S(1)} collective-permute-done((bf16[128,2048]{1,0:T(8,128)(2,1)S(1)}, bf16[128,2048]{1,0:T(8,128)(2,1)S(1)}, u32[]{:S(2)}, u32[]{:S(2)}) %collective-permute-start.13) | collective-permute-done | bytes 524320 | tf_op jit(solution)/shard_map/ppermute | solution.py:40
  292.4 17.6 %collective-permute-done.16.two = bf16[256,2048]{1,0:T(8,128)(2,1)S(1)} collective-permute-done((bf16[256,2048]{1,0:T(8,128)(2,1)S(1)}, bf16[256,2048]{1,0:T(8,128)(2,1)S(1)}, u32[]{:S(2)}, u32[]{:S(2)}) %collective-permute-start.16) | collective-permute-done | bytes 1048608 | tf_op jit(solution)/shard_map/ppermute | solution.py:40
  318.1 7.0 %multiply_convert_fusion.1 = bf16[256,2048]{1,0:T(8,128)(2,1)} fusion(bf16[1024,2048]{1,0:T(8,128)(2,1)} %get-tuple-element.116, bf16[256,2048]{1,0:T(8,128)(2,1)S(1)} %get-tuple-element.115, bf16[2048,2048]{1,0:T(8,128)(2,1)} %all-gather.8.cloned.1.call-done), kind=kOutput, calls=%fused_computation.65 | convolution fusion | flops 2149056512 | bytes 11534336 | tf_op jit(solution)/shard_map/dot_general | solution.py:31
  325.1 14.7 %collective-permute-done.17 = bf16[256,2048]{1,0:T(8,128)(2,1)S(1)} collective-permute-done((bf16[256,2048]{1,0:T(8,128)(2,1)S(1)}, bf16[256,2048]{1,0:T(8,128)(2,1)S(1)}, u32[]{:S(2)}, u32[]{:S(2)}) %collective-permute-start.17) | collective-permute-done | bytes 1048608 | tf_op jit(solution)/shard_map/ppermute | solution.py:40
  366.0 11.2 %multiply_convert_fusion = bf16[768,2048]{1,0:T(8,128)(2,1)S(1)} fusion(bf16[2048,2048]{1,0:T(8,128)(2,1)} %all-gather.8.cloned.1.call-done, bf16[256,2048]{1,0:T(8,128)(2,1)} %copy-done.31, bf16[256,2048]{1,0:T(8,128)(2,1)} %copy-done.30, bf16[256,2048]{1,0:T(8,128)(2,1)} %copy-done.29, bf16[1024,2048]{1,0:T(8,128)(2,1)} %get-tuple-element.116), kind=kOutput, calls=%fused_computation.20 | convolution fusion | flops 6456606720 | bytes 17825792 | tf_op jit(solution)/shard_map/dot_general | solution.py:31
  377.9 6.2 fusion.58
  389.9 7.0 %fusion.114 = (bf16[512,2048]{1,0:T(8,128)(2,1)S(1)}, f32[512,2048]{1,0:T(8,128)S(1)}) fusion(bf16[2048,2048]{0,1:T(8,128)(2,1)} %all-gather.6.cloned.1.call-done, bf16[768,2048]{1,0:T(8,128)(2,1)S(1)} %multiply_convert_fusion), kind=kOutput, calls=%fused_computation.261 | convolution fusion | flops 4296015872 | bytes 16777216 | tf_op jit(solution)/shard_map/dot_general | solution.py:27
  403.4 7.2 %fusion.116.h = f32[256,2048]{1,0:T(8,128)} fusion(bf16[256,2048]{1,0:T(8,128)(2,1)S(1)} %copy-done.27, bf16[2048,2048]{0,1:T(8,128)(2,1)} %all-gather.6.cloned.1.call-done), kind=kOutput, calls=%fused_computation.263 | convolution fusion | flops 2147483648 | bytes 11534336 | tf_op jit(solution)/shard_map/dot_general | solution.py:27
  410.5 6.8 %fusion.117 = f32[1024,2048]{1,0:T(8,128)S(1)} fusion(bf16[1024,1024]{1,0:T(8,128)(2,1)S(1)} %copy-done.59, bf16[1024,2048]{1,0:T(8,128)(2,1)} %collective-permute-done.29), kind=kOutput, calls=%fused_computation.264 | convolution fusion | flops 4294967296 | bytes 14680064 | tf_op jit(solution)/shard_map/dot_general | solution.py:35
  417.4 6.9 %add_convert_fusion = bf16[1024,2048]{1,0:T(8,128)(2,1)} fusion(f32[1024,2048]{1,0:T(8,128)S(1)} %fusion.117, bf16[1024,2048]{1,0:T(8,128)(2,1)S(1)} %pad_maximum_fusion.1, bf16[1024,256]{1,0:T(8,128)(2,1)S(1)} %copy-done.46, bf16[1024,256]{1,0:T(8,128)(2,1)S(1)} %copy-done.45, bf16[1024,256]{1,0:T(8,128)(2,1)S(1)} %copy-done.44, ...), kind=kOutput, calls=%fused_computation.14 | convolution fusion | flops 4307550208 | bytes 18874368 | tf_op jit(solution)/shard_map/dot_general | solution.py:35
  441.8 19.7 %collective-permute-done.33 = bf16[256,2048]{1,0:T(8,128)(2,1)S(1)} collective-permute-done((bf16[256,2048]{1,0:T(8,128)(2,1)}, bf16[256,2048]{1,0:T(8,128)(2,1)S(1)}, u32[]{:S(2)}, u32[]{:S(2)}) %collective-permute-start.33) | collective-permute-done | bytes 1048608 | tf_op jit(solution)/shard_map/ppermute | solution.py:40
  465.2 8.1 %collective-permute-done.34 = bf16[128,2048]{1,0:T(8,128)(2,1)S(1)} collective-permute-done((bf16[128,2048]{1,0:T(8,128)(2,1)S(1)}, bf16[128,2048]{1,0:T(8,128)(2,1)S(1)}, u32[]{:S(2)}, u32[]{:S(2)}) %collective-permute-start.34) | collective-permute-done | bytes 524320 | tf_op jit(solution)/shard_map/ppermute | solution.py:40
  478.2 28.3 %attention_backward.1 = (bf16[1024,512]{1,0:T(8,128)(2,1)S(1)}, f32[1024,512]{1,0:T(8,128)}, f32[1024,512]{1,0:T(8,128)}, bf16[2,1024,512]{2,1,0:T(8,128)(2,1)}) custom-call(bf16[1024,1536]{1,0:T(8,128)(2,1)} %copy-done.21, bf16[1024,512]{1,0:T(8,128)(2,1)S(1)} %convolution_convert_fusion.2.do_ref, bf16[1024,512]{1,0:T(8,128)(2,1)S(1)} %copy-done.2, ...), custom_call_target="tpu_custom_call" | custom-call | flops 4096 | bytes 1048576 | tf_op jit(solution)/shard_map/attention_backward/pallas_call | solution.py:299
  566.7 6.8 %collective-permute-done.45 = f32[15872]{0:T(1024)S(1)} collective-permute-done((f32[15872]{0:T(1024)S(1)}, f32[15872]{0:T(1024)S(1)}, u32[]{:S(2)}, u32[]{:S(2)}) %collective-permute-start.45) | collective-permute-done | bytes 63520 | tf_op jit(solution)/shard_map/ppermute | solution.py:40
  587.5 19.7 %collective-permute-done.47 = bf16[256,2048]{1,0:T(8,128)(2,1)S(1)} collective-permute-done((bf16[256,2048]{1,0:T(8,128)(2,1)}, bf16[256,2048]{1,0:T(8,128)(2,1)S(1)}, u32[]{:S(2)}, u32[]{:S(2)}) %collective-permute-start.47) | collective-permute-done | bytes 1048608 | tf_op jit(solution)/shard_map/ppermute | solution.py:40
  (381 shorter events, 264.3 us)
Async XLA Ops:
  7.2 90.8 %all-gather.4.cloned.1.call-start = ((), (), s32[]{:S(2)}) async-start(), calls=%async_computation.3 | async-start | bytes 9437184 | tf_op jit(solution)/shard_map/all_gather | solution.py:412
  12.7 206.9 %all-gather.6.cloned.1.call-start = ((), (), s32[]{:S(2)}) async-start(), calls=%async_computation.4 | async-start | bytes 9437184 | tf_op jit(solution)/shard_map/all_gather | solution.py:414
  14.5 249.2 %all-gather.8.cloned.1.call-start = ((), (), s32[]{:S(2)}) async-start(), calls=%async_computation.5 | async-start | bytes 9437184 | tf_op jit(solution)/shard_map/all_gather | solution.py:415
  113.2 327.8 %reduce-scatter.4.cloned.1.call-start = ((), (), s32[]{:S(2)}) async-start(), calls=%async_computation.6 | async-start | bytes 5242880 | tf_op jit(solution)/shard_map/reduce_scatter | solution.py:402
  155.4 24.4 %collective-permute-start.5 = (bf16[256,2048]{1,0:T(8,128)(2,1)S(1)}, bf16[256,2048]{1,0:T(8,128)(2,1)S(1)}, u32[]{:S(2)}, u32[]{:S(2)}) collective-permute-start(bf16[256,2048]{1,0:T(8,128)(2,1)S(1)} %pad_maximum_fusion.12), channel_id=1, source_target_pairs={{0,2},{1,3},{2,0},{3,1},{4,6},{5,7},{6,4},{7,5},{8,10},{9,11},{10,... | collective-permute-start | bytes 3145736 | tf_op jit(solution)/shard_map/ppermute | solution.py:40
  157.1 24.1 %collective-permute-start.4 = (bf16[256,2048]{1,0:T(8,128)(2,1)S(1)}, bf16[256,2048]{1,0:T(8,128)(2,1)S(1)}, u32[]{:S(2)}, u32[]{:S(2)}) collective-permute-start(bf16[256,2048]{1,0:T(8,128)(2,1)S(1)} %pad_maximum_fusion.11), channel_id=1, source_target_pairs={{0,1},{1,0},{2,3},{3,2},{4,5},{5,4},{6,7},{7,6},{8,9},{9,8},{10,11... | collective-permute-start | bytes 3145736 | tf_op jit(solution)/shard_map/ppermute | solution.py:40
  182.7 23.2 %collective-permute-start.7 = (bf16[256,2048]{1,0:T(8,128)(2,1)S(1)}, bf16[256,2048]{1,0:T(8,128)(2,1)S(1)}, u32[]{:S(2)}, u32[]{:S(2)}) collective-permute-start(bf16[256,2048]{1,0:T(8,128)(2,1)S(1)} %get-tuple-element.104), channel_id=1, source_target_pairs={{0,2},{1,3},{2,0},{3,1},{4,6},{5,7},{6,4},{7,5},{8,10},{9,11},{10,... | collective-permute-start | bytes 3145736 | tf_op jit(solution)/shard_map/ppermute | solution.py:40
  183.3 24.4 %collective-permute-start.6 = (bf16[256,2048]{1,0:T(8,128)(2,1)S(1)}, bf16[256,2048]{1,0:T(8,128)(2,1)S(1)}, u32[]{:S(2)}, u32[]{:S(2)}) collective-permute-start(bf16[256,2048]{1,0:T(8,128)(2,1)S(1)} %get-tuple-element.104), channel_id=1, source_target_pairs={{0,1},{1,0},{2,3},{3,2},{4,5},{5,4},{6,7},{7,6},{8,9},{9,8},{10,11... | collective-permute-start | bytes 3145736 | tf_op jit(solution)/shard_map/ppermute | solution.py:40
  285.7 24.3 %collective-permute-start.16 = (bf16[256,2048]{1,0:T(8,128)(2,1)S(1)}, bf16[256,2048]{1,0:T(8,128)(2,1)S(1)}, u32[]{:S(2)}, u32[]{:S(2)}) collective-permute-start(bf16[256,2048]{1,0:T(8,128)(2,1)S(1)} %pad_maximum_fusion.14), channel_id=1, source_target_pairs={{0,2},{1,3},{2,0},{3,1},{4,6},{5,7},{6,4},{7,5},{8,10},{9,11},{10,... | collective-permute-start | bytes 3145736 | tf_op jit(solution)/shard_map/ppermute | solution.py:40
  287.3 24.0 %collective-permute-start.15 = (bf16[256,2048]{1,0:T(8,128)(2,1)S(1)}, bf16[256,2048]{1,0:T(8,128)(2,1)S(1)}, u32[]{:S(2)}, u32[]{:S(2)}) collective-permute-start(bf16[256,2048]{1,0:T(8,128)(2,1)S(1)} %pad_maximum_fusion.13), channel_id=1, source_target_pairs={{0,1},{1,0},{2,3},{3,2},{4,5},{5,4},{6,7},{7,6},{8,9},{9,8},{10,11... | collective-permute-start | bytes 3145736 | tf_op jit(solution)/shard_map/ppermute | solution.py:40
  356.8 27.3 %collective-permute-start.23 = (bf16[256,2048]{1,0:T(8,128)(2,1)}, bf16[256,2048]{1,0:T(8,128)(2,1)}, u32[]{:S(2)}, u32[]{:S(2)}) collective-permute-start(bf16[256,2048]{1,0:T(8,128)(2,1)} %get-tuple-element.166), channel_id=1, source_target_pairs={{0,1},{1,0},{2,3},{3,2},{4,5},{5,4},{6,7},{7,6},{8,9},{9,8},{10,11... | collective-permute-start | bytes 3145736 | tf_op jit(solution)/shard_map/ppermute | solution.py:40
  358.1 26.0 %collective-permute-start.24 = (bf16[256,2048]{1,0:T(8,128)(2,1)}, bf16[256,2048]{1,0:T(8,128)(2,1)}, u32[]{:S(2)}, u32[]{:S(2)}) collective-permute-start(bf16[256,2048]{1,0:T(8,128)(2,1)} %get-tuple-element.166), channel_id=1, source_target_pairs={{0,2},{1,3},{2,0},{3,1},{4,6},{5,7},{6,4},{7,5},{8,10},{9,11},{10,... | collective-permute-start | bytes 3145736 | tf_op jit(solution)/shard_map/ppermute | solution.py:40
  365.9 162.4 %reduce-scatter.6.cloned.1.call-start = ((), (), s32[]{:S(2)}) async-start(), calls=%async_computation.7 | async-start | bytes 5242880 | tf_op jit(solution)/shard_map/reduce_scatter | solution.py:402
  377.8 32.7 %collective-permute-start.29 = (bf16[1024,2048]{1,0:T(8,128)(2,1)S(1)}, bf16[1024,2048]{1,0:T(8,128)(2,1)}, u32[]{:S(2)}, u32[]{:S(2)}) collective-permute-start(bf16[1024,2048]{1,0:T(8,128)(2,1)S(1)} %pad_maximum_fusion.1), channel_id=1, source_target_pairs={{0,4},{4,0},{8,12},{12,8},{16,20},{20,16},{24,28},{28,24},{1,5},{5... | collective-permute-start | bytes 12582920 | tf_op jit(solution)/shard_map/ppermute | solution.py:40
  400.1 24.4 %collective-permute-start.28 = (bf16[256,2048]{1,0:T(8,128)(2,1)}, bf16[256,2048]{1,0:T(8,128)(2,1)}, u32[]{:S(2)}, u32[]{:S(2)}) collective-permute-start(bf16[256,2048]{1,0:T(8,128)(2,1)} %pad_maximum_fusion.16), channel_id=1, source_target_pairs={{0,2},{1,3},{2,0},{3,1},{4,6},{5,7},{6,4},{7,5},{8,10},{9,11},{10,... | collective-permute-start | bytes 3145736 | tf_op jit(solution)/shard_map/ppermute | solution.py:40
  402.2 24.1 %collective-permute-start.27 = (bf16[256,2048]{1,0:T(8,128)(2,1)}, bf16[256,2048]{1,0:T(8,128)(2,1)}, u32[]{:S(2)}, u32[]{:S(2)}) collective-permute-start(bf16[256,2048]{1,0:T(8,128)(2,1)} %pad_maximum_fusion.15), channel_id=1, source_target_pairs={{0,1},{1,0},{2,3},{3,2},{4,5},{5,4},{6,7},{7,6},{8,9},{9,8},{10,11... | collective-permute-start | bytes 3145736 | tf_op jit(solution)/shard_map/ppermute | solution.py:40
  440.0 23.8 %collective-permute-start.32 = (bf16[256,2048]{1,0:T(8,128)(2,1)}, bf16[256,2048]{1,0:T(8,128)(2,1)S(1)}, u32[]{:S(2)}, u32[]{:S(2)}) collective-permute-start(bf16[256,2048]{1,0:T(8,128)(2,1)} %get-tuple-element.142), channel_id=1, source_target_pairs={{0,1},{1,0},{2,3},{3,2},{4,5},{5,4},{6,7},{7,6},{8,9},{9,8},{10,11... | collective-permute-start | bytes 3145736 | tf_op jit(solution)/shard_map/ppermute | solution.py:40
  441.1 190.3 %reduce-scatter.8.cloned.1.call-start = ((), (), s32[]{:S(2)}) async-start(), calls=%async_computation.8 | async-start | bytes 5242880 | tf_op jit(solution)/shard_map/reduce_scatter | solution.py:402
  526.0 26.3 %collective-permute-start.39 = (bf16[128,2048]{1,0:T(8,128)(2,1)}, bf16[128,2048]{1,0:T(8,128)(2,1)}, u32[]{:S(2)}, u32[]{:S(2)}) collective-permute-start(bf16[128,2048]{1,0:T(8,128)(2,1)} %get-tuple-element.279), channel_id=1, source_target_pairs={{0,1},{1,0},{2,3},{3,2},{4,5},{5,4},{6,7},{7,6},{8,9},{9,8},{10,11... | collective-permute-start | bytes 1572872 | tf_op jit(solution)/shard_map/ppermute | solution.py:40
  527.2 25.1 %collective-permute-start.40 = (bf16[128,2048]{1,0:T(8,128)(2,1)}, bf16[128,2048]{1,0:T(8,128)(2,1)}, u32[]{:S(2)}, u32[]{:S(2)}) collective-permute-start(bf16[128,2048]{1,0:T(8,128)(2,1)} %get-tuple-element.278), channel_id=1, source_target_pairs={{0,2},{1,3},{2,0},{3,1},{4,6},{5,7},{6,4},{7,5},{8,10},{9,11},{10,... | collective-permute-start | bytes 1572872 | tf_op jit(solution)/shard_map/ppermute | solution.py:40
  554.2 25.6 %collective-permute-start.42 = (bf16[256,2048]{1,0:T(8,128)(2,1)S(1)}, bf16[256,2048]{1,0:T(8,128)(2,1)S(1)}, u32[]{:S(2)}, u32[]{:S(2)}) collective-permute-start(bf16[256,2048]{1,0:T(8,128)(2,1)S(1)} %pad_maximum_fusion.18), channel_id=1, source_target_pairs={{0,2},{1,3},{2,0},{3,1},{4,6},{5,7},{6,4},{7,5},{8,10},{9,11},{10,... | collective-permute-start | bytes 3145736 | tf_op jit(solution)/shard_map/ppermute | solution.py:40
  555.2 25.2 %collective-permute-start.41 = (bf16[256,2048]{1,0:T(8,128)(2,1)S(1)}, bf16[256,2048]{1,0:T(8,128)(2,1)S(1)}, u32[]{:S(2)}, u32[]{:S(2)}) collective-permute-start(bf16[256,2048]{1,0:T(8,128)(2,1)S(1)} %pad_maximum_fusion.17), channel_id=1, source_target_pairs={{0,1},{1,0},{2,3},{3,2},{4,5},{5,4},{6,7},{7,6},{8,9},{9,8},{10,11... | collective-permute-start | bytes 3145736 | tf_op jit(solution)/shard_map/ppermute | solution.py:40
  582.5 24.7 %collective-permute-start.47 = (bf16[256,2048]{1,0:T(8,128)(2,1)}, bf16[256,2048]{1,0:T(8,128)(2,1)S(1)}, u32[]{:S(2)}, u32[]{:S(2)}) collective-permute-start(bf16[256,2048]{1,0:T(8,128)(2,1)} %get-tuple-element.208), channel_id=1, source_target_pairs={{0,2},{1,3},{2,0},{3,1},{4,6},{5,7},{6,4},{7,5},{8,10},{9,11},{10,... | collective-permute-start | bytes 3145736 | tf_op jit(solution)/shard_map/ppermute | solution.py:40
  583.5 24.6 %collective-permute-start.46 = (bf16[256,2048]{1,0:T(8,128)(2,1)}, bf16[256,2048]{1,0:T(8,128)(2,1)}, u32[]{:S(2)}, u32[]{:S(2)}) collective-permute-start(bf16[256,2048]{1,0:T(8,128)(2,1)} %get-tuple-element.208), channel_id=1, source_target_pairs={{0,1},{1,0},{2,3},{3,2},{4,5},{5,4},{6,7},{7,6},{8,9},{9,8},{10,11... | collective-permute-start | bytes 3145736 | tf_op jit(solution)/shard_map/ppermute | solution.py:40
  (102 other events, 883.0 us)
Sparse Core Ops, SparseCore 0:
  12.8 85.1 all-gather.3
  100.2 80.2 all-gather.5
  182.7 81.0 all-gather.7
  366.1 74.2 reduce-scatter.3
  443.2 77.2 reduce-scatter.5
  546.4 76.8 reduce-scatter.7

commit v7 on v6

--- a/solution.py
+++ b/solution.py
@@ -186,7 +186,7 @@
     add_sums(sum_ref, back, to_gain, grad)
 
 
-def on_rows(kernel, name, args, outs, sums, tile=64):
+def on_rows(kernel, name, args, outs, sums, tile=128):
     rows, model = args[0].shape
     tile = min(tile, rows)
 
@@ -511,10 +511,11 @@
         qkv, far_kv, mixed_low, mixed, lse, own_bias_wide, far_bias_wide, heads_here, 512, 256
     )
     attn_pair = shared_columns(after(attn_low, query_low))
-    far_key, far_value = after(swap(far_pair, "dp", 1), attn_pair).astype(F32)
+    far_key, far_value = swap(far_pair, "dp", 1).astype(F32)
     key_low = (own_key + far_key).astype(LOW)
     value_low = (own_value + far_value).astype(LOW)
     qkv_low = jnp.concatenate([query_low, key_low, value_low], axis=1)
+    qkv_low = after(qkv_low, attn_pair)
     qkv_far = swap(qkv_low, "dp", 1)
 
     def attn_weight(sent):

time: 648 us -> 647 us (level)
    unnamed x156 -> x154, local copies, waits for them, and re-layouts: 36.8 us -> 35.2 us
  transfers between devices with their start and end apart: 58 -> 58, of which waited for: 39 -> 38; matrix products, arithmetic and copies ran while one was open for 34% -> 34% of each run, Pallas kernels for 9% -> 9%
where the time goes in v7:
time: 647 us; the launch traced here: 642 us
  waiting for transfers between devices  271 us (42%)
  matrix products  156 us (24%)
  Pallas kernels  59.9 us (9%)
  local copies, waits for them, and re-layouts  53.5 us (8%)
  other arithmetic  43.9 us (7%)
  starting transfers between devices  41.7 us (6%)
  between operations  15.8 us (2%)
    ppermute x52, waiting for transfers between devices, swap(): lax.ppermute(value, axis, [(source, source ^ flip) for source in range(co...  189 us
    all_gather x1, waiting for transfers between devices, on_device(): full_attn = lax.all_gather(low_attn, 'dp', axis=1, tiled=True)  72.6 us
    dot_general x12, matrix products, mat_bf(): return jnp.dot(left, right, preferred_element_type=F32)  57.2 us
    dot_general x5, matrix products, mat_last(): return lax.dot_general(left, right, BOTH_LAST, preferred_element_type=F32)  51.1 us
    dot_general x10, matrix products, mat_first(): return lax.dot_general(left, right, BOTH_FIRST, preferred_element_type=F32)  47.6 us
    ppermute x52, starting transfers between devices, swap(): lax.ppermute(value, axis, [(source, source ^ flip) for source in range(co...  41.2 us
    unnamed x154, local copies, waits for them, and re-layouts  35.2 us
    pallas_call x1, Pallas kernels, attn_bwd(): pl.pallas_call(functools.partial(bwd_kernel, scale=scale, chunk=chunk), g...  28.3 us
  transfers between devices with their start and end apart: 58, of which 38 were waited for; matrix products, arithmetic and copies ran while one was open for 34% of the time, Pallas kernels for 9%

profile of v7, /device:TPU:0, one launch (start us, length us, event | category | flops | bytes accessed | tf_op | source)
XLA Modules:
  0.0 641.5 jit_solution(38080214830590664)
XLA Ops:
  25.4 72.6 %all-gather.4.cloned.1.call-done = bf16[2048,2048]{1,0:T(8,128)(2,1)} async-done(((bf16[2048,256]{1,0:T(8,128)(2,1)}), bf16[2048,2048]{1,0:T(8,128)(2,1)}) %all-gather.4.cloned.1.call-update) | async-done | bytes 8388624 | tf_op jit(solution)/shard_map/all_gather | solution.py:412
  98.0 10.1 %add_convert_fusion.3.q_ref.ko_ref.vo_ref = bf16[1024,1536]{1,0:T(8,128)(2,1)S(1)} fusion(bf16[1024,2048]{1,0:T(8,128)(2,1)} %copy-done.22, bf16[2048,2048]{1,0:T(8,128)(2,1)} %all-gather.4.cloned.1.call-done, f32[1536]{0:T(1024)S(1)} %pad_maximum_fusion.22), kind=kOutput, calls=%fused_computation.21 | convolution fusion | flops 6445596672 | bytes 13637632 | tf_op jit(solution)/shard_map/dot_general | solution.py:31
  115.8 21.1 %attention_forward.1 = (bf16[1024,512]{1,0:T(8,128)(2,1)S(1)}, f32[4,1,1024]{2,1,0:T(1,128)S(1)}) custom-call(bf16[1024,1536]{1,0:T(8,128)(2,1)} %copy-done.21, bf16[1024,1536]{1,0:T(8,128)(2,1)} %copy-done.21, bf16[1024,1024]{1,0:T(8,128)(2,1)S(1)} %collective-permute-done.1.kf_ref.vf_ref, bf16[1024,1536]{1,0:T(8,128)(2,1)} %copy-done.21, ...), custom_call_target="tpu_custom_call" | custom-call | flops 12884901888 | bytes 6291456 | tf_op jit(solution)/shard_map/attention_forward/pallas_call | solution.py:248
  145.7 8.2 %collective-permute-done.2 = bf16[128,2048]{1,0:T(8,128)(2,1)S(1)} collective-permute-done((bf16[128,2048]{1,0:T(8,128)(2,1)S(1)}, bf16[128,2048]{1,0:T(8,128)(2,1)S(1)}, u32[]{:S(2)}, u32[]{:S(2)}) %collective-permute-start.2) | collective-permute-done | bytes 524320 | tf_op jit(solution)/shard_map/ppermute | solution.py:40
  160.1 19.7 %collective-permute-done.5.two = bf16[256,2048]{1,0:T(8,128)(2,1)S(1)} collective-permute-done((bf16[256,2048]{1,0:T(8,128)(2,1)S(1)}, bf16[256,2048]{1,0:T(8,128)(2,1)S(1)}, u32[]{:S(2)}, u32[]{:S(2)}) %collective-permute-start.5) | collective-permute-done | bytes 1048608 | tf_op jit(solution)/shard_map/ppermute | solution.py:40
  183.9 22.0 %collective-permute-done.7 = bf16[256,2048]{1,0:T(8,128)(2,1)S(1)} collective-permute-done((bf16[256,2048]{1,0:T(8,128)(2,1)S(1)}, bf16[256,2048]{1,0:T(8,128)(2,1)S(1)}, u32[]{:S(2)}, u32[]{:S(2)}) %collective-permute-start.7) | collective-permute-done | bytes 1048608 | tf_op jit(solution)/shard_map/ppermute | solution.py:40
  210.8 6.6 %collective-permute-done.8 = bf16[128,2048]{1,0:T(8,128)(2,1)S(1)} collective-permute-done((bf16[128,2048]{1,0:T(8,128)(2,1)S(1)}, bf16[128,2048]{1,0:T(8,128)(2,1)S(1)}, u32[]{:S(2)}, u32[]{:S(2)}) %collective-permute-start.8) | collective-permute-done | bytes 524320 | tf_op jit(solution)/shard_map/ppermute | solution.py:40
  219.6 18.9 %fusion.7 = (bf16[1024,2048]{1,0:T(8,128)(2,1)}, bf16[1024,2048]{1,0:T(8,128)(2,1)S(1)}) fusion(f32[2048]{0:T(1024)S(1)} %copy-done.64, bf16[1024,2048]{1,0:T(8,128)(2,1)} %constant_dynamic-update-slice_fusion, bf16[2048,2048]{0,1:T(8,128)(2,1)} %all-gather.6.cloned.1.call-done), kind=kOutput, calls=%fused_computation.10 | convolution fusion | flops 8636071936 | bytes 20979712 | tf_op jit(solution)/shard_map/dot_general | solution.py:31
  254.6 9.1 %all-gather.8.cloned.1.call-done = bf16[2048,2048]{1,0:T(8,128)(2,1)} async-done(((bf16[2048,256]{1,0:T(8,128)(2,1)}), bf16[2048,2048]{1,0:T(8,128)(2,1)}) %all-gather.8.cloned.1.call-update) | async-done | bytes 8388624 | tf_op jit(solution)/shard_map/all_gather | solution.py:415
  277.7 6.5 %collective-permute-done.13 = bf16[128,2048]{1,0:T(8,128)(2,1)S(1)} collective-permute-done((bf16[128,2048]{1,0:T(8,128)(2,1)S(1)}, bf16[128,2048]{1,0:T(8,128)(2,1)S(1)}, u32[]{:S(2)}, u32[]{:S(2)}) %collective-permute-start.13) | collective-permute-done | bytes 524320 | tf_op jit(solution)/shard_map/ppermute | solution.py:40
  292.4 17.6 %collective-permute-done.16.two = bf16[256,2048]{1,0:T(8,128)(2,1)S(1)} collective-permute-done((bf16[256,2048]{1,0:T(8,128)(2,1)S(1)}, bf16[256,2048]{1,0:T(8,128)(2,1)S(1)}, u32[]{:S(2)}, u32[]{:S(2)}) %collective-permute-start.16) | collective-permute-done | bytes 1048608 | tf_op jit(solution)/shard_map/ppermute | solution.py:40
  317.7 7.1 %multiply_convert_fusion.1 = bf16[256,2048]{1,0:T(8,128)(2,1)} fusion(bf16[1024,2048]{1,0:T(8,128)(2,1)} %get-tuple-element.116, bf16[256,2048]{1,0:T(8,128)(2,1)S(1)} %get-tuple-element.115, bf16[2048,2048]{1,0:T(8,128)(2,1)} %all-gather.8.cloned.1.call-done), kind=kOutput, calls=%fused_computation.65 | convolution fusion | flops 2149056512 | bytes 11534336 | tf_op jit(solution)/shard_map/dot_general | solution.py:31
  324.8 14.7 %collective-permute-done.17 = bf16[256,2048]{1,0:T(8,128)(2,1)S(1)} collective-permute-done((bf16[256,2048]{1,0:T(8,128)(2,1)S(1)}, bf16[256,2048]{1,0:T(8,128)(2,1)S(1)}, u32[]{:S(2)}, u32[]{:S(2)}) %collective-permute-start.17) | collective-permute-done | bytes 1048608 | tf_op jit(solution)/shard_map/ppermute | solution.py:40
  365.7 11.2 %multiply_convert_fusion = bf16[768,2048]{1,0:T(8,128)(2,1)S(1)} fusion(bf16[2048,2048]{1,0:T(8,128)(2,1)} %all-gather.8.cloned.1.call-done, bf16[256,2048]{1,0:T(8,128)(2,1)} %copy-done.31, bf16[256,2048]{1,0:T(8,128)(2,1)} %copy-done.30, bf16[256,2048]{1,0:T(8,128)(2,1)} %copy-done.29, bf16[1024,2048]{1,0:T(8,128)(2,1)} %get-tuple-element.116), kind=kOutput, calls=%fused_computation.20 | convolution fusion | flops 6456606720 | bytes 17825792 | tf_op jit(solution)/shard_map/dot_general | solution.py:31
  389.6 7.0 %fusion.114 = (bf16[512,2048]{1,0:T(8,128)(2,1)S(1)}, f32[512,2048]{1,0:T(8,128)S(1)}) fusion(bf16[2048,2048]{0,1:T(8,128)(2,1)} %all-gather.6.cloned.1.call-done, bf16[768,2048]{1,0:T(8,128)(2,1)S(1)} %multiply_convert_fusion), kind=kOutput, calls=%fused_computation.261 | convolution fusion | flops 4296015872 | bytes 16777216 | tf_op jit(solution)/shard_map/dot_general | solution.py:27
  403.0 7.2 %fusion.116.h = f32[256,2048]{1,0:T(8,128)} fusion(bf16[256,2048]{1,0:T(8,128)(2,1)S(1)} %copy-done.27, bf16[2048,2048]{0,1:T(8,128)(2,1)} %all-gather.6.cloned.1.call-done), kind=kOutput, calls=%fused_computation.263 | convolution fusion | flops 2147483648 | bytes 11534336 | tf_op jit(solution)/shard_map/dot_general | solution.py:27
  410.2 6.8 %fusion.117 = f32[1024,2048]{1,0:T(8,128)S(1)} fusion(bf16[1024,1024]{1,0:T(8,128)(2,1)S(1)} %copy-done.59, bf16[1024,2048]{1,0:T(8,128)(2,1)} %collective-permute-done.29), kind=kOutput, calls=%fused_computation.264 | convolution fusion | flops 4294967296 | bytes 14680064 | tf_op jit(solution)/shard_map/dot_general | solution.py:35
  417.1 6.9 %add_convert_fusion = bf16[1024,2048]{1,0:T(8,128)(2,1)} fusion(f32[1024,2048]{1,0:T(8,128)S(1)} %fusion.117, bf16[1024,2048]{1,0:T(8,128)(2,1)S(1)} %pad_maximum_fusion.1, bf16[1024,256]{1,0:T(8,128)(2,1)S(1)} %copy-done.46, bf16[1024,256]{1,0:T(8,128)(2,1)S(1)} %copy-done.45, bf16[1024,256]{1,0:T(8,128)(2,1)S(1)} %copy-done.44, ...), kind=kOutput, calls=%fused_computation.14 | convolution fusion | flops 4307550208 | bytes 18874368 | tf_op jit(solution)/shard_map/dot_general | solution.py:35
  441.4 19.7 %collective-permute-done.33 = bf16[256,2048]{1,0:T(8,128)(2,1)S(1)} collective-permute-done((bf16[256,2048]{1,0:T(8,128)(2,1)}, bf16[256,2048]{1,0:T(8,128)(2,1)S(1)}, u32[]{:S(2)}, u32[]{:S(2)}) %collective-permute-start.33) | collective-permute-done | bytes 1048608 | tf_op jit(solution)/shard_map/ppermute | solution.py:40
  464.8 8.1 %collective-permute-done.34 = bf16[128,2048]{1,0:T(8,128)(2,1)S(1)} collective-permute-done((bf16[128,2048]{1,0:T(8,128)(2,1)S(1)}, bf16[128,2048]{1,0:T(8,128)(2,1)S(1)}, u32[]{:S(2)}, u32[]{:S(2)}) %collective-permute-start.34) | collective-permute-done | bytes 524320 | tf_op jit(solution)/shard_map/ppermute | solution.py:40
  477.8 28.3 %attention_backward.1 = (bf16[1024,512]{1,0:T(8,128)(2,1)S(1)}, f32[1024,512]{1,0:T(8,128)}, f32[1024,512]{1,0:T(8,128)}, bf16[2,1024,512]{2,1,0:T(8,128)(2,1)}) custom-call(bf16[1024,1536]{1,0:T(8,128)(2,1)} %copy-done.21, bf16[1024,512]{1,0:T(8,128)(2,1)S(1)} %convolution_convert_fusion.2.do_ref, bf16[1024,512]{1,0:T(8,128)(2,1)S(1)} %copy-done.2, ...), custom_call_target="tpu_custom_call" | custom-call | flops 4096 | bytes 1048576 | tf_op jit(solution)/shard_map/attention_backward/pallas_call | solution.py:299
  566.1 6.8 %collective-permute-done.45 = f32[15872]{0:T(1024)S(1)} collective-permute-done((f32[15872]{0:T(1024)S(1)}, f32[15872]{0:T(1024)S(1)}, u32[]{:S(2)}, u32[]{:S(2)}) %collective-permute-start.45) | collective-permute-done | bytes 63520 | tf_op jit(solution)/shard_map/ppermute | solution.py:40
  572.9 6.3 collective-permute-done.42
  586.8 19.7 %collective-permute-done.47 = bf16[256,2048]{1,0:T(8,128)(2,1)S(1)} collective-permute-done((bf16[256,2048]{1,0:T(8,128)(2,1)}, bf16[256,2048]{1,0:T(8,128)(2,1)S(1)}, u32[]{:S(2)}, u32[]{:S(2)}) %collective-permute-start.47) | collective-permute-done | bytes 1048608 | tf_op jit(solution)/shard_map/ppermute | solution.py:40
  (380 shorter events, 263.9 us)
Async XLA Ops:
  7.2 90.8 %all-gather.4.cloned.1.call-start = ((), (), s32[]{:S(2)}) async-start(), calls=%async_computation.3 | async-start | bytes 9437184 | tf_op jit(solution)/shard_map/all_gather | solution.py:412
  12.7 206.9 %all-gather.6.cloned.1.call-start = ((), (), s32[]{:S(2)}) async-start(), calls=%async_computation.4 | async-start | bytes 9437184 | tf_op jit(solution)/shard_map/all_gather | solution.py:414
  14.5 249.2 %all-gather.8.cloned.1.call-start = ((), (), s32[]{:S(2)}) async-start(), calls=%async_computation.5 | async-start | bytes 9437184 | tf_op jit(solution)/shard_map/all_gather | solution.py:415
  113.2 327.5 %reduce-scatter.4.cloned.1.call-start = ((), (), s32[]{:S(2)}) async-start(), calls=%async_computation.6 | async-start | bytes 5242880 | tf_op jit(solution)/shard_map/reduce_scatter | solution.py:402
  155.5 24.4 %collective-permute-start.5 = (bf16[256,2048]{1,0:T(8,128)(2,1)S(1)}, bf16[256,2048]{1,0:T(8,128)(2,1)S(1)}, u32[]{:S(2)}, u32[]{:S(2)}) collective-permute-start(bf16[256,2048]{1,0:T(8,128)(2,1)S(1)} %pad_maximum_fusion.12), channel_id=1, source_target_pairs={{0,2},{1,3},{2,0},{3,1},{4,6},{5,7},{6,4},{7,5},{8,10},{9,11},{10,... | collective-permute-start | bytes 3145736 | tf_op jit(solution)/shard_map/ppermute | solution.py:40
  157.1 24.1 %collective-permute-start.4 = (bf16[256,2048]{1,0:T(8,128)(2,1)S(1)}, bf16[256,2048]{1,0:T(8,128)(2,1)S(1)}, u32[]{:S(2)}, u32[]{:S(2)}) collective-permute-start(bf16[256,2048]{1,0:T(8,128)(2,1)S(1)} %pad_maximum_fusion.11), channel_id=1, source_target_pairs={{0,1},{1,0},{2,3},{3,2},{4,5},{5,4},{6,7},{7,6},{8,9},{9,8},{10,11... | collective-permute-start | bytes 3145736 | tf_op jit(solution)/shard_map/ppermute | solution.py:40
  182.7 23.2 %collective-permute-start.7 = (bf16[256,2048]{1,0:T(8,128)(2,1)S(1)}, bf16[256,2048]{1,0:T(8,128)(2,1)S(1)}, u32[]{:S(2)}, u32[]{:S(2)}) collective-permute-start(bf16[256,2048]{1,0:T(8,128)(2,1)S(1)} %get-tuple-element.104), channel_id=1, source_target_pairs={{0,2},{1,3},{2,0},{3,1},{4,6},{5,7},{6,4},{7,5},{8,10},{9,11},{10,... | collective-permute-start | bytes 3145736 | tf_op jit(solution)/shard_map/ppermute | solution.py:40
  183.3 24.5 %collective-permute-start.6 = (bf16[256,2048]{1,0:T(8,128)(2,1)S(1)}, bf16[256,2048]{1,0:T(8,128)(2,1)S(1)}, u32[]{:S(2)}, u32[]{:S(2)}) collective-permute-start(bf16[256,2048]{1,0:T(8,128)(2,1)S(1)} %get-tuple-element.104), channel_id=1, source_target_pairs={{0,1},{1,0},{2,3},{3,2},{4,5},{5,4},{6,7},{7,6},{8,9},{9,8},{10,11... | collective-permute-start | bytes 3145736 | tf_op jit(solution)/shard_map/ppermute | solution.py:40
  285.7 24.3 %collective-permute-start.16 = (bf16[256,2048]{1,0:T(8,128)(2,1)S(1)}, bf16[256,2048]{1,0:T(8,128)(2,1)S(1)}, u32[]{:S(2)}, u32[]{:S(2)}) collective-permute-start(bf16[256,2048]{1,0:T(8,128)(2,1)S(1)} %pad_maximum_fusion.14), channel_id=1, source_target_pairs={{0,2},{1,3},{2,0},{3,1},{4,6},{5,7},{6,4},{7,5},{8,10},{9,11},{10,... | collective-permute-start | bytes 3145736 | tf_op jit(solution)/shard_map/ppermute | solution.py:40
  287.3 24.0 %collective-permute-start.15 = (bf16[256,2048]{1,0:T(8,128)(2,1)S(1)}, bf16[256,2048]{1,0:T(8,128)(2,1)S(1)}, u32[]{:S(2)}, u32[]{:S(2)}) collective-permute-start(bf16[256,2048]{1,0:T(8,128)(2,1)S(1)} %pad_maximum_fusion.13), channel_id=1, source_target_pairs={{0,1},{1,0},{2,3},{3,2},{4,5},{5,4},{6,7},{7,6},{8,9},{9,8},{10,11... | collective-permute-start | bytes 3145736 | tf_op jit(solution)/shard_map/ppermute | solution.py:40
  356.5 27.3 %collective-permute-start.23 = (bf16[256,2048]{1,0:T(8,128)(2,1)}, bf16[256,2048]{1,0:T(8,128)(2,1)}, u32[]{:S(2)}, u32[]{:S(2)}) collective-permute-start(bf16[256,2048]{1,0:T(8,128)(2,1)} %get-tuple-element.166), channel_id=1, source_target_pairs={{0,1},{1,0},{2,3},{3,2},{4,5},{5,4},{6,7},{7,6},{8,9},{9,8},{10,11... | collective-permute-start | bytes 3145736 | tf_op jit(solution)/shard_map/ppermute | solution.py:40
  357.7 26.0 %collective-permute-start.24 = (bf16[256,2048]{1,0:T(8,128)(2,1)}, bf16[256,2048]{1,0:T(8,128)(2,1)}, u32[]{:S(2)}, u32[]{:S(2)}) collective-permute-start(bf16[256,2048]{1,0:T(8,128)(2,1)} %get-tuple-element.166), channel_id=1, source_target_pairs={{0,2},{1,3},{2,0},{3,1},{4,6},{5,7},{6,4},{7,5},{8,10},{9,11},{10,... | collective-permute-start | bytes 3145736 | tf_op jit(solution)/shard_map/ppermute | solution.py:40
  365.6 162.1 %reduce-scatter.6.cloned.1.call-start = ((), (), s32[]{:S(2)}) async-start(), calls=%async_computation.7 | async-start | bytes 5242880 | tf_op jit(solution)/shard_map/reduce_scatter | solution.py:402
  377.5 32.7 %collective-permute-start.29 = (bf16[1024,2048]{1,0:T(8,128)(2,1)S(1)}, bf16[1024,2048]{1,0:T(8,128)(2,1)}, u32[]{:S(2)}, u32[]{:S(2)}) collective-permute-start(bf16[1024,2048]{1,0:T(8,128)(2,1)S(1)} %pad_maximum_fusion.1), channel_id=1, source_target_pairs={{0,4},{4,0},{8,12},{12,8},{16,20},{20,16},{24,28},{28,24},{1,5},{5... | collective-permute-start | bytes 12582920 | tf_op jit(solution)/shard_map/ppermute | solution.py:40
  399.7 24.4 %collective-permute-start.28 = (bf16[256,2048]{1,0:T(8,128)(2,1)}, bf16[256,2048]{1,0:T(8,128)(2,1)}, u32[]{:S(2)}, u32[]{:S(2)}) collective-permute-start(bf16[256,2048]{1,0:T(8,128)(2,1)} %pad_maximum_fusion.16), channel_id=1, source_target_pairs={{0,2},{1,3},{2,0},{3,1},{4,6},{5,7},{6,4},{7,5},{8,10},{9,11},{10,... | collective-permute-start | bytes 3145736 | tf_op jit(solution)/shard_map/ppermute | solution.py:40
  401.9 24.1 %collective-permute-start.27 = (bf16[256,2048]{1,0:T(8,128)(2,1)}, bf16[256,2048]{1,0:T(8,128)(2,1)}, u32[]{:S(2)}, u32[]{:S(2)}) collective-permute-start(bf16[256,2048]{1,0:T(8,128)(2,1)} %pad_maximum_fusion.15), channel_id=1, source_target_pairs={{0,1},{1,0},{2,3},{3,2},{4,5},{5,4},{6,7},{7,6},{8,9},{9,8},{10,11... | collective-permute-start | bytes 3145736 | tf_op jit(solution)/shard_map/ppermute | solution.py:40
  439.6 23.9 %collective-permute-start.32 = (bf16[256,2048]{1,0:T(8,128)(2,1)}, bf16[256,2048]{1,0:T(8,128)(2,1)S(1)}, u32[]{:S(2)}, u32[]{:S(2)}) collective-permute-start(bf16[256,2048]{1,0:T(8,128)(2,1)} %get-tuple-element.142), channel_id=1, source_target_pairs={{0,1},{1,0},{2,3},{3,2},{4,5},{5,4},{6,7},{7,6},{8,9},{9,8},{10,11... | collective-permute-start | bytes 3145736 | tf_op jit(solution)/shard_map/ppermute | solution.py:40
  440.7 190.0 %reduce-scatter.8.cloned.1.call-start = ((), (), s32[]{:S(2)}) async-start(), calls=%async_computation.8 | async-start | bytes 5242880 | tf_op jit(solution)/shard_map/reduce_scatter | solution.py:402
  523.0 28.7 %collective-permute-start.39 = (bf16[128,2048]{1,0:T(8,128)(2,1)}, bf16[128,2048]{1,0:T(8,128)(2,1)}, u32[]{:S(2)}, u32[]{:S(2)}) collective-permute-start(bf16[128,2048]{1,0:T(8,128)(2,1)} %get-tuple-element.277), channel_id=1, source_target_pairs={{0,1},{1,0},{2,3},{3,2},{4,5},{5,4},{6,7},{7,6},{8,9},{9,8},{10,11... | collective-permute-start | bytes 1572872 | tf_op jit(solution)/shard_map/ppermute | solution.py:40
  524.2 27.5 %collective-permute-start.40 = (bf16[128,2048]{1,0:T(8,128)(2,1)}, bf16[128,2048]{1,0:T(8,128)(2,1)}, u32[]{:S(2)}, u32[]{:S(2)}) collective-permute-start(bf16[128,2048]{1,0:T(8,128)(2,1)} %get-tuple-element.276), channel_id=1, source_target_pairs={{0,2},{1,3},{2,0},{3,1},{4,6},{5,7},{6,4},{7,5},{8,10},{9,11},{10,... | collective-permute-start | bytes 1572872 | tf_op jit(solution)/shard_map/ppermute | solution.py:40
  553.5 25.6 %collective-permute-start.42 = (bf16[256,2048]{1,0:T(8,128)(2,1)S(1)}, bf16[256,2048]{1,0:T(8,128)(2,1)S(1)}, u32[]{:S(2)}, u32[]{:S(2)}) collective-permute-start(bf16[256,2048]{1,0:T(8,128)(2,1)S(1)} %pad_maximum_fusion.18), channel_id=1, source_target_pairs={{0,2},{1,3},{2,0},{3,1},{4,6},{5,7},{6,4},{7,5},{8,10},{9,11},{10,... | collective-permute-start | bytes 3145736 | tf_op jit(solution)/shard_map/ppermute | solution.py:40
  554.6 25.2 %collective-permute-start.41 = (bf16[256,2048]{1,0:T(8,128)(2,1)S(1)}, bf16[256,2048]{1,0:T(8,128)(2,1)S(1)}, u32[]{:S(2)}, u32[]{:S(2)}) collective-permute-start(bf16[256,2048]{1,0:T(8,128)(2,1)S(1)} %pad_maximum_fusion.17), channel_id=1, source_target_pairs={{0,1},{1,0},{2,3},{3,2},{4,5},{5,4},{6,7},{7,6},{8,9},{9,8},{10,11... | collective-permute-start | bytes 3145736 | tf_op jit(solution)/shard_map/ppermute | solution.py:40
  581.8 24.7 %collective-permute-start.47 = (bf16[256,2048]{1,0:T(8,128)(2,1)}, bf16[256,2048]{1,0:T(8,128)(2,1)S(1)}, u32[]{:S(2)}, u32[]{:S(2)}) collective-permute-start(bf16[256,2048]{1,0:T(8,128)(2,1)} %get-tuple-element.208), channel_id=1, source_target_pairs={{0,2},{1,3},{2,0},{3,1},{4,6},{5,7},{6,4},{7,5},{8,10},{9,11},{10,... | collective-permute-start | bytes 3145736 | tf_op jit(solution)/shard_map/ppermute | solution.py:40
  582.9 24.6 %collective-permute-start.46 = (bf16[256,2048]{1,0:T(8,128)(2,1)}, bf16[256,2048]{1,0:T(8,128)(2,1)}, u32[]{:S(2)}, u32[]{:S(2)}) collective-permute-start(bf16[256,2048]{1,0:T(8,128)(2,1)} %get-tuple-element.208), channel_id=1, source_target_pairs={{0,1},{1,0},{2,3},{3,2},{4,5},{5,4},{6,7},{7,6},{8,9},{9,8},{10,11... | collective-permute-start | bytes 3145736 | tf_op jit(solution)/shard_map/ppermute | solution.py:40
  (101 other events, 884.0 us)
Sparse Core Ops, SparseCore 0:
  12.8 85.1 all-gather.3
  100.2 80.2 all-gather.5
  182.7 81.0 all-gather.7
  365.7 74.2 reduce-scatter.3
  442.8 77.2 reduce-scatter.5
  545.8 76.8 reduce-scatter.7
